TPU v7x, 1024 devices: a whole 4x8x16 slice. The times are simulated.
1024 devices in a mesh: grp: 64 (over x, z), sp: 16 (over y, core).
Axes of the slice: x: 4, y: 8, z: 16, core: 2. Of those that a mesh axis runs over, the one named last changes fastest.
Arguments:
- vis_feats: bfloat16 [16384, 1152], P('grp'), may hold values from -6 to 6
- proj_w: bfloat16 [1152, 4096], P(None, 'sp'), may hold values from -0.1875 to 0.1875
- text_embed: bfloat16 [262144, 4096], P('grp', 'sp'), may hold values from -6 to 6
- dest_group: int32 [16384], replicated, may hold values from 0 to 63, as said below
- layout: int32 [64, 4096], P('grp'), may hold values from 0 to 4095, each once within a row
- norm_gain: float32 [4096], P('sp'), may hold values from 0.1 to 1.9
- key_w: bfloat16 [4096, 512], P('sp'), may hold values from -0.09375 to 0.09375
- value_w: bfloat16 [4096, 512], P('sp'), may hold values from -0.09375 to 0.09375
Outputs:
- key_out: bfloat16 [262144, 512], P(('grp', 'sp'))
- value_out: bfloat16 [262144, 512], P(('grp', 'sp'))
Inputs may be any that keep to these rules, and one draw needn't show every extreme that they name: `dest_group`: each block of 256 rows (one encoder shard's tokens) is 32 runs of 8 consecutive rows; a run names one group, and the runs of one block name distinct groups.
All inputs are finite; a program needn't handle non-finite values.
Results may differ from a plain program's by a relative error of at most 0.024.
Values may be sent and summed in bfloat16 or wider, within the bound.
No kernel may reach another device: no remote copies, remote signals or barrier semaphores. Data moves between devices by JAX's collectives and lax.ppermute only.
A program may use at most 32 MiB of HBM per device.

v0:
```python
import jax
import jax.numpy as jnp
from jax import lax
from jax.sharding import PartitionSpec as P

D = 4096


def local(vis_feats, proj_w, text_embed, dest_group, layout, norm_gain, key_w, value_w):
    group_count = lax.axis_size("grp")
    group_index = lax.axis_index("grp")
    seq_len = text_embed.shape[0]
    vis_dev = vis_feats.shape[0]
    run_count = group_count // 2
    capacity = vis_dev // run_count
    run_heads = dest_group.reshape(group_count, run_count, capacity)[:, :, 0]
    own_runs = lax.dynamic_index_in_dim(run_heads, group_index, 0, keepdims=False)
    raw_width = vis_feats.shape[1]
    outgoing = jnp.zeros((group_count, capacity, raw_width), jnp.bfloat16)
    outgoing = outgoing.at[own_runs].set(vis_feats.reshape(run_count, capacity, raw_width))
    incoming = lax.all_to_all(outgoing, "grp", split_axis=0, concat_axis=0, tiled=True)
    arrived = jnp.dot(
        incoming.reshape(group_count * capacity, raw_width),
        proj_w,
        preferred_element_type=jnp.float32,
    ).astype(jnp.bfloat16)
    senders = jnp.any(run_heads == group_index, axis=1).astype(jnp.int32)
    earlier = jnp.cumsum(senders) - senders
    slot_rank = earlier[:, None] * capacity + jnp.arange(capacity, dtype=jnp.int32)[None, :]
    order_row = layout[0]
    positions = jnp.where(
        senders[:, None] > 0, order_row[jnp.clip(slot_rank, 0, seq_len - 1)], seq_len
    )
    sequence = text_embed.at[positions.reshape(-1)].set(arrived, mode="drop")
    sequence_f = sequence.astype(jnp.float32)
    squares = jnp.sum(sequence_f * sequence_f, axis=1)
    scaled = (sequence_f * norm_gain).astype(jnp.bfloat16)
    kv_weight = jnp.concatenate([key_w, value_w], axis=1)
    rows_here = seq_len // lax.axis_size("sp")
    totals = lax.psum(squares, "sp")
    my_squares = lax.dynamic_slice_in_dim(totals, lax.axis_index("sp") * rows_here, rows_here, 0)
    key_value = lax.psum_scatter(
        jnp.dot(scaled, kv_weight, preferred_element_type=jnp.float32).astype(jnp.bfloat16),
        "sp",
        scatter_dimension=0,
        tiled=True,
    ).astype(jnp.float32)
    inv_rms = lax.rsqrt(my_squares / D + 1e-05)[:, None]
    key_cols = key_w.shape[1]
    key_out = (key_value[:, :key_cols] * inv_rms).astype(jnp.bfloat16)
    value_out = (key_value[:, key_cols:] * inv_rms).astype(jnp.bfloat16)
    return (key_out, value_out)


def solution(mesh):
    return jax.shard_map(
        local,
        mesh=mesh,
        in_specs=(
            P("grp", None),
            P(None, "sp"),
            P("grp", "sp"),
            P(),
            P("grp", None),
            P("sp"),
            P("sp", None),
            P("sp", None),
        ),
        out_specs=(P(("grp", "sp"), None), P(("grp", "sp"), None)),
        check_vma=False,
    )
```

profile of v0, /device:TPU:1, one launch (start us, length us, event | category | flops | bytes accessed | tf_op | source)
XLA Modules:
  0.0 187.1 jit_solution(7577718375865016636)
XLA Ops:
  7.2 0.0 copy-start
  7.2 0.9 copy-done.6
  8.1 0.6 reshape.156
  8.7 0.1 dynamic-slice_reduce_fusion
  8.8 1.1 broadcast_in_dim.9
  9.9 4.4 %scatter_fusion = bf16[64,8,1152]{2,1,0:T(8,128)(2,1)} fusion(bf16[64,8,1152]{2,1,0:T(8,128)(2,1)} %broadcast_in_dim.9, s32[32]{0:T(128)S(1)} %fusion.10, bf16[32,8,1152]{2,1,0:T(8,128)(2,1)S(1)} %bitcast.20), kind=kCustom, calls=%fused_computation.1 | custom fusion | bytes 1769600 | tf_op jit(solution)/shard_map/scatter | solution.py:20
  14.3 23.1 %all-to-all-start = ((bf16[64,8,1152]{2,1,0:T(8,128)(2,1)}), bf16[64,8,1152]{2,1,0:T(8,128)(2,1)}, u32[]{:S(2)}, u32[]{:S(2)}) async-start(bf16[64,8,1152]{2,1,0:T(8,128)(2,1)} %scatter_fusion), calls=%async_computation | async-start | bytes 2359296 | tf_op jit(solution)/shard_map/all_to_all | solution.py:21
  37.5 0.0 reduce-scatter.2.cloned.1.call-start
  37.5 1.3 compare_reduce_fusion
  38.8 0.1 copy.12
  38.9 0.1 reduce-window.8
  39.0 0.1 reduce.1
  39.1 0.1 compare_select_fusion
  39.2 0.1 reshape.163
  39.3 3.1 %gather_fusion = s32[512]{0:T(512)S(1)} fusion(s32[4096]{0:T(1024)S(1)} %bitcast.18, s32[1024]{0:T(1024)S(1)} %pad_clamp_fusion), kind=kCustom, calls=%fused_computation | custom fusion | bytes 6144 | tf_op jit(solution)/shard_map/gather | solution.py:32
  42.5 0.0 copy-start.2
  42.5 0.1 reshape.162
  42.6 0.1 broadcast_select_fusion
  42.7 0.1 select_n.54
  42.8 50.1 %all-to-all-done = bf16[64,8,1152]{2,1,0:T(8,128)(2,1)} async-done(((bf16[64,8,1152]{2,1,0:T(8,128)(2,1)}), bf16[64,8,1152]{2,1,0:T(8,128)(2,1)}, u32[]{:S(2)}, u32[]{:S(2)}) %all-to-all-start) | async-done | bytes 1179680 | tf_op jit(solution)/shard_map/all_to_all | solution.py:21
  92.9 1.8 convolution_convert_fusion.1
  94.7 0.0 copy-start.5
  94.7 0.0 copy-start.7
  94.7 3.5 %scatter_fusion.1 = bf16[4096,256]{1,0:T(8,128)(2,1)S(1)} fusion(bf16[4096,256]{1,0:T(8,128)(2,1)S(1)} %copy-done.2, s32[512]{0:T(512)S(1)} %bitcast.21, bf16[512,256]{1,0:T(8,128)(2,1)S(1)} %convolution_convert_fusion.1), kind=kCustom, calls=%fused_computation.2 | custom fusion | bytes 788480 | tf_op jit(solution)/shard_map/scatter | solution.py:34
  98.3 5.6 %convolution_convert_fusion = bf16[4096,1024]{1,0:T(8,128)(2,1)} fusion(bf16[4096,256]{1,0:T(8,128)(2,1)S(1)} %scatter_fusion.1, f32[256]{0:T(256)S(1)} %copy-done.7, bf16[256,512]{1,0:T(8,128)(2,1)S(1)} %copy-done.4, bf16[256,512]{1,0:T(8,128)(2,1)S(1)} %copy-done.5), kind=kOutput, calls=%fused_computation.3 | convolution fusion | flops 2155872256 | bytes 11011072 | tf_op jit(solution)/shard_map/dot_general | solution.py:43
  103.9 0.0 reduce-scatter.2.cloned.1.call-update
  103.9 0.6 fusion.1
  104.5 47.9 %psum.7 = f32[4096]{0:T(1024)S(1)} all-reduce(f32[4096]{0:T(1024)S(1)} %fusion.1), channel_id=1, replica_groups=mesh['grp'=64,'sp'=16] {'sp'}, use_global_device_ids=true, to_apply=%region_6.7 | all-reduce | flops 4096 | bytes 32768 | tf_op jit(solution)/shard_map/psum | solution.py:40
  152.4 0.1 add_rsqrt_fusion
  152.5 25.7 %reduce-scatter.2.cloned.1.call-done = bf16[256,1024]{1,0:T(8,128)(2,1)} async-done(((bf16[4096,1024]{1,0:T(8,128)(2,1)}), bf16[256,1024]{1,0:T(8,128)(2,1)}) %reduce-scatter.2.cloned.1.call-update) | async-done | bytes 524304 | tf_op jit(solution)/shard_map/reduce_scatter | solution.py:42
  178.2 1.1 convert_element_type.49
  179.4 0.9 fusion.5
  (16 shorter events, 0.1 us)
Async XLA Ops:
  7.2 85.7 %copy-start = (bf16[1152,256]{1,0:T(8,128)(2,1)S(1)}, bf16[1152,256]{1,0:T(8,128)(2,1)}, u32[]{:S(2)}) copy-start(bf16[1152,256]{1,0:T(8,128)(2,1)} %param.9) | copy-start | bytes 1769476
  7.2 0.9 copy-start.6
  7.2 2.7 %copy-start.3 = (bf16[256,1152]{1,0:T(8,128)(2,1)S(1)}, bf16[256,1152]{1,0:T(8,128)(2,1)}, u32[]{:S(2)}) copy-start(bf16[256,1152]{1,0:T(8,128)(2,1)} %param.8) | copy-start | bytes 1769476
  14.3 25.0 %copy-start.1 = (s32[1,4096]{1,0:T(1,128)S(1)}, s32[1,4096]{1,0:T(1,128)}, u32[]{:S(2)}) copy-start(s32[1,4096]{1,0:T(1,128)} %param.12) | copy-start | bytes 49156
  14.3 78.6 %all-to-all-start = ((bf16[64,8,1152]{2,1,0:T(8,128)(2,1)}), bf16[64,8,1152]{2,1,0:T(8,128)(2,1)}, u32[]{:S(2)}, u32[]{:S(2)}) async-start(bf16[64,8,1152]{2,1,0:T(8,128)(2,1)} %scatter_fusion), calls=%async_computation | async-start | bytes 2359296 | tf_op jit(solution)/shard_map/all_to_all | solution.py:21
  37.5 140.7 %reduce-scatter.2.cloned.1.call-start = ((), (), s32[]{:S(2)}) async-start(), calls=%async_computation.2 | async-start | bytes 8912896 | tf_op jit(solution)/shard_map/reduce_scatter | solution.py:42
  42.5 52.2 %copy-start.2 = (bf16[4096,256]{1,0:T(8,128)(2,1)S(1)}, bf16[4096,256]{1,0:T(8,128)(2,1)}, u32[]{:S(2)}) copy-start(bf16[4096,256]{1,0:T(8,128)(2,1)} %param.10) | copy-start | bytes 6291460
  94.7 3.6 %copy-start.4 = (bf16[256,512]{1,0:T(8,128)(2,1)S(1)}, bf16[256,512]{1,0:T(8,128)(2,1)}, u32[]{:S(2)}) copy-start(bf16[256,512]{1,0:T(8,128)(2,1)} %param.15) | copy-start | bytes 786436
  94.7 3.6 %copy-start.5 = (bf16[256,512]{1,0:T(8,128)(2,1)S(1)}, bf16[256,512]{1,0:T(8,128)(2,1)}, u32[]{:S(2)}) copy-start(bf16[256,512]{1,0:T(8,128)(2,1)} %param.14) | copy-start | bytes 786436
  94.7 3.6 %copy-start.7 = (f32[256]{0:T(256)S(1)}, f32[256]{0:T(256)}, u32[]{:S(2)}) copy-start(f32[256]{0:T(256)} %param.13) | copy-start | bytes 3076
Sparse Core Ops, SparseCore 0:
  104.0 74.1 reduce-scatter.1
where the time goes:
time: 188 us; the launch traced here: 187 us
  waiting for transfers between devices  75.9 us (40%)
  blocking collectives  47.9 us (25%)
  starting transfers between devices  23.2 us (12%)
  local copies, waits for them, and re-layouts  14.2 us (8%)
  between operations  14.2 us (8%)
  matrix products  7.35 us (4%)
  other arithmetic  4.43 us (2%)
    all_to_all x1, waiting for transfers between devices, local(): lax.all_to_all(outgoing, 'grp', split_axis=0, concat_axis=0, tiled=True)  50.1 us
    psum x1, blocking collectives, local(): totals = lax.psum(squares, 'sp')  47.9 us
    reduce_scatter x1, waiting for transfers between devices, local(): lax.psum_scatter(jnp.dot(scaled, kv_weight, preferred_element_type=jnp.fl...  25.7 us
    all_to_all x1, starting transfers between devices, local(): lax.all_to_all(outgoing, 'grp', split_axis=0, concat_axis=0, tiled=True)  23.1 us
    dot_general x1, matrix products, local(): jnp.dot(scaled, kv_weight, preferred_element_type=jnp.float32)  5.57 us
    scatter x1, local copies, waits for them, and re-layouts, local(): outgoing.at[own_runs].set(vis_feats.reshape(run_count, capacity, raw_width))  4.39 us
  transfers between devices with their start and end apart: 2, of which 2 were waited for; matrix products, arithmetic and copies ran while one was open for 3% of the time, Pallas kernels for 0%

commit v1 on v0

v1 whole, which is shorter than its diff:
```python
import functools

import jax
import jax.numpy as jnp
from jax import lax
from jax.experimental import pallas as pl
from jax.experimental.pallas import tpu as pltpu
from jax.sharding import Mesh
from jax.sharding import PartitionSpec as P

D = 4096
LANES = 128
EXTRA = 16
EPS = 1e-05
F32 = jnp.float32
BF16 = jnp.bfloat16


def three_parts(x):
    hi = x.astype(BF16).astype(F32)
    rest = x - hi
    mid = rest.astype(BF16).astype(F32)
    low = (rest - mid).astype(BF16).astype(F32)
    return [hi, mid, low]


def source_kernel(capacity, n_y, feats_ref, proj_ref, weight_ref, squares_ref, out_ref):
    tokens = feats_ref.shape[0]
    half = tokens // 2
    per_core = capacity // 2
    projected = jnp.dot(feats_ref[...], proj_ref[...], preferred_element_type=F32).astype(BF16)
    row = lax.broadcasted_iota(jnp.int32, (tokens, tokens), 0)
    col = lax.broadcasted_iota(jnp.int32, (tokens, tokens), 1)
    core = (row >= half).astype(jnp.int32)
    inner = row - core * half
    run = lax.div(inner, per_core)
    token = run * capacity + core * per_core + (inner - run * per_core)
    order = (col == token).astype(F32).astype(BF16)
    tokens_by_core = jnp.dot(order, projected, preferred_element_type=F32)
    lane_squares = jnp.sum((tokens_by_core * tokens_by_core).T, axis=0, keepdims=True)
    products = jnp.dot(
        tokens_by_core.astype(BF16), weight_ref[...], preferred_element_type=F32
    ).astype(BF16)
    text_rows = squares_ref.shape[1]
    pad = jnp.zeros((EXTRA - 3 * (text_rows + 1), LANES), F32)
    for y in range(n_y):
        for c in range(2):
            to = 2 * y + c
            out_ref[to, :half, :] = products[c * half : (c + 1) * half, y * LANES : (y + 1) * LANES]
            parts = three_parts(squares_ref[to])
            parts += three_parts(lane_squares[:, c * half : (c + 1) * half])
            out_ref[to, half:, :] = jnp.concatenate(parts + [pad], axis=0).astype(BF16)


def route_kernel(text_rows, target_ref, parts_ref, out_ref, squares_ref):
    half = parts_ref.shape[1] - EXTRA
    sums = jnp.sum(parts_ref[:, :half, :].astype(F32), axis=0)
    extra = jnp.sum(parts_ref[:, half:, :].astype(F32), axis=0)
    text = extra[:text_rows] + extra[text_rows : 2 * text_rows] + extra[2 * text_rows : 3 * text_rows]
    squares_ref[...] = jnp.concatenate(
        [text, jnp.zeros((8 - text_rows, LANES), F32)], axis=0
    )
    first = 3 * text_rows
    visual = extra[first : first + 1] + extra[first + 1 : first + 2] + extra[first + 2 : first + 3]
    scale = jnp.broadcast_to(lax.rsqrt(visual / D + EPS), (half, half)).T
    rows = (sums * scale).astype(BF16)
    slot = lax.broadcasted_iota(jnp.int32, (out_ref.shape[0], half), 0)
    place = (slot == target_ref[0:1, :]).astype(F32).astype(BF16)
    out_ref[...] = jnp.dot(place, rows, preferred_element_type=F32).astype(BF16)


def finish_kernel(sums_ref, squares_ref, slots_ref, own_ref, other_ref, key_ref, value_ref):
    rows = sums_ref.shape[0]
    n_y, slots, _ = own_ref.shape
    position = lax.broadcasted_iota(jnp.int32, (rows, slots), 0)
    own_f = (position == slots_ref[0:1, :]).astype(F32)
    other_f = (position == slots_ref[1:2, :]).astype(F32)
    is_visual = jnp.sum(own_f + other_f, axis=1, keepdims=True) > 0.5
    own = own_f.astype(BF16)
    other = other_f.astype(BF16)
    inverse = lax.rsqrt(squares_ref[...] / D + EPS)
    scale = jnp.concatenate(
        [
            jnp.broadcast_to(inverse[i : i + 1, :], (LANES, LANES)).T
            for i in range(rows // LANES)
        ],
        axis=0,
    )
    for y in range(n_y):
        visual = jnp.dot(own, own_ref[y], preferred_element_type=F32)
        visual += jnp.dot(other, other_ref[y], preferred_element_type=F32)
        text = sums_ref[:, y * LANES : (y + 1) * LANES].astype(F32) * scale
        block = jnp.where(is_visual, visual, text).astype(BF16)
        if y < n_y // 2:
            key_ref[:, y * LANES : (y + 1) * LANES] = block
        else:
            z = y - n_y // 2
            value_ref[:, z * LANES : (z + 1) * LANES] = block


def vmem(n):
    return [pl.BlockSpec(memory_space=pltpu.VMEM)] * n


PARAMS = pltpu.CompilerParams(vmem_limit_bytes=24 * 2**20)


def local(vis_feats, proj_w, text_embed, dest_group, layout, norm_gain, key_w, value_w):
    n_grp = lax.axis_size("grp")
    n_y = lax.axis_size("y")
    n_sp = 2 * n_y
    h = lax.axis_index("grp")
    c = lax.axis_index("core")
    s = lax.axis_index("y") * 2 + c
    seq_len = text_embed.shape[0]
    rows_here = seq_len // n_sp
    tokens = vis_feats.shape[0]
    run_count = n_grp // 2
    capacity = tokens // run_count
    per_core = capacity // 2
    half = tokens // 2
    columns = key_w.shape[1] + value_w.shape[1]
    text_rows = rows_here // LANES

    weight = jnp.concatenate([key_w, value_w], axis=1).astype(F32) * norm_gain[:, None]
    weight = weight.astype(BF16)
    text_sums = lax.psum_scatter(
        jnp.dot(text_embed, weight, preferred_element_type=F32).astype(BF16),
        ("y", "core"),
        scatter_dimension=0,
        tiled=True,
    )
    text_f = text_embed.astype(F32)
    squares = jnp.sum(text_f * text_f, axis=1).reshape(n_sp, text_rows, LANES)

    outgoing = pl.pallas_call(
        functools.partial(source_kernel, capacity, n_y),
        out_shape=jax.ShapeDtypeStruct((n_sp, half + EXTRA, LANES), BF16),
        in_specs=vmem(4),
        out_specs=pl.BlockSpec(memory_space=pltpu.VMEM),
        compiler_params=PARAMS,
        name="source",
    )(vis_feats, proj_w, weight, squares)
    parts = lax.all_to_all(outgoing, ("y", "core"), 0, 0, tiled=True)

    run_heads = dest_group.reshape(n_grp, run_count, capacity)[:, :, 0]
    own_runs = lax.dynamic_index_in_dim(run_heads, h, 0, keepdims=False)
    target = own_runs[:, None] * per_core + jnp.arange(per_core, dtype=jnp.int32)[None, :]
    target = jnp.broadcast_to(target.reshape(1, half), (8, half))
    routed, my_squares = pl.pallas_call(
        functools.partial(route_kernel, text_rows),
        out_shape=(
            jax.ShapeDtypeStruct((n_grp * per_core, LANES), BF16),
            jax.ShapeDtypeStruct((8, LANES), F32),
        ),
        in_specs=vmem(2),
        out_specs=tuple(vmem(2)),
        compiler_params=PARAMS,
        name="route",
    )(target, parts)
    arrived = lax.all_to_all(
        routed.reshape(n_grp, per_core, LANES), "grp", 0, 0, tiled=True
    ).reshape(n_grp * per_core, LANES)
    own = lax.all_to_all(
        jnp.broadcast_to(arrived[None], (n_y, n_grp * per_core, LANES)), "y", 0, 0, tiled=True
    )
    other = lax.ppermute(own, "core", [(0, 1), (1, 0)])

    senders = jnp.any(run_heads == h, axis=1)
    group = jnp.arange(n_grp, dtype=jnp.int32)
    earlier = jnp.sum(
        jnp.where(senders[None, :] & (group[None, :] < group[:, None]), 1, 0), axis=1
    )
    first_ranks = layout[0, : n_grp * capacity].reshape(n_grp, capacity)
    where = jnp.sum(
        jnp.where((earlier[:, None] == group[None, :])[:, :, None], first_ranks[None], 0), axis=1
    )
    where = jnp.where(senders[:, None], where - s * rows_here, -1)
    where = where.reshape(n_grp, 2, per_core).transpose(1, 0, 2).reshape(2, n_grp * per_core)
    mine = lax.dynamic_index_in_dim(where, c, 0)
    theirs = lax.dynamic_index_in_dim(where, 1 - c, 0)
    slots = jnp.concatenate([mine, theirs, jnp.full((6, n_grp * per_core), -1, jnp.int32)], axis=0)

    return pl.pallas_call(
        finish_kernel,
        out_shape=(
            jax.ShapeDtypeStruct((rows_here, key_w.shape[1]), BF16),
            jax.ShapeDtypeStruct((rows_here, value_w.shape[1]), BF16),
        ),
        in_specs=vmem(5),
        out_specs=tuple(vmem(2)),
        compiler_params=PARAMS,
        name="finish",
    )(text_sums, my_squares, slots, own, other)


def solution(mesh):
    n_grp, n_sp = mesh.devices.shape
    split = Mesh(mesh.devices.reshape(n_grp, n_sp // 2, 2), ("grp", "y", "core"))
    sp = ("y", "core")
    return jax.shard_map(
        local,
        mesh=split,
        in_specs=(
            P("grp", None),
            P(None, sp),
            P("grp", sp),
            P(),
            P("grp", None),
            P(sp),
            P(sp, None),
            P(sp, None),
        ),
        out_specs=(P(("grp", "y", "core"), None), P(("grp", "y", "core"), None)),
        check_vma=False,
    )
```

time: 188 us -> 128 us (0.68)
  the two profiles are of different devices: /device:TPU:1 before, /device:TPU:25 now
where the time goes in v1:
time: 128 us
  waiting for transfers between devices  51.2 us (40%)
  starting transfers between devices  40.9 us (32%)
  between operations  14.2 us (11%)
  matrix products  7.16 us (6%)
  other arithmetic  6.4 us (5%)
  Pallas kernels  4.2 us (3%)
  local copies, waits for them, and re-layouts  3.85 us (3%)
    all_to_all x1, waiting for transfers between devices, local(): parts = lax.all_to_all(outgoing, ('y', 'core'), 0, 0, tiled=True)  16.7 us
    all_to_all x1, starting transfers between devices, local(): parts = lax.all_to_all(outgoing, ('y', 'core'), 0, 0, tiled=True)  16.6 us
    all_to_all x1, waiting for transfers between devices, local(): lax.all_to_all(routed.reshape(n_grp, per_core, LANES), 'grp', 0, 0, tiled...  13.5 us
    all_to_all x1, starting transfers between devices, local(): lax.all_to_all(routed.reshape(n_grp, per_core, LANES), 'grp', 0, 0, tiled...  12.9 us
    all_to_all x1, waiting for transfers between devices, local(): lax.all_to_all(jnp.broadcast_to(arrived[None], (n_y, n_grp * per_core, LA...  11.6 us
    reduce_scatter x1, waiting for transfers between devices, local(): lax.psum_scatter(jnp.dot(text_embed, weight, preferred_element_type=F32)....  8.28 us
    dot_general x1, matrix products, local(): jnp.dot(text_embed, weight, preferred_element_type=F32).astype(BF16)  7.16 us
    all_to_all x1, starting transfers between devices, local(): lax.all_to_all(jnp.broadcast_to(arrived[None], (n_y, n_grp * per_core, LA...  6.16 us
  transfers between devices with their start and end apart: 5, of which 5 were waited for; matrix products, arithmetic and copies ran while one was open for 6% of the time, Pallas kernels for 2%

profile of v1, /device:TPU:25, one launch (start us, length us, event | category | flops | bytes accessed | tf_op | source)
XLA Modules:
  0.0 127.9 jit_solution(8769580877326647757)
XLA Ops:
  7.2 1.2 multiply_convert_fusion.weight_ref
  8.4 7.2 %convert_bitcast_fusion = bf16[4096,1024]{1,0:T(8,128)(2,1)} fusion(bf16[4096,256]{1,0:T(8,128)(2,1)} %param.10, bf16[256,1024]{1,0:T(8,128)(2,1)S(1)} %multiply_convert_fusion.weight_ref), kind=kOutput, calls=%fused_computation | convolution fusion | flops 2151677952 | bytes 11010048 | tf_op jit(solution)/shard_map/dot_general | solution.py:128
  15.6 2.3 %multiply_reduce_fusion = f32[4096]{0:T(1024)S(1)} fusion(bf16[4096,256]{1,0:T(8,128)(2,1)} %param.10), kind=kLoop, calls=%fused_computation.1 | loop fusion | flops 3141632 | bytes 2113536 | tf_op jit(solution)/shard_map/reduce_sum | solution.py:134
  17.9 1.9 %source.1 = bf16[16,144,128]{2,1,0:T(8,128)(2,1)} custom-call(bf16[256,1152]{1,0:T(8,128)(2,1)S(1)} %copy-done, bf16[1152,256]{1,0:T(8,128)(2,1)S(1)} %copy-done.1, bf16[256,1024]{1,0:T(8,128)(2,1)S(1)} %multiply_convert_fusion.weight_ref, f32[16,2,128]{2,1,0:T(2,128)S(1)} %bitcast.11), custom_call_target="tpu_custom_call" | custom-call | tf_op jit(solution)/shard_map/source/pallas_call | solution.py:136
  19.8 16.6 %all-to-all-start = ((bf16[16,144,128]{2,1,0:T(8,128)(2,1)}), bf16[16,144,128]{2,1,0:T(8,128)(2,1)S(1)}, u32[]{:S(2)}, u32[]{:S(2)}) async-start(bf16[16,144,128]{2,1,0:T(8,128)(2,1)} %source.1), calls=%async_computation.1 | async-start | bytes 1179648 | tf_op jit(solution)/shard_map/all_to_all | solution.py:144
  36.4 0.6 reshape.80
  37.0 0.1 multiply_reduce_fusion.1
  37.1 0.1 iota_add_fusion
  37.2 0.1 add.41
  37.3 16.7 %all-to-all-done.parts_ref = bf16[16,144,128]{2,1,0:T(8,128)(2,1)S(1)} async-done(((bf16[16,144,128]{2,1,0:T(8,128)(2,1)}), bf16[16,144,128]{2,1,0:T(8,128)(2,1)S(1)}, u32[]{:S(2)}, u32[]{:S(2)}) %all-to-all-start) | async-done | bytes 589856 | tf_op jit(solution)/shard_map/all_to_all | solution.py:144
  54.0 0.9 route.1
  54.8 12.9 %all-to-all-start.1 = ((bf16[64,4,128]{2,1,0:T(4,128)(2,1)}), bf16[64,4,128]{2,1,0:T(4,128)(2,1)S(1)}, u32[]{:S(2)}, u32[]{:S(2)}) async-start(bf16[64,4,128]{2,1,0:T(4,128)(2,1)} %bitcast.4), calls=%async_computation.2 | async-start | bytes 131072 | tf_op jit(solution)/shard_map/all_to_all | solution.py:161
  67.7 13.5 %all-to-all-done.1 = bf16[64,4,128]{2,1,0:T(4,128)(2,1)S(1)} async-done(((bf16[64,4,128]{2,1,0:T(4,128)(2,1)}), bf16[64,4,128]{2,1,0:T(4,128)(2,1)S(1)}, u32[]{:S(2)}, u32[]{:S(2)}) %all-to-all-start.1) | async-done | bytes 65568 | tf_op jit(solution)/shard_map/all_to_all | solution.py:161
  81.3 0.9 broadcast_in_dim.78
  82.2 6.2 %all-to-all-start.2 = ((bf16[8,256,128]{2,1,0:T(8,128)(2,1)}), bf16[8,256,128]{2,1,0:T(8,128)(2,1)S(1)}, u32[]{:S(2)}, u32[]{:S(2)}) async-start(bf16[8,256,128]{2,1,0:T(8,128)(2,1)} %broadcast_in_dim.78), calls=%async_computation.3 | async-start | bytes 1048576 | tf_op jit(solution)/shard_map/all_to_all | solution.py:164
  88.3 0.7 slice_reduce_fusion
  89.0 0.1 broadcast_in_dim.72
  89.1 0.1 copy.20
  89.2 1.3 %compare_reduce_fusion = pred[64]{0:T(512)(128)(4,1)S(1)} fusion(s32[]{:T(128)S(6)} %axis_index.33, s32[64,32,8]{2,1,0:T(8,128)S(1)} %reshape.80), kind=kLoop, calls=%fused_computation.3 | loop fusion | flops 4032 | bytes 8260 | tf_op jit(solution)/shard_map/reduce_or | solution.py:169
  90.5 0.1 select_reduce_fusion.1
  90.6 0.1 iota_compare_fusion
  90.7 1.2 select_reduce_fusion
  91.9 11.6 %all-to-all-done.2.own_ref = bf16[8,256,128]{2,1,0:T(8,128)(2,1)S(1)} async-done(((bf16[8,256,128]{2,1,0:T(8,128)(2,1)}), bf16[8,256,128]{2,1,0:T(8,128)(2,1)S(1)}, u32[]{:S(2)}, u32[]{:S(2)}) %all-to-all-start.2) | async-done | bytes 524320 | tf_op jit(solution)/shard_map/all_to_all | solution.py:164
  103.5 5.2 %collective-permute-start = (bf16[8,256,128]{2,1,0:T(8,128)(2,1)S(1)}, bf16[8,256,128]{2,1,0:T(8,128)(2,1)S(1)}, u32[]{:S(2)}, u32[]{:S(2)}) collective-permute-start(bf16[8,256,128]{2,1,0:T(8,128)(2,1)S(1)} %all-to-all-done.2.own_ref), channel_id=1, source_target_pairs={{0,1},{1,0},{2,3},{3,2},{4,5},{5,4},{6,7},{7,6},{8,9},{9,8},{10,11... | collective-permute-start | bytes 1572872 | tf_op jit(solution)/shard_map/ppermute | solution.py:167
  108.7 0.1 copy.22
  108.9 0.1 reshape.82
  109.0 0.1 pad.2.clone
  109.1 0.1 add_add_fusion.slots_ref
  109.1 1.1 collective-permute-done.other_ref
  110.3 8.3 %reduce-scatter.2.cloned.1.call-done.sums_ref = bf16[256,1024]{1,0:T(8,128)(2,1)} async-done(((bf16[4096,1024]{1,0:T(8,128)(2,1)}), bf16[256,1024]{1,0:T(8,128)(2,1)}) %reduce-scatter.2.cloned.1.call-update) | async-done | bytes 524304 | tf_op jit(solution)/shard_map/reduce_scatter | solution.py:127
  118.5 1.0 copy-done.2
  119.6 1.4 %finish.1 = (bf16[256,512]{1,0:T(8,128)(2,1)}, bf16[256,512]{1,0:T(8,128)(2,1)}) custom-call(bf16[256,1024]{1,0:T(8,128)(2,1)S(1)} %copy-done.2, f32[8,128]{1,0:T(8,128)S(1)} %get-tuple-element.4.squares_ref, s32[8,256]{1,0:T(8,128)S(1)} %add_add_fusion.slots_ref, bf16[8,256,128]{2,1,0:T(8,128)(2,1)S(1)} %all-to-all-done.2.own_ref, ...), custom_call_target="tpu_custom_call" | custom-call | tf_op jit(solution)/shard_map/finish/pallas_call | solution.py:184
  (15 shorter events, 0.2 us)
Async XLA Ops:
  7.2 111.4 %reduce-scatter.2.cloned.1.call-start = ((), (), s32[]{:S(2)}) async-start(), calls=%async_computation.4 | async-start | bytes 8912896 | tf_op jit(solution)/shard_map/reduce_scatter | solution.py:127
  15.6 2.3 %copy-start = (bf16[256,1152]{1,0:T(8,128)(2,1)S(1)}, bf16[256,1152]{1,0:T(8,128)(2,1)}, u32[]{:S(2)}) copy-start(bf16[256,1152]{1,0:T(8,128)(2,1)} %feats_ref.1) | copy-start | bytes 1769476
  15.6 2.4 %copy-start.1 = (bf16[1152,256]{1,0:T(8,128)(2,1)S(1)}, bf16[1152,256]{1,0:T(8,128)(2,1)}, u32[]{:S(2)}) copy-start(bf16[1152,256]{1,0:T(8,128)(2,1)} %proj_ref.1) | copy-start | bytes 1769476
  15.6 20.8 %copy-start.3 = (s32[16384]{0:T(1024)S(1)}, s32[16384]{0:T(1024)}, u32[]{:S(2)}) copy-start(s32[16384]{0:T(1024)} %param.11) | copy-start | bytes 196612
  19.8 34.2 %all-to-all-start = ((bf16[16,144,128]{2,1,0:T(8,128)(2,1)}), bf16[16,144,128]{2,1,0:T(8,128)(2,1)S(1)}, u32[]{:S(2)}, u32[]{:S(2)}) async-start(bf16[16,144,128]{2,1,0:T(8,128)(2,1)} %source.1), calls=%async_computation.1 | async-start | bytes 1179648 | tf_op jit(solution)/shard_map/all_to_all | solution.py:144
  54.8 26.4 %all-to-all-start.1 = ((bf16[64,4,128]{2,1,0:T(4,128)(2,1)}), bf16[64,4,128]{2,1,0:T(4,128)(2,1)S(1)}, u32[]{:S(2)}, u32[]{:S(2)}) async-start(bf16[64,4,128]{2,1,0:T(4,128)(2,1)} %bitcast.4), calls=%async_computation.2 | async-start | bytes 131072 | tf_op jit(solution)/shard_map/all_to_all | solution.py:161
  82.2 21.3 %all-to-all-start.2 = ((bf16[8,256,128]{2,1,0:T(8,128)(2,1)}), bf16[8,256,128]{2,1,0:T(8,128)(2,1)S(1)}, u32[]{:S(2)}, u32[]{:S(2)}) async-start(bf16[8,256,128]{2,1,0:T(8,128)(2,1)} %broadcast_in_dim.78), calls=%async_computation.3 | async-start | bytes 1048576 | tf_op jit(solution)/shard_map/all_to_all | solution.py:164
  103.5 6.7 %collective-permute-start = (bf16[8,256,128]{2,1,0:T(8,128)(2,1)S(1)}, bf16[8,256,128]{2,1,0:T(8,128)(2,1)S(1)}, u32[]{:S(2)}, u32[]{:S(2)}) collective-permute-start(bf16[8,256,128]{2,1,0:T(8,128)(2,1)S(1)} %all-to-all-done.2.own_ref), channel_id=1, source_target_pairs={{0,1},{1,0},{2,3},{3,2},{4,5},{5,4},{6,7},{7,6},{8,9},{9,8},{10,11... | collective-permute-start | bytes 1572872 | tf_op jit(solution)/shard_map/ppermute | solution.py:167
  118.5 1.0 copy-start.2
Sparse Core Ops, SparseCore 0:
  15.7 102.7 reduce-scatter.1

commit v2 on v0

v2 whole, which is shorter than its diff:
```python
import functools

import jax
import jax.numpy as jnp
from jax import lax
from jax.experimental import pallas as pl
from jax.experimental.pallas import tpu as pltpu
from jax.sharding import Mesh
from jax.sharding import PartitionSpec as P

D = 4096
LANES = 128
STRIPE = 16
EPS = 1e-05
F32 = jnp.float32
BF16 = jnp.bfloat16
PARAMS = pltpu.CompilerParams(vmem_limit_bytes=32 * 2**20)


def vmem(n):
    return [pl.BlockSpec(memory_space=pltpu.VMEM)] * n


def one_hot(mask):
    return mask.astype(F32).astype(BF16)


def dot(a, b):
    return jnp.dot(a, b, preferred_element_type=F32)


def three_parts(x):
    hi = x.astype(BF16).astype(F32)
    rest = x - hi
    mid = rest.astype(BF16).astype(F32)
    low = (rest - mid).astype(BF16).astype(F32)
    return [hi, mid, low]


def source_kernel(target_ref, feats_ref, proj_ref, out_ref):
    projected = dot(feats_ref[...], proj_ref[...]).astype(BF16)
    slot = lax.broadcasted_iota(jnp.int32, (out_ref.shape[0], feats_ref.shape[0]), 0)
    place = one_hot(slot == target_ref[0:1, :])
    out_ref[...] = dot(place, projected).astype(BF16)


def source(target, feats, proj, slots):
    return pl.pallas_call(
        source_kernel,
        out_shape=jax.ShapeDtypeStruct((slots, proj.shape[1]), BF16),
        in_specs=vmem(3),
        out_specs=pl.BlockSpec(memory_space=pltpu.VMEM),
        compiler_params=PARAMS,
        name="source",
    )(target, feats, proj)


def copy_kernel(order_ref, block_ref, out_ref):
    out_ref[...] = block_ref[...]


def pick(order, blocks):
    n = order.shape[0]
    spec = (1,) + blocks.shape[1:]
    return pl.pallas_call(
        copy_kernel,
        out_shape=jax.ShapeDtypeStruct((n,) + blocks.shape[1:], blocks.dtype),
        grid_spec=pltpu.PrefetchScalarGridSpec(
            num_scalar_prefetch=1,
            grid=(n,),
            in_specs=[pl.BlockSpec(spec, lambda i, order: (order[i], 0, 0))],
            out_specs=pl.BlockSpec(spec, lambda i, order: (i, 0, 0)),
        ),
        compiler_params=PARAMS,
        name="pick",
    )(order, blocks)


def product_kernel(
    first, order_ref, own_ref, other_ref, w_own_ref, w_other_ref, v_own_ref, v_other_ref,
    slots_ref, out_ref, squares_ref,
):
    rows = own_ref.shape[1]
    block = order_ref[first + pl.program_id(0)]
    position = lax.broadcasted_iota(jnp.int32, (rows, slots_ref.shape[1]), 0) + block * rows
    hit = (position == slots_ref[0:1, :]).astype(F32)
    is_visual = jnp.sum(hit, axis=1, keepdims=True) > 0.5
    hit = hit.astype(BF16)
    ones = jnp.ones((8, own_ref.shape[2]), BF16)
    total = None
    lane_squares = None
    for text, visual, weight in (
        (own_ref, v_own_ref, w_own_ref),
        (other_ref, v_other_ref, w_other_ref),
    ):
        x = jnp.where(is_visual, dot(hit, visual[...]), text[0].astype(F32))
        term = dot(x.astype(BF16), weight[...])
        total = term if total is None else total + term
        square = x * x
        hi = square.astype(BF16)
        low = (square - hi.astype(F32)).astype(BF16)
        for part in (hi, low):
            term = lax.dot_general(
                ones, part, (((1,), (1,)), ((), ())), preferred_element_type=F32
            )
            lane_squares = term if lane_squares is None else lane_squares + term
    out_ref[0] = total.astype(BF16)
    squares_ref[0] = lane_squares


def products(order, first, count, own, other, w_own, w_other, v_own, v_other, slots):
    _, rows, feats = own.shape
    cols = w_own.shape[1]
    whole = lambda a: pl.BlockSpec(a.shape, lambda i, order: (0,) * a.ndim)
    return pl.pallas_call(
        functools.partial(product_kernel, first),
        out_shape=(
            jax.ShapeDtypeStruct((count, rows, cols), BF16),
            jax.ShapeDtypeStruct((count, 8, rows), F32),
        ),
        grid_spec=pltpu.PrefetchScalarGridSpec(
            num_scalar_prefetch=1,
            grid=(count,),
            in_specs=[
                pl.BlockSpec((1, rows, feats), lambda i, order: (order[first + i], 0, 0)),
                pl.BlockSpec((1, rows, feats), lambda i, order: (first + i, 0, 0)),
                whole(w_own),
                whole(w_other),
                whole(v_own),
                whole(v_other),
                whole(slots),
            ],
            out_specs=(
                pl.BlockSpec((1, rows, cols), lambda i, order: (i, 0, 0)),
                pl.BlockSpec((1, 8, rows), lambda i, order: (i, 0, 0)),
            ),
        ),
        compiler_params=PARAMS,
        cost_estimate=pl.CostEstimate(
            flops=count * 4 * rows * feats * (cols + slots.shape[1]),
            bytes_accessed=count * rows * (4 * feats + 2 * cols) + 8 * feats * cols,
            transcendentals=0,
        ),
        name="products",
    )(order, own, other, w_own, w_other, v_own, v_other, slots)


def stripe_of(squares, width):
    parts = three_parts(squares)
    pad = jnp.zeros((STRIPE - 3, squares.shape[1]), F32)
    stripe = jnp.concatenate(parts + [pad], axis=0)
    return stripe.astype(BF16)


def stripe_sum(stripe):
    return stripe[0:1] + stripe[1:2] + stripe[2:3]


def leaf_kernel(part, product_ref, squares_ref, out_ref):
    rows = product_ref.shape[1]
    out_ref[:rows, :] = product_ref[0]
    if part == 0:
        squares = squares_ref[0, 0:1, :]
        wide = jnp.concatenate([squares, jnp.zeros_like(squares)], axis=1)
        out_ref[rows:, :] = stripe_of(wide, out_ref.shape[1])


def hop_kernel(part, came_rows, product_ref, squares_ref, came_ref, out_ref):
    rows = product_ref.shape[1]
    for i in range(2):
        to = slice(i * rows, (i + 1) * rows)
        if i * rows < came_rows:
            total = product_ref[i].astype(F32) + came_ref[to, :].astype(F32)
            out_ref[to, :] = total.astype(BF16)
        else:
            out_ref[to, :] = product_ref[i]
    if part == 0:
        squares = jnp.concatenate([squares_ref[0, 0:1, :], squares_ref[1, 0:1, :]], axis=1)
        squares += stripe_sum(came_ref[came_rows:, :].astype(F32))
        out_ref[2 * rows :, :] = stripe_of(squares, out_ref.shape[1])


def add_call(kernel, name, part, at, count, product, squares, came, cols, rows_out):
    rows = product.shape[1]
    whole = lambda a: pl.BlockSpec(a.shape, lambda i: (0,) * a.ndim)
    return pl.pallas_call(
        kernel,
        out_shape=jax.ShapeDtypeStruct((rows_out, cols), BF16),
        grid=(1,),
        in_specs=[
            pl.BlockSpec((pl.Element(count), pl.Element(rows), pl.Element(cols)), lambda i: (at, 0, part * cols)),
            pl.BlockSpec((pl.Element(count), pl.Element(8), pl.Element(rows)), lambda i: (at, 0, 0)),
        ]
        + [whole(a) for a in came],
        out_specs=pl.BlockSpec((rows_out, cols), lambda i: (0, 0)),
        compiler_params=PARAMS,
        name=name,
    )(product, squares, *came)


def finish_kernel(product_ref, squares_ref, k_ref, v_ref, k2_ref, v2_ref, key_ref, value_ref):
    rows = product_ref.shape[1]
    cols = key_ref.shape[1]
    squares = squares_ref[0, 0:1, :]
    squares += stripe_sum(k_ref[2 * rows :, :].astype(F32))[:, :rows]
    squares += stripe_sum(k2_ref[rows:, :].astype(F32))[:, rows:]
    inverse = lax.rsqrt(squares / D + EPS)
    for i in range(rows // LANES):
        to = slice(i * LANES, (i + 1) * LANES)
        scale = jnp.broadcast_to(inverse[:, to], (LANES, LANES)).T
        for out_ref, a_ref, b_ref, at in (
            (key_ref, k_ref, k2_ref, 0),
            (value_ref, v_ref, v2_ref, cols),
        ):
            for j in range(cols // LANES):
                lane = slice(j * LANES, (j + 1) * LANES)
                own = product_ref[0, to, at + j * LANES : at + (j + 1) * LANES].astype(F32)
                total = own + a_ref[to, lane].astype(F32) + b_ref[to, lane].astype(F32)
                out_ref[to, lane] = (total * scale).astype(BF16)


def finish(product, squares, k, v, k2, v2, cols):
    rows = product.shape[1]
    whole = lambda a: pl.BlockSpec(a.shape, lambda i: (0,) * a.ndim)
    last = product.shape[0] - 1
    return pl.pallas_call(
        finish_kernel,
        out_shape=(jax.ShapeDtypeStruct((rows, cols), BF16),) * 2,
        grid=(1,),
        in_specs=[
            pl.BlockSpec((1,) + product.shape[1:], lambda i: (last, 0, 0)),
            pl.BlockSpec((1,) + squares.shape[1:], lambda i: (last, 0, 0)),
        ]
        + [whole(a) for a in (k, v, k2, v2)],
        out_specs=(pl.BlockSpec((rows, cols), lambda i: (0, 0)),) * 2,
        compiler_params=PARAMS,
        name="finish",
    )(product, squares, k, v, k2, v2)


def local(vis_feats, proj_w, text_embed, dest_group, layout, norm_gain, key_w, value_w):
    n_grp = lax.axis_size("grp")
    n_y = lax.axis_size("y")
    h = lax.axis_index("grp")
    y = lax.axis_index("y")
    c = lax.axis_index("core")
    seq_len, feats = text_embed.shape
    rows = seq_len // (2 * n_y)
    tokens = vis_feats.shape[0]
    run_count = n_grp // 2
    capacity = tokens // run_count
    slot_count = n_grp * capacity
    cols = key_w.shape[1]
    swap = [(0, 1), (1, 0)]
    ring = []
    for i in range(n_y):
        ring.append((2 * i, 2 * ((i + 1) % n_y)))
        ring.append((2 * i + 1, 2 * ((i - 1) % n_y) + 1))

    own_dest = lax.dynamic_slice_in_dim(dest_group, h * tokens, tokens, 0)
    target = own_dest * capacity + jnp.arange(tokens, dtype=jnp.int32) % capacity
    target = jnp.broadcast_to(target[None, :], (8, tokens))
    outgoing = source(target, vis_feats, proj_w, slot_count)
    arrived = lax.all_to_all(
        outgoing.reshape(n_grp, capacity, feats), "grp", 0, 0, tiled=True
    ).reshape(slot_count, feats)

    weight = jnp.concatenate([key_w, value_w], axis=1).astype(F32) * norm_gain[:, None]
    weight = weight.astype(BF16)
    w_other = lax.ppermute(weight, "core", swap)

    far = n_y // 2
    offset = [far] + [o for o in range(far - 1, 0, -1) for _ in (0, 1)] + [0]
    second = [0] + [0, 1] * (far - 1) + [0]
    offset = jnp.asarray(offset, jnp.int32)
    second = jnp.asarray(second, jnp.int32)
    up = 2 * ((y + offset) % n_y) + second
    down = 2 * ((y - offset + n_y) % n_y) + 1 - second
    mine = jnp.where(c == 0, up, down)
    theirs = jnp.where(c == 0, down, up)
    blocks = text_embed.reshape(2 * n_y, rows, feats)
    other = lax.ppermute(pick(theirs, blocks), "core", swap)

    run_heads = dest_group.reshape(n_grp, run_count, capacity)[:, :, 0]
    senders = jnp.any(run_heads == h, axis=1)
    group = jnp.arange(n_grp, dtype=jnp.int32)
    earlier = jnp.sum(
        jnp.where(senders[None, :] & (group[None, :] < group[:, None]), 1, 0), axis=1
    )
    first_ranks = layout[0, :slot_count].reshape(n_grp, capacity)
    where = jnp.sum(
        jnp.where((earlier[:, None] == group[None, :])[:, :, None], first_ranks[None], 0), axis=1
    )
    where = jnp.where(senders[:, None], where, -1)
    slots = jnp.broadcast_to(where.reshape(1, slot_count), (8, slot_count))

    arrived_other = lax.ppermute(arrived, "core", swap)
    operands = (blocks, other, weight, w_other, arrived, arrived_other, slots)
    leaf, leaf_squares = products(mine, 0, 1, *operands)
    product, squares = products(mine, 1, n_y - 1, *operands)

    flat = ("y", "core")
    streams = []
    for part in range(2):
        sent = add_call(
            functools.partial(leaf_kernel, part), "leaf", part, 0, 1, leaf, leaf_squares, [],
            cols, rows + (STRIPE if part == 0 else 0),
        )
        streams.append(lax.ppermute(sent, flat, ring))
    came_rows = rows
    for step in range(far - 1):
        for part in range(2):
            sent = add_call(
                functools.partial(hop_kernel, part, came_rows), "hop", part, 2 * step, 2,
                product, squares, [streams[part]], cols,
                2 * rows + (STRIPE if part == 0 else 0),
            )
            streams[part] = lax.ppermute(sent, flat, ring)
        came_rows = 2 * rows
    key_sums, value_sums = streams
    key_rest = lax.ppermute(key_sums[rows:], "core", swap)
    value_rest = lax.ppermute(value_sums[rows:], "core", swap)
    return finish(product, squares, key_sums, value_sums, key_rest, value_rest, cols)


def solution(mesh):
    n_grp, n_sp = mesh.devices.shape
    split = Mesh(mesh.devices.reshape(n_grp, n_sp // 2, 2), ("grp", "y", "core"))
    sp = ("y", "core")
    return jax.shard_map(
        local,
        mesh=split,
        in_specs=(
            P("grp", None),
            P(None, sp),
            P("grp", sp),
            P(),
            P("grp", None),
            P(sp),
            P(sp, None),
            P(sp, None),
        ),
        out_specs=(P(("grp", "y", "core"), None), P(("grp", "y", "core"), None)),
        check_vma=False,
    )
```

time: 188 us -> 121 us (0.64)
  waiting for transfers between devices: 75.9 us -> 15.3 us
  starting transfers between devices: 23.2 us -> 73.3 us
  blocking collectives: 47.9 us -> 0 us
  Pallas kernels: 0 us -> 18.4 us
  between operations: 14.2 us -> 0.96 us
  local copies, waits for them, and re-layouts: 14.2 us -> 6.26 us
  matrix products: 7.35 us -> 0 us
    ppermute x0 -> x13, starting transfers between devices: none -> 50.5 us  [the longest x6 21.6 us: local(): streams[part] = lax.ppermute(sent, flat, ring)]
    all_to_all x1, waiting for transfers between devices: 50.1 us -> 2.23 us  [local(): lax.all_to_all(outgoing.reshape(n_grp, capacity, feats), 'grp', 0, 0, til...]
    psum x1 -> x0, blocking collectives: 47.9 us -> none  [local(): totals = lax.psum(squares, 'sp')]
    reduce_scatter x1 -> x0, waiting for transfers between devices: 25.7 us -> none  [local(): lax.psum_scatter(jnp.dot(scaled, kv_weight, preferred_element_type=jnp.fl...]
    pallas_call x0 -> x13, Pallas kernels: none -> 18.4 us  [the longest x2 11.9 us: products(): pl.pallas_call(functools.partial(product_kernel, first), out_shape=(jax.S...]
    ppermute x0 -> x13, waiting for transfers between devices: none -> 13.1 us  [the longest x6 10.9 us: local(): streams[part] = lax.ppermute(sent, flat, ring)]
    scatter x2 -> x0, local copies, waits for them, and re-layouts: 7.92 us -> none  [the longest x1 4.39 us: local(): outgoing.at[own_runs].set(vis_feats.reshape(run_count, capacity, raw_width))]
    dot_general x2 -> x0, matrix products: 7.35 us -> none  [the longest x1 5.57 us: local(): jnp.dot(scaled, kv_weight, preferred_element_type=jnp.float32)]
  transfers between devices with their start and end apart: 2 -> 14, of which waited for: 2 -> 8; matrix products, arithmetic and copies ran while one was open for 3% -> 6% of each run, Pallas kernels for 0% -> 11%
where the time goes in v2:
time: 121 us; the launch traced here: 120 us
  starting transfers between devices  73.3 us (61%)
  Pallas kernels  18.4 us (15%)
  waiting for transfers between devices  15.3 us (13%)
  local copies, waits for them, and re-layouts  6.26 us (5%)
  other arithmetic  5.54 us (5%)
    all_to_all x1, starting transfers between devices, local(): lax.all_to_all(outgoing.reshape(n_grp, capacity, feats), 'grp', 0, 0, til...  22.8 us
    ppermute x6, starting transfers between devices, local(): streams[part] = lax.ppermute(sent, flat, ring)  21.6 us
    pallas_call x2, Pallas kernels, products(): pl.pallas_call(functools.partial(product_kernel, first), out_shape=(jax.S...  11.9 us
    ppermute x6, waiting for transfers between devices, local(): streams[part] = lax.ppermute(sent, flat, ring)  10.9 us
    ppermute x2, starting transfers between devices, local(): streams.append(lax.ppermute(sent, flat, ring))  8.08 us
    ppermute x1, starting transfers between devices, local(): key_rest = lax.ppermute(key_sums[rows:], 'core', swap)  5.65 us
    ppermute x1, starting transfers between devices, local(): value_rest = lax.ppermute(value_sums[rows:], 'core', swap)  5.57 us
    ppermute x1, starting transfers between devices, local(): arrived_other = lax.ppermute(arrived, 'core', swap)  4.78 us
  transfers between devices with their start and end apart: 14, of which 8 were waited for; matrix products, arithmetic and copies ran while one was open for 6% of the time, Pallas kernels for 11%

profile of v2, /device:TPU:1, one launch (start us, length us, event | category | flops | bytes accessed | tf_op | source)
XLA Modules:
  0.0 119.8 jit_solution(8228755078399995)
XLA Ops:
  1.4 1.1 copy-done.2
  2.5 1.1 copy-done.3
  3.6 1.4 %source.1 = bf16[512,256]{1,0:T(8,128)(2,1)} custom-call(s32[8,256]{1,0:T(8,128)S(1)} %broadcast_in_dim.61.target_ref, bf16[256,1152]{1,0:T(8,128)(2,1)S(1)} %copy-done.2, bf16[1152,256]{1,0:T(8,128)(2,1)S(1)} %copy-done.3), custom_call_target="tpu_custom_call" | custom-call | tf_op jit(solution)/shard_map/source/pallas_call | solution.py:48
  4.9 22.8 %all-to-all-start = ((bf16[64,8,256]{2,1,0:T(8,128)(2,1)}), bf16[64,8,256]{2,1,0:T(8,128)(2,1)S(1)}, u32[]{:S(2)}, u32[]{:S(2)}) async-start(bf16[64,8,256]{2,1,0:T(8,128)(2,1)} %bitcast.1), calls=%async_computation | async-start | bytes 524288 | tf_op jit(solution)/shard_map/all_to_all | solution.py:264
  28.4 1.6 %copy-done = bf16[4096,256]{1,0:T(8,128)(2,1)S(1)} copy-done((bf16[4096,256]{1,0:T(8,128)(2,1)S(1)}, bf16[4096,256]{1,0:T(8,128)(2,1)}, u32[]{:S(2)}) %copy-start) | copy-done | bytes 2097176
  30.0 3.3 %pick.1 = bf16[8,256,256]{2,1,0:T(8,128)(2,1)} custom-call(s32[8]{0:T(128)S(1)} %get-tuple-element.10.order_ref, bf16[16,256,256]{2,1,0:T(8,128)(2,1)S(1)} %bitcast.3), custom_call_target="tpu_custom_call" | custom-call | tf_op jit(solution)/shard_map/pick/pallas_call | solution.py:65
  33.3 2.9 %collective-permute-start = (bf16[8,256,256]{2,1,0:T(8,128)(2,1)}, bf16[8,256,256]{2,1,0:T(8,128)(2,1)}, u32[]{:S(2)}, u32[]{:S(2)}) collective-permute-start(bf16[8,256,256]{2,1,0:T(8,128)(2,1)} %pick.1), channel_id=1, source_target_pairs={{0,1},{1,0},{2,3},{3,2},{4,5},{5,4},{6,7},{7,6},{8,9},{9,8},{10,11... | collective-permute-start | bytes 3145736 | tf_op jit(solution)/shard_map/ppermute | solution.py:282
  36.3 1.9 %collective-permute-start.1 = (bf16[256,1024]{1,0:T(8,128)(2,1)S(1)}, bf16[256,1024]{1,0:T(8,128)(2,1)S(1)}, u32[]{:S(2)}, u32[]{:S(2)}) collective-permute-start(bf16[256,1024]{1,0:T(8,128)(2,1)S(1)} %multiply_convert_fusion.w_own_ref), channel_id=1, source_target_pairs={{0,1},{1,0},{2,3},{3,2},{4,5},{5,4},{6,7},{7,6},{8,9},{9,8},{10,11... | collective-permute-start | bytes 1572872 | tf_op jit(solution)/shard_map/ppermute | solution.py:270
  38.3 1.6 %reshape.61 = s32[64,32,8]{2,1,0:T(8,128)} reshape(s32[16384]{0:T(1024)S(1)} %copy-done.6) | data formatting | bytes 131072 | tf_op jit(solution)/shard_map/reshape | solution.py:284
  40.7 2.5 %fusion = pred[64]{0:T(512)(128)(4,1)S(1)} fusion(s32[64,32,8]{2,1,0:T(8,128)} %reshape.61, s32[]{:T(128)S(6)} %axis_index.38), kind=kLoop, calls=%fused_computation.2 | loop fusion | flops 4032 | bytes 8260 | tf_op jit(solution)/shard_map/reduce_or | solution.py:285
  43.4 1.2 select_reduce_fusion
  44.5 2.2 %all-to-all-done = bf16[64,8,256]{2,1,0:T(8,128)(2,1)S(1)} async-done(((bf16[64,8,256]{2,1,0:T(8,128)(2,1)}), bf16[64,8,256]{2,1,0:T(8,128)(2,1)S(1)}, u32[]{:S(2)}, u32[]{:S(2)}) %all-to-all-start) | async-done | bytes 262176 | tf_op jit(solution)/shard_map/all_to_all | solution.py:264
  46.8 4.8 %collective-permute-start.2 = (bf16[512,256]{1,0:T(8,128)(2,1)S(1)}, bf16[512,256]{1,0:T(8,128)(2,1)}, u32[]{:S(2)}, u32[]{:S(2)}) collective-permute-start(bf16[512,256]{1,0:T(8,128)(2,1)S(1)} %bitcast.6), channel_id=1, source_target_pairs={{0,1},{1,0},{2,3},{3,2},{4,5},{5,4},{6,7},{7,6},{8,9},{9,8},{10,11... | collective-permute-start | bytes 786440 | tf_op jit(solution)/shard_map/ppermute | solution.py:297
  51.7 1.1 collective-permute-done.2.v_other_ref
  52.8 2.6 %products.3 = (bf16[1,256,1024]{2,1,0:T(8,128)(2,1)S(1)}, f32[1,8,256]{2,1,0:T(8,128)S(1)}) custom-call(s32[8]{0:T(128)S(1)} %broadcast_select_fusion.2.order_ref, bf16[16,256,256]{2,1,0:T(8,128)(2,1)S(1)} %bitcast.4, bf16[8,256,256]{2,1,0:T(8,128)(2,1)} %collective-permute-done.other_ref, bf16[256,1024]{1,0:T(8,128)(2,1)S(1)} %multiply_convert_fusion.w_own_ref, ...), custom_call_target="tpu_custom_call" | custom-call | flops 402653184 | bytes 2883584 | tf_op jit(solution)/shard_map/products/pallas_call | solution.py:115
  55.5 5.1 %collective-permute-start.3 = (bf16[272,512]{1,0:T(8,128)(2,1)S(1)}, bf16[272,512]{1,0:T(8,128)(2,1)S(1)}, u32[]{:S(2)}, u32[]{:S(2)}) collective-permute-start(bf16[272,512]{1,0:T(8,128)(2,1)S(1)} %leaf.2), channel_id=1, source_target_pairs={{0,2},{1,15},{2,4},{3,1},{4,6},{5,3},{6,8},{7,5},{8,10},{9,7},{10,... | collective-permute-start | bytes 835592 | tf_op jit(solution)/shard_map/ppermute | solution.py:309
  60.6 3.0 %collective-permute-start.7 = (bf16[256,512]{1,0:T(8,128)(2,1)S(1)}, bf16[256,512]{1,0:T(8,128)(2,1)S(1)}, u32[]{:S(2)}, u32[]{:S(2)}) collective-permute-start(bf16[256,512]{1,0:T(8,128)(2,1)S(1)} %leaf.3), channel_id=1, source_target_pairs={{0,2},{1,15},{2,4},{3,1},{4,6},{5,3},{6,8},{7,5},{8,10},{9,7},{10,... | collective-permute-start | bytes 786440 | tf_op jit(solution)/shard_map/ppermute | solution.py:309
  63.6 9.3 %products.2 = (bf16[7,256,1024]{2,1,0:T(8,128)(2,1)S(1)}, f32[7,8,256]{2,1,0:T(8,128)S(1)}) custom-call(s32[8]{0:T(128)S(1)} %broadcast_select_fusion.2.order_ref, bf16[16,256,256]{2,1,0:T(8,128)(2,1)S(1)} %bitcast.5, bf16[8,256,256]{2,1,0:T(8,128)(2,1)} %collective-permute-done.other_ref, bf16[256,1024]{1,0:T(8,128)(2,1)S(1)} %multiply_convert_fusion.w_own_ref, ...), custom_call_target="tpu_custom_call" | custom-call | flops 2818572288 | bytes 7602176 | tf_op jit(solution)/shard_map/products/pallas_call | solution.py:115
  73.0 3.0 %collective-permute-start.4 = (bf16[528,512]{1,0:T(8,128)(2,1)S(1)}, bf16[528,512]{1,0:T(8,128)(2,1)S(1)}, u32[]{:S(2)}, u32[]{:S(2)}) collective-permute-start(bf16[528,512]{1,0:T(8,128)(2,1)S(1)} %hop.6), channel_id=1, source_target_pairs={{0,2},{1,15},{2,4},{3,1},{4,6},{5,3},{6,8},{7,5},{8,10},{9,7},{10,... | collective-permute-start | bytes 1622024 | tf_op jit(solution)/shard_map/ppermute | solution.py:318
  76.1 3.0 %collective-permute-start.8 = (bf16[512,512]{1,0:T(8,128)(2,1)S(1)}, bf16[512,512]{1,0:T(8,128)(2,1)S(1)}, u32[]{:S(2)}, u32[]{:S(2)}) collective-permute-start(bf16[512,512]{1,0:T(8,128)(2,1)S(1)} %hop.9), channel_id=1, source_target_pairs={{0,2},{1,15},{2,4},{3,1},{4,6},{5,3},{6,8},{7,5},{8,10},{9,7},{10,... | collective-permute-start | bytes 1572872 | tf_op jit(solution)/shard_map/ppermute | solution.py:318
  79.1 4.4 %collective-permute-done.4.came_ref = bf16[528,512]{1,0:T(8,128)(2,1)S(1)} collective-permute-done((bf16[528,512]{1,0:T(8,128)(2,1)S(1)}, bf16[528,512]{1,0:T(8,128)(2,1)S(1)}, u32[]{:S(2)}, u32[]{:S(2)}) %collective-permute-start.4) | collective-permute-done | bytes 540704 | tf_op jit(solution)/shard_map/ppermute | solution.py:318
  83.6 3.9 %collective-permute-start.5 = (bf16[528,512]{1,0:T(8,128)(2,1)S(1)}, bf16[528,512]{1,0:T(8,128)(2,1)S(1)}, u32[]{:S(2)}, u32[]{:S(2)}) collective-permute-start(bf16[528,512]{1,0:T(8,128)(2,1)S(1)} %hop.7), channel_id=1, source_target_pairs={{0,2},{1,15},{2,4},{3,1},{4,6},{5,3},{6,8},{7,5},{8,10},{9,7},{10,... | collective-permute-start | bytes 1622024 | tf_op jit(solution)/shard_map/ppermute | solution.py:318
  87.5 1.6 %collective-permute-done.8.came_ref = bf16[512,512]{1,0:T(8,128)(2,1)S(1)} collective-permute-done((bf16[512,512]{1,0:T(8,128)(2,1)S(1)}, bf16[512,512]{1,0:T(8,128)(2,1)S(1)}, u32[]{:S(2)}, u32[]{:S(2)}) %collective-permute-start.8) | collective-permute-done | bytes 524320 | tf_op jit(solution)/shard_map/ppermute | solution.py:318
  89.2 3.9 %collective-permute-start.9 = (bf16[512,512]{1,0:T(8,128)(2,1)S(1)}, bf16[512,512]{1,0:T(8,128)(2,1)S(1)}, u32[]{:S(2)}, u32[]{:S(2)}) collective-permute-start(bf16[512,512]{1,0:T(8,128)(2,1)S(1)} %hop.10), channel_id=1, source_target_pairs={{0,2},{1,15},{2,4},{3,1},{4,6},{5,3},{6,8},{7,5},{8,10},{9,7},{10,... | collective-permute-start | bytes 1572872 | tf_op jit(solution)/shard_map/ppermute | solution.py:318
  93.1 1.8 %collective-permute-done.5.came_ref = bf16[528,512]{1,0:T(8,128)(2,1)S(1)} collective-permute-done((bf16[528,512]{1,0:T(8,128)(2,1)S(1)}, bf16[528,512]{1,0:T(8,128)(2,1)S(1)}, u32[]{:S(2)}, u32[]{:S(2)}) %collective-permute-start.5) | collective-permute-done | bytes 540704 | tf_op jit(solution)/shard_map/ppermute | solution.py:318
  95.0 4.0 %collective-permute-start.6 = (bf16[528,512]{1,0:T(8,128)(2,1)S(1)}, bf16[528,512]{1,0:T(8,128)(2,1)S(1)}, u32[]{:S(2)}, u32[]{:S(2)}) collective-permute-start(bf16[528,512]{1,0:T(8,128)(2,1)S(1)} %hop.8), channel_id=1, source_target_pairs={{0,2},{1,15},{2,4},{3,1},{4,6},{5,3},{6,8},{7,5},{8,10},{9,7},{10,... | collective-permute-start | bytes 1622024 | tf_op jit(solution)/shard_map/ppermute | solution.py:318
  99.0 1.5 %collective-permute-done.9.came_ref = bf16[512,512]{1,0:T(8,128)(2,1)S(1)} collective-permute-done((bf16[512,512]{1,0:T(8,128)(2,1)S(1)}, bf16[512,512]{1,0:T(8,128)(2,1)S(1)}, u32[]{:S(2)}, u32[]{:S(2)}) %collective-permute-start.9) | collective-permute-done | bytes 524320 | tf_op jit(solution)/shard_map/ppermute | solution.py:318
  100.6 3.9 %collective-permute-start.10 = (bf16[512,512]{1,0:T(8,128)(2,1)S(1)}, bf16[512,512]{1,0:T(8,128)(2,1)S(1)}, u32[]{:S(2)}, u32[]{:S(2)}) collective-permute-start(bf16[512,512]{1,0:T(8,128)(2,1)S(1)} %hop.11), channel_id=1, source_target_pairs={{0,2},{1,15},{2,4},{3,1},{4,6},{5,3},{6,8},{7,5},{8,10},{9,7},{10,... | collective-permute-start | bytes 1572872 | tf_op jit(solution)/shard_map/ppermute | solution.py:318
  104.6 1.7 %collective-permute-done.6.k_ref = bf16[528,512]{1,0:T(8,128)(2,1)S(1)} collective-permute-done((bf16[528,512]{1,0:T(8,128)(2,1)S(1)}, bf16[528,512]{1,0:T(8,128)(2,1)S(1)}, u32[]{:S(2)}, u32[]{:S(2)}) %collective-permute-start.6) | collective-permute-done | bytes 540704 | tf_op jit(solution)/shard_map/ppermute | solution.py:318
  106.3 5.6 %collective-permute-start.11 = (bf16[272,512]{1,0:T(8,128)(2,1)S(1)}, bf16[272,512]{1,0:T(8,128)(2,1)S(1)}, u32[]{:S(2)}, u32[]{:S(2)}) collective-permute-start(bf16[272,512]{1,0:T(8,128)(2,1)S(1)} %slice.17), channel_id=1, source_target_pairs={{0,1},{1,0},{2,3},{3,2},{4,5},{5,4},{6,7},{7,6},{8,9},{9,8},{10,11... | collective-permute-start | bytes 835592 | tf_op jit(solution)/shard_map/ppermute | solution.py:321
  112.0 5.6 %collective-permute-start.12 = (bf16[256,512]{1,0:T(8,128)(2,1)S(1)}, bf16[256,512]{1,0:T(8,128)(2,1)S(1)}, u32[]{:S(2)}, u32[]{:S(2)}) collective-permute-start(bf16[256,512]{1,0:T(8,128)(2,1)S(1)} %slice.18), channel_id=1, source_target_pairs={{0,1},{1,0},{2,3},{3,2},{4,5},{5,4},{6,7},{7,6},{8,9},{9,8},{10,11... | collective-permute-start | bytes 786440 | tf_op jit(solution)/shard_map/ppermute | solution.py:322
  117.6 1.1 collective-permute-done.12.v2_ref
  (43 shorter events, 4.8 us)
Async XLA Ops:
  0.6 35.5 %copy-start.7 = (f32[256]{0:T(256)S(1)}, f32[256]{0:T(256)}, u32[]{:S(2)}) copy-start(f32[256]{0:T(256)} %param.15) | copy-start | bytes 3076
  1.4 1.1 copy-start.2
  2.5 1.1 copy-start.3
  3.5 32.6 %copy-start.4 = (bf16[256,512]{1,0:T(8,128)(2,1)S(1)}, bf16[256,512]{1,0:T(8,128)(2,1)}, u32[]{:S(2)}) copy-start(bf16[256,512]{1,0:T(8,128)(2,1)} %param.17) | copy-start | bytes 786436
  3.5 32.6 %copy-start.5 = (bf16[256,512]{1,0:T(8,128)(2,1)S(1)}, bf16[256,512]{1,0:T(8,128)(2,1)}, u32[]{:S(2)}) copy-start(bf16[256,512]{1,0:T(8,128)(2,1)} %param.16) | copy-start | bytes 786436
  3.6 34.7 %copy-start.6 = (s32[16384]{0:T(1024)S(1)}, s32[16384]{0:T(1024)}, u32[]{:S(2)}) copy-start(s32[16384]{0:T(1024)} %param.13) | copy-start | bytes 196612
  4.9 41.8 %all-to-all-start = ((bf16[64,8,256]{2,1,0:T(8,128)(2,1)}), bf16[64,8,256]{2,1,0:T(8,128)(2,1)S(1)}, u32[]{:S(2)}, u32[]{:S(2)}) async-start(bf16[64,8,256]{2,1,0:T(8,128)(2,1)} %bitcast.1), calls=%async_computation | async-start | bytes 524288 | tf_op jit(solution)/shard_map/all_to_all | solution.py:264
  28.4 1.6 %copy-start = (bf16[4096,256]{1,0:T(8,128)(2,1)S(1)}, bf16[4096,256]{1,0:T(8,128)(2,1)}, u32[]{:S(2)}) copy-start(bf16[4096,256]{1,0:T(8,128)(2,1)} %param.12) | copy-start | bytes 6291460
  30.0 22.8 %copy-start.1 = (bf16[4096,256]{1,0:T(8,128)(2,1)S(1)}, bf16[4096,256]{1,0:T(8,128)(2,1)}, u32[]{:S(2)}) copy-start(bf16[4096,256]{1,0:T(8,128)(2,1)} %param.12) | copy-start | bytes 6291460
  33.3 18.4 %collective-permute-start = (bf16[8,256,256]{2,1,0:T(8,128)(2,1)}, bf16[8,256,256]{2,1,0:T(8,128)(2,1)}, u32[]{:S(2)}, u32[]{:S(2)}) collective-permute-start(bf16[8,256,256]{2,1,0:T(8,128)(2,1)} %pick.1), channel_id=1, source_target_pairs={{0,1},{1,0},{2,3},{3,2},{4,5},{5,4},{6,7},{7,6},{8,9},{9,8},{10,11... | collective-permute-start | bytes 3145736 | tf_op jit(solution)/shard_map/ppermute | solution.py:282
  36.3 15.4 %collective-permute-start.1 = (bf16[256,1024]{1,0:T(8,128)(2,1)S(1)}, bf16[256,1024]{1,0:T(8,128)(2,1)S(1)}, u32[]{:S(2)}, u32[]{:S(2)}) collective-permute-start(bf16[256,1024]{1,0:T(8,128)(2,1)S(1)} %multiply_convert_fusion.w_own_ref), channel_id=1, source_target_pairs={{0,1},{1,0},{2,3},{3,2},{4,5},{5,4},{6,7},{7,6},{8,9},{9,8},{10,11... | collective-permute-start | bytes 1572872 | tf_op jit(solution)/shard_map/ppermute | solution.py:270
  46.8 6.1 %collective-permute-start.2 = (bf16[512,256]{1,0:T(8,128)(2,1)S(1)}, bf16[512,256]{1,0:T(8,128)(2,1)}, u32[]{:S(2)}, u32[]{:S(2)}) collective-permute-start(bf16[512,256]{1,0:T(8,128)(2,1)S(1)} %bitcast.6), channel_id=1, source_target_pairs={{0,1},{1,0},{2,3},{3,2},{4,5},{5,4},{6,7},{7,6},{8,9},{9,8},{10,11... | collective-permute-start | bytes 786440 | tf_op jit(solution)/shard_map/ppermute | solution.py:297
  55.5 17.4 %collective-permute-start.3 = (bf16[272,512]{1,0:T(8,128)(2,1)S(1)}, bf16[272,512]{1,0:T(8,128)(2,1)S(1)}, u32[]{:S(2)}, u32[]{:S(2)}) collective-permute-start(bf16[272,512]{1,0:T(8,128)(2,1)S(1)} %leaf.2), channel_id=1, source_target_pairs={{0,2},{1,15},{2,4},{3,1},{4,6},{5,3},{6,8},{7,5},{8,10},{9,7},{10,... | collective-permute-start | bytes 835592 | tf_op jit(solution)/shard_map/ppermute | solution.py:309
  60.6 15.4 %collective-permute-start.7 = (bf16[256,512]{1,0:T(8,128)(2,1)S(1)}, bf16[256,512]{1,0:T(8,128)(2,1)S(1)}, u32[]{:S(2)}, u32[]{:S(2)}) collective-permute-start(bf16[256,512]{1,0:T(8,128)(2,1)S(1)} %leaf.3), channel_id=1, source_target_pairs={{0,2},{1,15},{2,4},{3,1},{4,6},{5,3},{6,8},{7,5},{8,10},{9,7},{10,... | collective-permute-start | bytes 786440 | tf_op jit(solution)/shard_map/ppermute | solution.py:309
  73.0 10.4 %collective-permute-start.4 = (bf16[528,512]{1,0:T(8,128)(2,1)S(1)}, bf16[528,512]{1,0:T(8,128)(2,1)S(1)}, u32[]{:S(2)}, u32[]{:S(2)}) collective-permute-start(bf16[528,512]{1,0:T(8,128)(2,1)S(1)} %hop.6), channel_id=1, source_target_pairs={{0,2},{1,15},{2,4},{3,1},{4,6},{5,3},{6,8},{7,5},{8,10},{9,7},{10,... | collective-permute-start | bytes 1622024 | tf_op jit(solution)/shard_map/ppermute | solution.py:318
  76.1 12.9 %collective-permute-start.8 = (bf16[512,512]{1,0:T(8,128)(2,1)S(1)}, bf16[512,512]{1,0:T(8,128)(2,1)S(1)}, u32[]{:S(2)}, u32[]{:S(2)}) collective-permute-start(bf16[512,512]{1,0:T(8,128)(2,1)S(1)} %hop.9), channel_id=1, source_target_pairs={{0,2},{1,15},{2,4},{3,1},{4,6},{5,3},{6,8},{7,5},{8,10},{9,7},{10,... | collective-permute-start | bytes 1572872 | tf_op jit(solution)/shard_map/ppermute | solution.py:318
  83.6 11.3 %collective-permute-start.5 = (bf16[528,512]{1,0:T(8,128)(2,1)S(1)}, bf16[528,512]{1,0:T(8,128)(2,1)S(1)}, u32[]{:S(2)}, u32[]{:S(2)}) collective-permute-start(bf16[528,512]{1,0:T(8,128)(2,1)S(1)} %hop.7), channel_id=1, source_target_pairs={{0,2},{1,15},{2,4},{3,1},{4,6},{5,3},{6,8},{7,5},{8,10},{9,7},{10,... | collective-permute-start | bytes 1622024 | tf_op jit(solution)/shard_map/ppermute | solution.py:318
  89.2 11.3 %collective-permute-start.9 = (bf16[512,512]{1,0:T(8,128)(2,1)S(1)}, bf16[512,512]{1,0:T(8,128)(2,1)S(1)}, u32[]{:S(2)}, u32[]{:S(2)}) collective-permute-start(bf16[512,512]{1,0:T(8,128)(2,1)S(1)} %hop.10), channel_id=1, source_target_pairs={{0,2},{1,15},{2,4},{3,1},{4,6},{5,3},{6,8},{7,5},{8,10},{9,7},{10,... | collective-permute-start | bytes 1572872 | tf_op jit(solution)/shard_map/ppermute | solution.py:318
  95.0 11.3 %collective-permute-start.6 = (bf16[528,512]{1,0:T(8,128)(2,1)S(1)}, bf16[528,512]{1,0:T(8,128)(2,1)S(1)}, u32[]{:S(2)}, u32[]{:S(2)}) collective-permute-start(bf16[528,512]{1,0:T(8,128)(2,1)S(1)} %hop.8), channel_id=1, source_target_pairs={{0,2},{1,15},{2,4},{3,1},{4,6},{5,3},{6,8},{7,5},{8,10},{9,7},{10,... | collective-permute-start | bytes 1622024 | tf_op jit(solution)/shard_map/ppermute | solution.py:318
  100.6 11.3 %collective-permute-start.10 = (bf16[512,512]{1,0:T(8,128)(2,1)S(1)}, bf16[512,512]{1,0:T(8,128)(2,1)S(1)}, u32[]{:S(2)}, u32[]{:S(2)}) collective-permute-start(bf16[512,512]{1,0:T(8,128)(2,1)S(1)} %hop.11), channel_id=1, source_target_pairs={{0,2},{1,15},{2,4},{3,1},{4,6},{5,3},{6,8},{7,5},{8,10},{9,7},{10,... | collective-permute-start | bytes 1572872 | tf_op jit(solution)/shard_map/ppermute | solution.py:318
  106.3 12.4 %collective-permute-start.11 = (bf16[272,512]{1,0:T(8,128)(2,1)S(1)}, bf16[272,512]{1,0:T(8,128)(2,1)S(1)}, u32[]{:S(2)}, u32[]{:S(2)}) collective-permute-start(bf16[272,512]{1,0:T(8,128)(2,1)S(1)} %slice.17), channel_id=1, source_target_pairs={{0,1},{1,0},{2,3},{3,2},{4,5},{5,4},{6,7},{7,6},{8,9},{9,8},{10,11... | collective-permute-start | bytes 835592 | tf_op jit(solution)/shard_map/ppermute | solution.py:321
  112.0 6.7 %collective-permute-start.12 = (bf16[256,512]{1,0:T(8,128)(2,1)S(1)}, bf16[256,512]{1,0:T(8,128)(2,1)S(1)}, u32[]{:S(2)}, u32[]{:S(2)}) collective-permute-start(bf16[256,512]{1,0:T(8,128)(2,1)S(1)} %slice.18), channel_id=1, source_target_pairs={{0,1},{1,0},{2,3},{3,2},{4,5},{5,4},{6,7},{7,6},{8,9},{9,8},{10,11... | collective-permute-start | bytes 786440 | tf_op jit(solution)/shard_map/ppermute | solution.py:322

commit v3 on v2

v3 whole, which is shorter than its diff:
```python
import functools

import jax
import jax.numpy as jnp
from jax import lax
from jax.experimental import pallas as pl
from jax.experimental.pallas import tpu as pltpu
from jax.sharding import Mesh
from jax.sharding import PartitionSpec as P

D = 4096
LANES = 128
STRIPE = 16
EPS = 1e-05
F32 = jnp.float32
BF16 = jnp.bfloat16
PARAMS = pltpu.CompilerParams(vmem_limit_bytes=32 * 2**20)


def vmem(n):
    return [pl.BlockSpec(memory_space=pltpu.VMEM)] * n


def in_hbm(x):
    return pltpu.with_memory_space_constraint(x, pltpu.HBM)


def one_hot(mask):
    return mask.astype(F32).astype(BF16)


def dot(a, b):
    return jnp.dot(a, b, preferred_element_type=F32)


def three_parts(x):
    hi = x.astype(BF16).astype(F32)
    rest = x - hi
    mid = rest.astype(BF16).astype(F32)
    low = (rest - mid).astype(BF16).astype(F32)
    return [hi, mid, low]


def source_kernel(capacity, group_ref, dest_ref, feats_ref, proj_ref, out_ref, acc_ref):
    step = pl.program_id(0)
    lines = feats_ref.shape[0] // LANES

    @pl.when(step == 0)
    def _():
        acc_ref[...] = jnp.zeros_like(acc_ref)

    acc_ref[...] += dot(feats_ref[...], proj_ref[...])

    @pl.when(step == pl.num_programs(0) - 1)
    def _():
        first = lax.rem(group_ref[0] * lines, dest_ref.shape[0])
        lane = lax.broadcasted_iota(jnp.int32, (1, LANES), 1)
        slot = lax.broadcasted_iota(jnp.int32, (out_ref.shape[0], LANES), 0)
        total = None
        for i in range(lines):
            target = dest_ref[pl.ds(first + i, 1), :] * capacity + lax.rem(lane, capacity)
            rows = acc_ref[i * LANES : (i + 1) * LANES, :].astype(BF16)
            term = dot(one_hot(slot == target), rows)
            total = term if total is None else total + term
        out_ref[...] = total.astype(BF16)


def source(group, dest, feats, proj, slots, capacity):
    tokens, width = feats.shape
    cols = proj.shape[1]
    lines = tokens // LANES
    chunk = 384 if width % 384 == 0 else width
    return pl.pallas_call(
        functools.partial(source_kernel, capacity),
        out_shape=jax.ShapeDtypeStruct((slots, cols), BF16),
        grid_spec=pltpu.PrefetchScalarGridSpec(
            num_scalar_prefetch=1,
            grid=(width // chunk,),
            in_specs=[
                pl.BlockSpec((8, LANES), lambda i, group: (group[0] * lines // 8, 0)),
                pl.BlockSpec((tokens, chunk), lambda i, group: (0, i)),
                pl.BlockSpec((chunk, cols), lambda i, group: (i, 0)),
            ],
            out_specs=pl.BlockSpec((slots, cols), lambda i, group: (0, 0)),
            scratch_shapes=[pltpu.VMEM((tokens, cols), F32)],
        ),
        compiler_params=PARAMS,
        name="source",
    )(group, in_hbm(dest), in_hbm(feats), in_hbm(proj))


def slots_kernel(capacity, lines, group_ref, dest_ref, layout_ref, out_ref):
    slots = out_ref.shape[1]
    hits = one_hot(dest_ref[...] == group_ref[0])
    ones = jnp.ones((8, LANES), BF16)
    counts = lax.dot_general(
        ones, hits, (((1,), (1,)), ((), ())), preferred_element_type=F32
    ).astype(BF16)
    shape = (dest_ref.shape[0], slots)
    sender = lax.div(lax.broadcasted_iota(jnp.int32, shape, 0), lines)
    slot = lax.div(lax.broadcasted_iota(jnp.int32, shape, 1), capacity)
    before = dot(counts, one_hot(sender < slot)).astype(jnp.int32)
    sends = dot(counts, one_hot(sender == slot))
    token = lax.rem(lax.broadcasted_iota(jnp.int32, (1, slots), 1), capacity)
    rank = lax.broadcasted_iota(jnp.int32, (slots, slots), 0)
    chosen = one_hot(rank == before[0:1, :] + token)
    order = layout_ref[...]
    high = lax.div(order, 64)
    both = jnp.concatenate(
        [high.astype(F32), (order - high * 64).astype(F32), jnp.zeros((6, slots), F32)], axis=0
    )
    found = dot(both.astype(BF16), chosen).astype(jnp.int32)
    place = found[0:1, :] * 64 + found[1:2, :]
    place = jnp.where(sends[0:1, :] > 0.5, place, -1)
    out_ref[...] = jnp.broadcast_to(place, out_ref.shape)


def slot_positions(group, dest, layout, slots, capacity, lines):
    return pl.pallas_call(
        functools.partial(slots_kernel, capacity, lines),
        out_shape=jax.ShapeDtypeStruct((8, slots), jnp.int32),
        grid_spec=pltpu.PrefetchScalarGridSpec(
            num_scalar_prefetch=1,
            grid=(1,),
            in_specs=[
                pl.BlockSpec(dest.shape, lambda i, group: (0, 0)),
                pl.BlockSpec((1, slots), lambda i, group: (0, 0)),
            ],
            out_specs=pl.BlockSpec((8, slots), lambda i, group: (0, 0)),
        ),
        compiler_params=PARAMS,
        cost_estimate=pl.CostEstimate(flops=1, bytes_accessed=1, transcendentals=0),
        name="slots",
    )(group, dest, layout)


def lane_sums(x):
    square = x * x
    hi = square.astype(BF16)
    low = (square - hi.astype(F32)).astype(BF16)
    ones = jnp.ones((8, x.shape[1]), BF16)
    dims = (((1,), (1,)), ((), ()))
    total = lax.dot_general(ones, hi, dims, preferred_element_type=F32)
    return total + lax.dot_general(ones, low, dims, preferred_element_type=F32)


def text_kernel(order_ref, own_ref, other_ref, w_own_ref, w_other_ref, out_ref, squares_ref):
    own = own_ref[0]
    other = other_ref[0]
    total = dot(own, w_own_ref[...]) + dot(other, w_other_ref[...])
    out_ref[0] = total.astype(BF16)
    squares_ref[0] = lane_sums(own.astype(F32)) + lane_sums(other.astype(F32))


def text_products(order, own, other, w_own, w_other):
    _, rows, feats = own.shape
    count = order.shape[0]
    cols = w_own.shape[1]
    block = pl.BlockSpec((1, rows, feats), lambda i, order: (order[i], 0, 0))
    whole = pl.BlockSpec(w_own.shape, lambda i, order: (0, 0))
    return pl.pallas_call(
        text_kernel,
        out_shape=(
            pltpu.HBM((count, rows, cols), BF16),
            jax.ShapeDtypeStruct((count, 8, rows), F32),
        ),
        grid_spec=pltpu.PrefetchScalarGridSpec(
            num_scalar_prefetch=1,
            grid=(count,),
            in_specs=[block, block, whole, whole],
            out_specs=(
                pl.BlockSpec((1, rows, cols), lambda i, order: (i, 0, 0)),
                pl.BlockSpec((1, 8, rows), lambda i, order: (i, 0, 0)),
            ),
        ),
        compiler_params=PARAMS,
        cost_estimate=pl.CostEstimate(flops=1, bytes_accessed=1, transcendentals=0),
        name="text",
    )(order, in_hbm(own), other, w_own, w_other)


def merged(block, slots_ref, visual, visual_squares, text, text_squares):
    rows = text.shape[0]
    position = lax.broadcasted_iota(jnp.int32, (rows, slots_ref.shape[1]), 0) + block * rows
    hit = (position == slots_ref[0:1, :]).astype(F32)
    is_visual = jnp.sum(hit, axis=1, keepdims=True) > 0.5
    hit = hit.astype(BF16)
    out = jnp.where(is_visual, dot(hit, visual), text.astype(F32))
    parts = jnp.concatenate(
        three_parts(visual_squares) + [jnp.ones((1, hit.shape[1]), F32)]
        + [jnp.zeros((4, hit.shape[1]), F32)],
        axis=0,
    )
    found = lax.dot_general(
        parts.astype(BF16), hit, (((1,), (1,)), ((), ())), preferred_element_type=F32
    )
    squares = jnp.where(found[3:4, :] > 0.5, stripe_sum(found), text_squares)
    return out.astype(BF16), squares


def visual_kernel(
    order_ref, v_own_ref, v_other_ref, w_own_ref, w_other_ref, slots_ref, text_ref, squares_ref,
    visual_ref, vis_squares_ref, key_ref, value_ref,
):
    own = v_own_ref[...]
    other = v_other_ref[...]
    visual = (dot(own, w_own_ref[...]) + dot(other, w_other_ref[...])).astype(BF16)
    visual_ref[...] = visual
    vis_squares = lane_sums(own.astype(F32)) + lane_sums(other.astype(F32))
    vis_squares_ref[...] = vis_squares
    out, squares = merged(
        order_ref[0], slots_ref, visual, vis_squares[0:1, :], text_ref[0], squares_ref[0, 0:1, :]
    )
    rows = out.shape[0]
    cols = key_ref.shape[1]
    key_ref[:rows, :] = out[:, :cols]
    value_ref[...] = out[:, cols:]
    wide = jnp.concatenate([squares, jnp.zeros((1, cols - rows), F32)], axis=1)
    key_ref[rows:, :] = stripe_of(wide)


def visual_products(order, v_own, v_other, w_own, w_other, slots, text, squares):
    _, rows, cols2 = text.shape
    cols = cols2 // 2
    count = v_own.shape[0]
    whole = lambda a: pl.BlockSpec(a.shape, lambda i, order: (0,) * a.ndim)
    shapes = [((count, cols2), BF16), ((8, count), F32), ((rows + STRIPE, cols), BF16), ((rows, cols), BF16)]
    return pl.pallas_call(
        visual_kernel,
        out_shape=tuple(jax.ShapeDtypeStruct(*s) for s in shapes),
        grid_spec=pltpu.PrefetchScalarGridSpec(
            num_scalar_prefetch=1,
            grid=(1,),
            in_specs=[
                whole(v_own),
                whole(v_other),
                whole(w_own),
                whole(w_other),
                whole(slots),
                pl.BlockSpec((1, rows, cols2), lambda i, order: (0, 0, 0)),
                pl.BlockSpec((1, 8, rows), lambda i, order: (0, 0, 0)),
            ],
            out_specs=tuple(pl.BlockSpec(s[0], lambda i, order: (0, 0)) for s in shapes),
        ),
        compiler_params=PARAMS,
        name="visual",
    )(order, v_own, v_other, w_own, w_other, slots, text, squares)


def merge_kernel(
    order_ref, slots_ref, visual_ref, vis_squares_ref, text_ref, squares_ref, out_ref, sums_ref
):
    out, squares = merged(
        order_ref[pl.program_id(0) + 1], slots_ref, visual_ref[...], vis_squares_ref[0:1, :],
        text_ref[0], squares_ref[0, 0:1, :],
    )
    out_ref[0] = out
    sums_ref[0] = jnp.broadcast_to(squares, sums_ref.shape[1:])


def merge(order, slots, visual, vis_squares, text, squares):
    count = text.shape[0] - 1
    _, rows, cols = text.shape
    whole = lambda a: pl.BlockSpec(a.shape, lambda i, order: (0,) * a.ndim)
    later = lambda a: pl.BlockSpec((1,) + a.shape[1:], lambda i, order: (i + 1, 0, 0))
    same = lambda a: pl.BlockSpec((1,) + a.shape[1:], lambda i, order: (i, 0, 0))
    return pl.pallas_call(
        merge_kernel,
        out_shape=(
            jax.ShapeDtypeStruct((count, rows, cols), BF16),
            jax.ShapeDtypeStruct((count, 8, rows), F32),
        ),
        grid_spec=pltpu.PrefetchScalarGridSpec(
            num_scalar_prefetch=1,
            grid=(count,),
            in_specs=[whole(slots), whole(visual), whole(vis_squares), later(text), later(squares)],
            out_specs=(same(text), same(squares)),
        ),
        compiler_params=PARAMS,
        cost_estimate=pl.CostEstimate(
            flops=count * 2 * rows * slots.shape[1] * cols,
            bytes_accessed=count * rows * cols * 4,
            transcendentals=0,
        ),
        name="merge",
    )(order, slots, visual, vis_squares, text, squares)


def stripe_of(squares):
    parts = three_parts(squares)
    pad = jnp.zeros((STRIPE - 3, squares.shape[1]), F32)
    stripe = jnp.concatenate(parts + [pad], axis=0)
    return stripe.astype(BF16)


def stripe_sum(stripe):
    return stripe[0:1] + stripe[1:2] + stripe[2:3]


def hop_kernel(part, came_rows, last, product_ref, squares_ref, came_ref, *out_refs):
    rows = product_ref.shape[1]
    cols = product_ref.shape[2]
    squares = []
    for i in range(2):
        ref = out_refs[i] if last else out_refs[0]
        to = slice(0, rows) if last else slice(i * rows, (i + 1) * rows)
        if i * rows < came_rows:
            came = came_ref[i * rows : (i + 1) * rows, :].astype(F32)
            ref[to, :] = (product_ref[i].astype(F32) + came).astype(BF16)
        else:
            ref[to, :] = product_ref[i]
        squares.append(squares_ref[i, 0:1, :])
    if part == 0:
        sums = jnp.concatenate(squares, axis=1) + stripe_sum(came_ref[came_rows:, :].astype(F32))
        if last:
            pad = jnp.zeros((1, cols - rows), F32)
            for i in range(2):
                wide = jnp.concatenate([sums[:, i * rows : (i + 1) * rows], pad], axis=1)
                out_refs[i][rows:, :] = stripe_of(wide)
        else:
            out_refs[0][2 * rows :, :] = stripe_of(sums)


def hop(part, at, last, product, squares, came):
    rows = product.shape[1]
    cols = product.shape[2] // 2
    extra = STRIPE if part == 0 else 0
    came_rows = came.shape[0] - extra
    shapes = [(rows + extra, cols)] * 2 if last else [(2 * rows + extra, cols)]
    return pl.pallas_call(
        functools.partial(hop_kernel, part, came_rows, last),
        out_shape=tuple(jax.ShapeDtypeStruct(s, BF16) for s in shapes),
        grid=(1,),
        in_specs=[
            pl.BlockSpec(
                (pl.Element(2), pl.Element(rows), pl.Element(cols)), lambda i: (at, 0, part * cols)
            ),
            pl.BlockSpec((pl.Element(2), pl.Element(8), pl.Element(rows)), lambda i: (at, 0, 0)),
            pl.BlockSpec(came.shape, lambda i: (0, 0)),
        ],
        out_specs=tuple(pl.BlockSpec(s, lambda i: (0, 0)) for s in shapes),
        compiler_params=PARAMS,
        name="hop",
    )(product, squares, came)


def finish_kernel(product_ref, squares_ref, k_ref, v_ref, k2_ref, v2_ref, key_ref, value_ref):
    rows = product_ref.shape[1]
    cols = key_ref.shape[1]
    squares = squares_ref[0, 0:1, :]
    squares += stripe_sum(k_ref[rows:, :].astype(F32))[:, :rows]
    squares += stripe_sum(k2_ref[rows:, :].astype(F32))[:, :rows]
    inverse = lax.rsqrt(squares / D + EPS)
    for i in range(rows // LANES):
        to = slice(i * LANES, (i + 1) * LANES)
        scale = jnp.broadcast_to(inverse[:, to], (LANES, LANES)).T
        for out_ref, a_ref, b_ref, at in (
            (key_ref, k_ref, k2_ref, 0),
            (value_ref, v_ref, v2_ref, cols),
        ):
            for j in range(cols // LANES):
                lane = slice(j * LANES, (j + 1) * LANES)
                own = product_ref[0, to, at + j * LANES : at + (j + 1) * LANES].astype(F32)
                total = own + a_ref[to, lane].astype(F32) + b_ref[to, lane].astype(F32)
                out_ref[to, lane] = (total * scale).astype(BF16)


def finish(product, squares, k, v, k2, v2, cols):
    rows = product.shape[1]
    whole = lambda a: pl.BlockSpec(a.shape, lambda i: (0,) * a.ndim)
    last = product.shape[0] - 1
    return pl.pallas_call(
        finish_kernel,
        out_shape=(jax.ShapeDtypeStruct((rows, cols), BF16),) * 2,
        grid=(1,),
        in_specs=[
            pl.BlockSpec((1,) + product.shape[1:], lambda i: (last, 0, 0)),
            pl.BlockSpec((1,) + squares.shape[1:], lambda i: (last, 0, 0)),
        ]
        + [whole(a) for a in (k, v, k2, v2)],
        out_specs=(pl.BlockSpec((rows, cols), lambda i: (0, 0)),) * 2,
        compiler_params=PARAMS,
        name="finish",
    )(product, squares, k, v, k2, v2)


def local(vis_feats, proj_w, text_embed, dest_group, layout, norm_gain, key_w, value_w):
    n_grp = lax.axis_size("grp")
    n_y = lax.axis_size("y")
    h = lax.axis_index("grp")
    y = lax.axis_index("y")
    c = lax.axis_index("core")
    seq_len, feats = text_embed.shape
    rows = seq_len // (2 * n_y)
    tokens = vis_feats.shape[0]
    run_count = n_grp // 2
    capacity = tokens // run_count
    slot_count = n_grp * capacity
    cols = key_w.shape[1]
    swap = [(0, 1), (1, 0)]
    ring = []
    cross = []
    for i in range(n_y):
        above = 2 * ((i + 1) % n_y)
        below = 2 * ((i - 1) % n_y)
        ring += [(2 * i, above), (2 * i + 1, below + 1)]
        cross += [(2 * i, above + 1), (2 * i + 1, below)]

    group = jnp.full((1,), h, jnp.int32)
    dest = dest_group.reshape(-1, LANES)
    outgoing = source(group, dest, vis_feats, proj_w, slot_count, capacity)
    arrived = lax.all_to_all(
        outgoing.reshape(n_grp, capacity, feats), "grp", 0, 0, tiled=True
    ).reshape(slot_count, feats)

    weight = jnp.concatenate([key_w, value_w], axis=1).astype(F32) * norm_gain[:, None]
    weight = weight.astype(BF16)
    blocks = text_embed.reshape(2 * n_y, rows, feats)
    other = lax.ppermute(blocks, "core", swap)
    w_other = lax.ppermute(weight, "core", swap)

    far = n_y // 2
    offset = [far] + [o for o in range(far - 1, 0, -1) for _ in (0, 1)] + [0]
    second = [0] + [0, 1] * (far - 1) + [0]
    offset = jnp.asarray(offset, jnp.int32)
    second = jnp.asarray(second, jnp.int32)
    up = 2 * ((y + offset) % n_y) + second
    down = 2 * ((y - offset + n_y) % n_y) + 1 - second
    mine = jnp.where(c == 0, up, down)
    slots = slot_positions(group, dest, layout, slot_count, capacity, tokens // LANES)
    text, text_squares = text_products(mine, blocks, other, weight, w_other)
    text = in_hbm(text)

    arrived, text_squares, slots = lax.optimization_barrier((arrived, text_squares, slots))
    arrived_other = lax.ppermute(arrived, "core", swap)
    visual, visual_squares, key_leaf, value_leaf = visual_products(
        mine, arrived, arrived_other, weight, w_other, slots, text, text_squares
    )
    flat = ("y", "core")
    streams = [lax.ppermute(key_leaf, flat, ring), lax.ppermute(value_leaf, flat, ring)]
    product, squares = merge(mine, slots, visual, visual_squares, text, text_squares)
    ends = []
    for step in range(far - 1):
        last = step == far - 2
        for part in range(2):
            sent = hop(part, 2 * step, last, product, squares, streams[part])
            streams[part] = lax.ppermute(sent[0], flat, ring)
            if last:
                ends.append(lax.ppermute(sent[1], flat, cross))
    return finish(product, squares, streams[0], streams[1], ends[0], ends[1], cols)


def solution(mesh):
    n_grp, n_sp = mesh.devices.shape
    split = Mesh(mesh.devices.reshape(n_grp, n_sp // 2, 2), ("grp", "y", "core"))
    sp = ("y", "core")
    return jax.shard_map(
        local,
        mesh=split,
        in_specs=(
            P("grp", None),
            P(None, sp),
            P("grp", sp),
            P(),
            P("grp", None),
            P(sp),
            P(sp, None),
            P(sp, None),
        ),
        out_specs=(P(("grp", "y", "core"), None), P(("grp", "y", "core"), None)),
        check_vma=False,
    )
```

time: 121 us -> 116 us (0.959)
  starting transfers between devices: 73.3 us -> 67.7 us
  Pallas kernels: 18.4 us -> 23.5 us
  local copies, waits for them, and re-layouts: 6.26 us -> 1.55 us
  waiting for transfers between devices: 15.3 us -> 19.9 us
  other arithmetic: 5.54 us -> 1.91 us
    all_to_all x1, starting transfers between devices: 22.8 us -> 9.3 us  [local(): lax.all_to_all(outgoing.reshape(n_grp, capacity, feats), 'grp', 0, 0, til...]
    ppermute x11, starting transfers between devices: 43.8 us -> 52.5 us  [the longest x6 19.6 us: local(): streams[part] = lax.ppermute(sent[0], flat, ring)]
    pallas_call x12 -> x11, Pallas kernels: 17.4 us -> 22.4 us  [the longest x1 8.24 us: text_products(): pl.pallas_call(text_kernel, out_shape=(pltpu.HBM((count, rows, cols), BF1...]
    all_to_all x1, waiting for transfers between devices: 2.23 us -> 5.69 us  [local(): lax.all_to_all(outgoing.reshape(n_grp, capacity, feats), 'grp', 0, 0, til...]
    reduce_or x1 -> x0, other arithmetic: 2.47 us -> none  [local(): senders = jnp.any(run_heads == h, axis=1)]
    unnamed x16 -> x4, local copies, waits for them, and re-layouts: 3.73 us -> 1.55 us
    reshape x1 -> x0, local copies, waits for them, and re-layouts: 1.55 us -> none  [local(): run_heads = dest_group.reshape(n_grp, run_count, capacity)[:, :, 0]]
    reduce_sum x2 -> x0, other arithmetic: 1.27 us -> none  [the longest x1 1.16 us: local(): jnp.sum(jnp.where((earlier[:, None] == group[None, :])[:, :, None], first...]
  transfers between devices with their start and end apart: 14 -> 14, of which waited for: 8 -> 7; matrix products, arithmetic and copies ran while one was open for 6% -> 2% of each run, Pallas kernels for 11% -> 17%
where the time goes in v3:
time: 116 us; the launch traced here: 115 us
  starting transfers between devices  67.7 us (58%)
  Pallas kernels  23.5 us (20%)
  waiting for transfers between devices  19.9 us (17%)
  other arithmetic  1.91 us (2%)
  local copies, waits for them, and re-layouts  1.55 us (1%)
    ppermute x6, starting transfers between devices, local(): streams[part] = lax.ppermute(sent[0], flat, ring)  19.6 us
    ppermute x1, starting transfers between devices, local(): other = lax.ppermute(blocks, 'core', swap)  16.1 us
    ppermute x6, waiting for transfers between devices, local(): streams[part] = lax.ppermute(sent[0], flat, ring)  9.63 us
    all_to_all x1, starting transfers between devices, local(): lax.all_to_all(outgoing.reshape(n_grp, capacity, feats), 'grp', 0, 0, til...  9.3 us
    ppermute x2, starting transfers between devices, local(): ends.append(lax.ppermute(sent[1], flat, cross))  8.76 us
    pallas_call x1, Pallas kernels, text_products(): pl.pallas_call(text_kernel, out_shape=(pltpu.HBM((count, rows, cols), BF1...  8.24 us
    pallas_call x1, Pallas kernels, merge(): pl.pallas_call(merge_kernel, out_shape=(jax.ShapeDtypeStruct((count, rows...  6.65 us
    all_to_all x1, waiting for transfers between devices, local(): lax.all_to_all(outgoing.reshape(n_grp, capacity, feats), 'grp', 0, 0, til...  5.69 us
  transfers between devices with their start and end apart: 14, of which 7 were waited for; matrix products, arithmetic and copies ran while one was open for 2% of the time, Pallas kernels for 17%

profile of v3, /device:TPU:1, one launch (start us, length us, event | category | flops | bytes accessed | tf_op | source)
XLA Modules:
  0.0 115.4 jit_solution(5877356620162675542)
XLA Ops:
  0.6 16.1 %collective-permute-start = (bf16[16,256,256]{2,1,0:T(8,128)(2,1)}, bf16[16,256,256]{2,1,0:T(8,128)(2,1)S(1)}, u32[]{:S(2)}, u32[]{:S(2)}) collective-permute-start(bf16[16,256,256]{2,1,0:T(8,128)(2,1)} %bitcast.9), channel_id=1, source_target_pairs={{0,1},{1,0},{2,3},{3,2},{4,5},{5,4},{6,7},{7,6},{8,9},{9,8},{10,11... | collective-permute-start | bytes 6291464 | tf_op jit(solution)/shard_map/ppermute | solution.py:419
  16.7 3.5 %source.1 = bf16[512,256]{1,0:T(8,128)(2,1)} custom-call(s32[1]{0:T(128)} %bitcast.group_ref, s32[128,128]{1,0:T(8,128)} %bitcast.7, bf16[256,1152]{1,0:T(8,128)(2,1)} %feats_ref.1, bf16[1152,256]{1,0:T(8,128)(2,1)} %proj_ref.1), custom_call_target="tpu_custom_call" | custom-call | tf_op jit(solution)/shard_map/source/pallas_call | solution.py:73
  20.2 9.3 %all-to-all-start = ((bf16[64,8,256]{2,1,0:T(8,128)(2,1)}), bf16[64,8,256]{2,1,0:T(8,128)(2,1)S(1)}, u32[]{:S(2)}, u32[]{:S(2)}) async-start(bf16[64,8,256]{2,1,0:T(8,128)(2,1)} %bitcast.2), calls=%async_computation | async-start | bytes 524288 | tf_op jit(solution)/shard_map/all_to_all | solution.py:412
  29.6 1.2 %multiply_convert_fusion.w_own_ref = bf16[256,1024]{1,0:T(8,128)(2,1)S(1)} fusion(bf16[256,512]{1,0:T(8,128)(2,1)} %param.17, bf16[256,512]{1,0:T(8,128)(2,1)} %param.16, f32[256]{0:T(256)} %param.15), kind=kLoop, calls=%fused_computation | loop fusion | flops 1572864 | bytes 1049600 | tf_op jit(solution)/shard_map/convert_element_type | solution.py:417
  30.7 2.2 %collective-permute-start.1 = (bf16[256,1024]{1,0:T(8,128)(2,1)S(1)}, bf16[256,1024]{1,0:T(8,128)(2,1)S(1)}, u32[]{:S(2)}, u32[]{:S(2)}) collective-permute-start(bf16[256,1024]{1,0:T(8,128)(2,1)S(1)} %multiply_convert_fusion.w_own_ref), channel_id=1, source_target_pairs={{0,1},{1,0},{2,3},{3,2},{4,5},{5,4},{6,7},{7,6},{8,9},{9,8},{10,11... | collective-permute-start | bytes 1572872 | tf_op jit(solution)/shard_map/ppermute | solution.py:420
  33.0 0.8 copy-done
  33.8 0.7 copy-done.1
  34.5 0.5 slots.1.slots_ref
  35.0 0.7 broadcast_select_fusion.order_ref
  35.7 8.2 %text.1 = (bf16[8,256,1024]{2,1,0:T(8,128)(2,1)}, f32[8,8,256]{2,1,0:T(8,128)S(1)}) custom-call(s32[8]{0:T(128)S(1)} %broadcast_select_fusion.order_ref, bf16[16,256,256]{2,1,0:T(8,128)(2,1)} %bitcast.10, bf16[16,256,256]{2,1,0:T(8,128)(2,1)S(1)} %collective-permute-done.other_ref, bf16[256,1024]{1,0:T(8,128)(2,1)S(1)} %multiply_convert_fusion.w_own_ref, ...), custom_call_target="tpu_custom_call" | custom-call | flops 1 | bytes 1 | tf_op jit(solution)/shard_map/text/pallas_call | solution.py:161
  44.0 5.7 %all-to-all-done = bf16[64,8,256]{2,1,0:T(8,128)(2,1)S(1)} async-done(((bf16[64,8,256]{2,1,0:T(8,128)(2,1)}), bf16[64,8,256]{2,1,0:T(8,128)(2,1)S(1)}, u32[]{:S(2)}, u32[]{:S(2)}) %all-to-all-start) | async-done | bytes 262176 | tf_op jit(solution)/shard_map/all_to_all | solution.py:412
  49.7 3.7 %collective-permute-start.2 = (bf16[512,256]{1,0:T(8,128)(2,1)S(1)}, bf16[512,256]{1,0:T(8,128)(2,1)S(1)}, u32[]{:S(2)}, u32[]{:S(2)}) collective-permute-start(bf16[512,256]{1,0:T(8,128)(2,1)S(1)} %bitcast.5), channel_id=1, source_target_pairs={{0,1},{1,0},{2,3},{3,2},{4,5},{5,4},{6,7},{7,6},{8,9},{9,8},{10,11... | collective-permute-start | bytes 786440 | tf_op jit(solution)/shard_map/ppermute | solution.py:435
  53.4 1.1 collective-permute-done.2.v_other_ref
  54.5 2.8 %visual.1 = (bf16[512,1024]{1,0:T(8,128)(2,1)S(1)}, f32[8,512]{1,0:T(8,128)S(1)}, bf16[272,512]{1,0:T(8,128)(2,1)S(1)}, bf16[256,512]{1,0:T(8,128)(2,1)S(1)}) custom-call(s32[8]{0:T(128)S(1)} %broadcast_select_fusion.order_ref, bf16[512,256]{1,0:T(8,128)(2,1)S(1)} %bitcast.6, bf16[512,256]{1,0:T(8,128)(2,1)S(1)} %collective-permute-done.2.v_other_ref, ...), custom_call_target="tpu_custom_call" | custom-call | tf_op jit(solution)/shard_map/visual/pallas_call | solution.py:228
  57.4 5.1 %collective-permute-start.3 = (bf16[272,512]{1,0:T(8,128)(2,1)S(1)}, bf16[272,512]{1,0:T(8,128)(2,1)S(1)}, u32[]{:S(2)}, u32[]{:S(2)}) collective-permute-start(bf16[272,512]{1,0:T(8,128)(2,1)S(1)} %get-tuple-element.26), channel_id=1, source_target_pairs={{0,2},{1,15},{2,4},{3,1},{4,6},{5,3},{6,8},{7,5},{8,10},{9,7},{10,... | collective-permute-start | bytes 835592 | tf_op jit(solution)/shard_map/ppermute | solution.py:440
  62.5 3.0 %collective-permute-start.7 = (bf16[256,512]{1,0:T(8,128)(2,1)S(1)}, bf16[256,512]{1,0:T(8,128)(2,1)S(1)}, u32[]{:S(2)}, u32[]{:S(2)}) collective-permute-start(bf16[256,512]{1,0:T(8,128)(2,1)S(1)} %get-tuple-element.28), channel_id=1, source_target_pairs={{0,2},{1,15},{2,4},{3,1},{4,6},{5,3},{6,8},{7,5},{8,10},{9,7},{10,... | collective-permute-start | bytes 786440 | tf_op jit(solution)/shard_map/ppermute | solution.py:440
  65.5 6.6 %merge.1 = (bf16[7,256,1024]{2,1,0:T(8,128)(2,1)S(1)}, f32[7,8,256]{2,1,0:T(8,128)S(1)}) custom-call(s32[8]{0:T(128)S(1)} %broadcast_select_fusion.order_ref, s32[8,512]{1,0:T(8,128)S(1)} %slots.1.slots_ref, bf16[512,1024]{1,0:T(8,128)(2,1)S(1)} %get-tuple-element.22.visual_ref, f32[8,512]{1,0:T(8,128)S(1)} %get-tuple-element.23.vis_squares_ref, ...), custom_call_target="tpu_custom_call" | custom-call | flops 1879048192 | bytes 7340032 | tf_op jit(solution)/shard_map/merge/pallas_call | solution.py:267
  72.2 3.0 %collective-permute-start.4 = (bf16[528,512]{1,0:T(8,128)(2,1)S(1)}, bf16[528,512]{1,0:T(8,128)(2,1)S(1)}, u32[]{:S(2)}, u32[]{:S(2)}) collective-permute-start(bf16[528,512]{1,0:T(8,128)(2,1)S(1)} %hop.6), channel_id=1, source_target_pairs={{0,2},{1,15},{2,4},{3,1},{4,6},{5,3},{6,8},{7,5},{8,10},{9,7},{10,... | collective-permute-start | bytes 1622024 | tf_op jit(solution)/shard_map/ppermute | solution.py:447
  75.3 3.0 %collective-permute-start.8 = (bf16[512,512]{1,0:T(8,128)(2,1)S(1)}, bf16[512,512]{1,0:T(8,128)(2,1)S(1)}, u32[]{:S(2)}, u32[]{:S(2)}) collective-permute-start(bf16[512,512]{1,0:T(8,128)(2,1)S(1)} %hop.9), channel_id=1, source_target_pairs={{0,2},{1,15},{2,4},{3,1},{4,6},{5,3},{6,8},{7,5},{8,10},{9,7},{10,... | collective-permute-start | bytes 1572872 | tf_op jit(solution)/shard_map/ppermute | solution.py:447
  78.3 4.3 %collective-permute-done.4.came_ref = bf16[528,512]{1,0:T(8,128)(2,1)S(1)} collective-permute-done((bf16[528,512]{1,0:T(8,128)(2,1)S(1)}, bf16[528,512]{1,0:T(8,128)(2,1)S(1)}, u32[]{:S(2)}, u32[]{:S(2)}) %collective-permute-start.4) | collective-permute-done | bytes 540704 | tf_op jit(solution)/shard_map/ppermute | solution.py:447
  82.6 0.1 hop.7
  82.8 3.9 %collective-permute-start.5 = (bf16[528,512]{1,0:T(8,128)(2,1)S(1)}, bf16[528,512]{1,0:T(8,128)(2,1)S(1)}, u32[]{:S(2)}, u32[]{:S(2)}) collective-permute-start(bf16[528,512]{1,0:T(8,128)(2,1)S(1)} %hop.7), channel_id=1, source_target_pairs={{0,2},{1,15},{2,4},{3,1},{4,6},{5,3},{6,8},{7,5},{8,10},{9,7},{10,... | collective-permute-start | bytes 1622024 | tf_op jit(solution)/shard_map/ppermute | solution.py:447
  86.7 1.6 %collective-permute-done.8.came_ref = bf16[512,512]{1,0:T(8,128)(2,1)S(1)} collective-permute-done((bf16[512,512]{1,0:T(8,128)(2,1)S(1)}, bf16[512,512]{1,0:T(8,128)(2,1)S(1)}, u32[]{:S(2)}, u32[]{:S(2)}) %collective-permute-start.8) | collective-permute-done | bytes 524320 | tf_op jit(solution)/shard_map/ppermute | solution.py:447
  88.4 3.9 %collective-permute-start.9 = (bf16[512,512]{1,0:T(8,128)(2,1)S(1)}, bf16[512,512]{1,0:T(8,128)(2,1)S(1)}, u32[]{:S(2)}, u32[]{:S(2)}) collective-permute-start(bf16[512,512]{1,0:T(8,128)(2,1)S(1)} %hop.10), channel_id=1, source_target_pairs={{0,2},{1,15},{2,4},{3,1},{4,6},{5,3},{6,8},{7,5},{8,10},{9,7},{10,... | collective-permute-start | bytes 1572872 | tf_op jit(solution)/shard_map/ppermute | solution.py:447
  92.3 1.8 %collective-permute-done.5.came_ref = bf16[528,512]{1,0:T(8,128)(2,1)S(1)} collective-permute-done((bf16[528,512]{1,0:T(8,128)(2,1)S(1)}, bf16[528,512]{1,0:T(8,128)(2,1)S(1)}, u32[]{:S(2)}, u32[]{:S(2)}) %collective-permute-start.5) | collective-permute-done | bytes 540704 | tf_op jit(solution)/shard_map/ppermute | solution.py:447
  94.2 3.9 %collective-permute-start.6 = (bf16[272,512]{1,0:T(8,128)(2,1)S(1)}, bf16[272,512]{1,0:T(8,128)(2,1)S(1)}, u32[]{:S(2)}, u32[]{:S(2)}) collective-permute-start(bf16[272,512]{1,0:T(8,128)(2,1)S(1)} %get-tuple-element.27), channel_id=1, source_target_pairs={{0,2},{1,15},{2,4},{3,1},{4,6},{5,3},{6,8},{7,5},{8,10},{9,7},{10,... | collective-permute-start | bytes 835592 | tf_op jit(solution)/shard_map/ppermute | solution.py:447
  98.1 5.2 %collective-permute-start.11 = (bf16[272,512]{1,0:T(8,128)(2,1)S(1)}, bf16[272,512]{1,0:T(8,128)(2,1)S(1)}, u32[]{:S(2)}, u32[]{:S(2)}) collective-permute-start(bf16[272,512]{1,0:T(8,128)(2,1)S(1)} %get-tuple-element.30), channel_id=1, source_target_pairs={{0,3},{1,14},{2,5},{3,0},{4,7},{5,2},{6,9},{7,4},{8,11},{9,6},{10,... | collective-permute-start | bytes 835592 | tf_op jit(solution)/shard_map/ppermute | solution.py:449
  103.5 1.9 %collective-permute-start.10 = (bf16[256,512]{1,0:T(8,128)(2,1)S(1)}, bf16[256,512]{1,0:T(8,128)(2,1)S(1)}, u32[]{:S(2)}, u32[]{:S(2)}) collective-permute-start(bf16[256,512]{1,0:T(8,128)(2,1)S(1)} %get-tuple-element.29), channel_id=1, source_target_pairs={{0,2},{1,15},{2,4},{3,1},{4,6},{5,3},{6,8},{7,5},{8,10},{9,7},{10,... | collective-permute-start | bytes 786440 | tf_op jit(solution)/shard_map/ppermute | solution.py:447
  105.4 3.5 %collective-permute-start.12 = (bf16[256,512]{1,0:T(8,128)(2,1)S(1)}, bf16[256,512]{1,0:T(8,128)(2,1)S(1)}, u32[]{:S(2)}, u32[]{:S(2)}) collective-permute-start(bf16[256,512]{1,0:T(8,128)(2,1)S(1)} %get-tuple-element.31), channel_id=1, source_target_pairs={{0,3},{1,14},{2,5},{3,0},{4,7},{5,2},{6,9},{7,4},{8,11},{9,6},{10,... | collective-permute-start | bytes 786440 | tf_op jit(solution)/shard_map/ppermute | solution.py:449
  109.0 2.0 %collective-permute-done.10.v_ref = bf16[256,512]{1,0:T(8,128)(2,1)S(1)} collective-permute-done((bf16[256,512]{1,0:T(8,128)(2,1)S(1)}, bf16[256,512]{1,0:T(8,128)(2,1)S(1)}, u32[]{:S(2)}, u32[]{:S(2)}) %collective-permute-start.10) | collective-permute-done | bytes 262176 | tf_op jit(solution)/shard_map/ppermute | solution.py:447
  110.9 3.4 %collective-permute-done.12.v2_ref = bf16[256,512]{1,0:T(8,128)(2,1)S(1)} collective-permute-done((bf16[256,512]{1,0:T(8,128)(2,1)S(1)}, bf16[256,512]{1,0:T(8,128)(2,1)S(1)}, u32[]{:S(2)}, u32[]{:S(2)}) %collective-permute-start.12) | collective-permute-done | bytes 262176 | tf_op jit(solution)/shard_map/ppermute | solution.py:449
  114.3 1.0 finish.1
  (14 shorter events, 0.6 us)
Async XLA Ops:
  0.6 35.1 %collective-permute-start = (bf16[16,256,256]{2,1,0:T(8,128)(2,1)}, bf16[16,256,256]{2,1,0:T(8,128)(2,1)S(1)}, u32[]{:S(2)}, u32[]{:S(2)}) collective-permute-start(bf16[16,256,256]{2,1,0:T(8,128)(2,1)} %bitcast.9), channel_id=1, source_target_pairs={{0,1},{1,0},{2,3},{3,2},{4,5},{5,4},{6,7},{7,6},{8,9},{9,8},{10,11... | collective-permute-start | bytes 6291464 | tf_op jit(solution)/shard_map/ppermute | solution.py:419
  20.2 29.4 %all-to-all-start = ((bf16[64,8,256]{2,1,0:T(8,128)(2,1)}), bf16[64,8,256]{2,1,0:T(8,128)(2,1)S(1)}, u32[]{:S(2)}, u32[]{:S(2)}) async-start(bf16[64,8,256]{2,1,0:T(8,128)(2,1)} %bitcast.2), calls=%async_computation | async-start | bytes 524288 | tf_op jit(solution)/shard_map/all_to_all | solution.py:412
  30.7 5.0 %collective-permute-start.1 = (bf16[256,1024]{1,0:T(8,128)(2,1)S(1)}, bf16[256,1024]{1,0:T(8,128)(2,1)S(1)}, u32[]{:S(2)}, u32[]{:S(2)}) collective-permute-start(bf16[256,1024]{1,0:T(8,128)(2,1)S(1)} %multiply_convert_fusion.w_own_ref), channel_id=1, source_target_pairs={{0,1},{1,0},{2,3},{3,2},{4,5},{5,4},{6,7},{7,6},{8,9},{9,8},{10,11... | collective-permute-start | bytes 1572872 | tf_op jit(solution)/shard_map/ppermute | solution.py:420
  33.0 0.8 copy-start
  33.8 0.7 copy-start.1
  49.7 4.8 %collective-permute-start.2 = (bf16[512,256]{1,0:T(8,128)(2,1)S(1)}, bf16[512,256]{1,0:T(8,128)(2,1)S(1)}, u32[]{:S(2)}, u32[]{:S(2)}) collective-permute-start(bf16[512,256]{1,0:T(8,128)(2,1)S(1)} %bitcast.5), channel_id=1, source_target_pairs={{0,1},{1,0},{2,3},{3,2},{4,5},{5,4},{6,7},{7,6},{8,9},{9,8},{10,11... | collective-permute-start | bytes 786440 | tf_op jit(solution)/shard_map/ppermute | solution.py:435
  57.4 14.8 %collective-permute-start.3 = (bf16[272,512]{1,0:T(8,128)(2,1)S(1)}, bf16[272,512]{1,0:T(8,128)(2,1)S(1)}, u32[]{:S(2)}, u32[]{:S(2)}) collective-permute-start(bf16[272,512]{1,0:T(8,128)(2,1)S(1)} %get-tuple-element.26), channel_id=1, source_target_pairs={{0,2},{1,15},{2,4},{3,1},{4,6},{5,3},{6,8},{7,5},{8,10},{9,7},{10,... | collective-permute-start | bytes 835592 | tf_op jit(solution)/shard_map/ppermute | solution.py:440
  62.5 12.7 %collective-permute-start.7 = (bf16[256,512]{1,0:T(8,128)(2,1)S(1)}, bf16[256,512]{1,0:T(8,128)(2,1)S(1)}, u32[]{:S(2)}, u32[]{:S(2)}) collective-permute-start(bf16[256,512]{1,0:T(8,128)(2,1)S(1)} %get-tuple-element.28), channel_id=1, source_target_pairs={{0,2},{1,15},{2,4},{3,1},{4,6},{5,3},{6,8},{7,5},{8,10},{9,7},{10,... | collective-permute-start | bytes 786440 | tf_op jit(solution)/shard_map/ppermute | solution.py:440
  72.2 10.4 %collective-permute-start.4 = (bf16[528,512]{1,0:T(8,128)(2,1)S(1)}, bf16[528,512]{1,0:T(8,128)(2,1)S(1)}, u32[]{:S(2)}, u32[]{:S(2)}) collective-permute-start(bf16[528,512]{1,0:T(8,128)(2,1)S(1)} %hop.6), channel_id=1, source_target_pairs={{0,2},{1,15},{2,4},{3,1},{4,6},{5,3},{6,8},{7,5},{8,10},{9,7},{10,... | collective-permute-start | bytes 1622024 | tf_op jit(solution)/shard_map/ppermute | solution.py:447
  75.3 12.9 %collective-permute-start.8 = (bf16[512,512]{1,0:T(8,128)(2,1)S(1)}, bf16[512,512]{1,0:T(8,128)(2,1)S(1)}, u32[]{:S(2)}, u32[]{:S(2)}) collective-permute-start(bf16[512,512]{1,0:T(8,128)(2,1)S(1)} %hop.9), channel_id=1, source_target_pairs={{0,2},{1,15},{2,4},{3,1},{4,6},{5,3},{6,8},{7,5},{8,10},{9,7},{10,... | collective-permute-start | bytes 1572872 | tf_op jit(solution)/shard_map/ppermute | solution.py:447
  82.8 11.3 %collective-permute-start.5 = (bf16[528,512]{1,0:T(8,128)(2,1)S(1)}, bf16[528,512]{1,0:T(8,128)(2,1)S(1)}, u32[]{:S(2)}, u32[]{:S(2)}) collective-permute-start(bf16[528,512]{1,0:T(8,128)(2,1)S(1)} %hop.7), channel_id=1, source_target_pairs={{0,2},{1,15},{2,4},{3,1},{4,6},{5,3},{6,8},{7,5},{8,10},{9,7},{10,... | collective-permute-start | bytes 1622024 | tf_op jit(solution)/shard_map/ppermute | solution.py:447
  88.4 15.0 %collective-permute-start.9 = (bf16[512,512]{1,0:T(8,128)(2,1)S(1)}, bf16[512,512]{1,0:T(8,128)(2,1)S(1)}, u32[]{:S(2)}, u32[]{:S(2)}) collective-permute-start(bf16[512,512]{1,0:T(8,128)(2,1)S(1)} %hop.10), channel_id=1, source_target_pairs={{0,2},{1,15},{2,4},{3,1},{4,6},{5,3},{6,8},{7,5},{8,10},{9,7},{10,... | collective-permute-start | bytes 1572872 | tf_op jit(solution)/shard_map/ppermute | solution.py:447
  94.2 20.2 %collective-permute-start.6 = (bf16[272,512]{1,0:T(8,128)(2,1)S(1)}, bf16[272,512]{1,0:T(8,128)(2,1)S(1)}, u32[]{:S(2)}, u32[]{:S(2)}) collective-permute-start(bf16[272,512]{1,0:T(8,128)(2,1)S(1)} %get-tuple-element.27), channel_id=1, source_target_pairs={{0,2},{1,15},{2,4},{3,1},{4,6},{5,3},{6,8},{7,5},{8,10},{9,7},{10,... | collective-permute-start | bytes 835592 | tf_op jit(solution)/shard_map/ppermute | solution.py:447
  98.1 16.2 %collective-permute-start.11 = (bf16[272,512]{1,0:T(8,128)(2,1)S(1)}, bf16[272,512]{1,0:T(8,128)(2,1)S(1)}, u32[]{:S(2)}, u32[]{:S(2)}) collective-permute-start(bf16[272,512]{1,0:T(8,128)(2,1)S(1)} %get-tuple-element.30), channel_id=1, source_target_pairs={{0,3},{1,14},{2,5},{3,0},{4,7},{5,2},{6,9},{7,4},{8,11},{9,6},{10,... | collective-permute-start | bytes 835592 | tf_op jit(solution)/shard_map/ppermute | solution.py:449
  103.5 7.4 %collective-permute-start.10 = (bf16[256,512]{1,0:T(8,128)(2,1)S(1)}, bf16[256,512]{1,0:T(8,128)(2,1)S(1)}, u32[]{:S(2)}, u32[]{:S(2)}) collective-permute-start(bf16[256,512]{1,0:T(8,128)(2,1)S(1)} %get-tuple-element.29), channel_id=1, source_target_pairs={{0,2},{1,15},{2,4},{3,1},{4,6},{5,3},{6,8},{7,5},{8,10},{9,7},{10,... | collective-permute-start | bytes 786440 | tf_op jit(solution)/shard_map/ppermute | solution.py:447
  105.4 8.9 %collective-permute-start.12 = (bf16[256,512]{1,0:T(8,128)(2,1)S(1)}, bf16[256,512]{1,0:T(8,128)(2,1)S(1)}, u32[]{:S(2)}, u32[]{:S(2)}) collective-permute-start(bf16[256,512]{1,0:T(8,128)(2,1)S(1)} %get-tuple-element.31), channel_id=1, source_target_pairs={{0,3},{1,14},{2,5},{3,0},{4,7},{5,2},{6,9},{7,4},{8,11},{9,6},{10,... | collective-permute-start | bytes 786440 | tf_op jit(solution)/shard_map/ppermute | solution.py:449

commit v4 on v3

--- a/solution.py
+++ b/solution.py
@@ -25,6 +25,10 @@
     return pltpu.with_memory_space_constraint(x, pltpu.HBM)
 
 
+def hbm_out(shape, dtype):
+    return pltpu.HBM(shape, dtype)
+
+
 def one_hot(mask):
     return mask.astype(F32).astype(BF16)
 
@@ -41,48 +45,35 @@
     return [hi, mid, low]
 
 
-def source_kernel(capacity, group_ref, dest_ref, feats_ref, proj_ref, out_ref, acc_ref):
-    step = pl.program_id(0)
+def source_kernel(capacity, group_ref, dest_ref, feats_ref, proj_ref, out_ref):
     lines = feats_ref.shape[0] // LANES
-
-    @pl.when(step == 0)
-    def _():
-        acc_ref[...] = jnp.zeros_like(acc_ref)
-
-    acc_ref[...] += dot(feats_ref[...], proj_ref[...])
-
-    @pl.when(step == pl.num_programs(0) - 1)
-    def _():
-        first = lax.rem(group_ref[0] * lines, dest_ref.shape[0])
-        lane = lax.broadcasted_iota(jnp.int32, (1, LANES), 1)
-        slot = lax.broadcasted_iota(jnp.int32, (out_ref.shape[0], LANES), 0)
-        total = None
-        for i in range(lines):
-            target = dest_ref[pl.ds(first + i, 1), :] * capacity + lax.rem(lane, capacity)
-            rows = acc_ref[i * LANES : (i + 1) * LANES, :].astype(BF16)
-            term = dot(one_hot(slot == target), rows)
-            total = term if total is None else total + term
-        out_ref[...] = total.astype(BF16)
+    projected = dot(feats_ref[...], proj_ref[...]).astype(BF16)
+    first = lax.rem(group_ref[0] * lines, dest_ref.shape[0])
+    lane = lax.broadcasted_iota(jnp.int32, (1, LANES), 1)
+    slot = lax.broadcasted_iota(jnp.int32, (out_ref.shape[0], LANES), 0)
+    places = []
+    for i in range(lines):
+        target = dest_ref[pl.ds(first + i, 1), :] * capacity + lax.rem(lane, capacity)
+        places.append(one_hot(slot == target))
+    out_ref[...] = dot(jnp.concatenate(places, axis=1), projected).astype(BF16)
 
 
 def source(group, dest, feats, proj, slots, capacity):
-    tokens, width = feats.shape
+    tokens = feats.shape[0]
     cols = proj.shape[1]
     lines = tokens // LANES
-    chunk = 384 if width % 384 == 0 else width
     return pl.pallas_call(
         functools.partial(source_kernel, capacity),
-        out_shape=jax.ShapeDtypeStruct((slots, cols), BF16),
+        out_shape=hbm_out((slots, cols), BF16),
         grid_spec=pltpu.PrefetchScalarGridSpec(
             num_scalar_prefetch=1,
-            grid=(width // chunk,),
+            grid=(1,),
             in_specs=[
                 pl.BlockSpec((8, LANES), lambda i, group: (group[0] * lines // 8, 0)),
-                pl.BlockSpec((tokens, chunk), lambda i, group: (0, i)),
-                pl.BlockSpec((chunk, cols), lambda i, group: (i, 0)),
+                pl.BlockSpec(feats.shape, lambda i, group: (0, 0)),
+                pl.BlockSpec(proj.shape, lambda i, group: (0, 0)),
             ],
             out_specs=pl.BlockSpec((slots, cols), lambda i, group: (0, 0)),
-            scratch_shapes=[pltpu.VMEM((tokens, cols), F32)],
         ),
         compiler_params=PARAMS,
         name="source",
@@ -161,7 +152,7 @@
     return pl.pallas_call(
         text_kernel,
         out_shape=(
-            pltpu.HBM((count, rows, cols), BF16),
+            hbm_out((count, rows, cols), BF16),
             jax.ShapeDtypeStruct((count, 8, rows), F32),
         ),
         grid_spec=pltpu.PrefetchScalarGridSpec(
@@ -248,24 +239,23 @@
 
 
 def merge_kernel(
-    order_ref, slots_ref, visual_ref, vis_squares_ref, text_ref, squares_ref, out_ref, sums_ref
+    first, order_ref, slots_ref, visual_ref, vis_squares_ref, text_ref, squares_ref, out_ref, sums_ref
 ):
     out, squares = merged(
-        order_ref[pl.program_id(0) + 1], slots_ref, visual_ref[...], vis_squares_ref[0:1, :],
+        order_ref[pl.program_id(0) + first], slots_ref, visual_ref[...], vis_squares_ref[0:1, :],
         text_ref[0], squares_ref[0, 0:1, :],
     )
     out_ref[0] = out
     sums_ref[0] = jnp.broadcast_to(squares, sums_ref.shape[1:])
 
 
-def merge(order, slots, visual, vis_squares, text, squares):
-    count = text.shape[0] - 1
+def merge(first, count, order, slots, visual, vis_squares, text, squares):
     _, rows, cols = text.shape
     whole = lambda a: pl.BlockSpec(a.shape, lambda i, order: (0,) * a.ndim)
-    later = lambda a: pl.BlockSpec((1,) + a.shape[1:], lambda i, order: (i + 1, 0, 0))
+    later = lambda a: pl.BlockSpec((1,) + a.shape[1:], lambda i, order: (i + first, 0, 0))
     same = lambda a: pl.BlockSpec((1,) + a.shape[1:], lambda i, order: (i, 0, 0))
     return pl.pallas_call(
-        merge_kernel,
+        functools.partial(merge_kernel, first),
         out_shape=(
             jax.ShapeDtypeStruct((count, rows, cols), BF16),
             jax.ShapeDtypeStruct((count, 8, rows), F32),
@@ -415,9 +405,9 @@
 
     weight = jnp.concatenate([key_w, value_w], axis=1).astype(F32) * norm_gain[:, None]
     weight = weight.astype(BF16)
+    w_other = lax.ppermute(weight, "core", swap)
     blocks = text_embed.reshape(2 * n_y, rows, feats)
     other = lax.ppermute(blocks, "core", swap)
-    w_other = lax.ppermute(weight, "core", swap)
 
     far = n_y // 2
     offset = [far] + [o for o in range(far - 1, 0, -1) for _ in (0, 1)] + [0]
@@ -438,16 +428,22 @@
     )
     flat = ("y", "core")
     streams = [lax.ppermute(key_leaf, flat, ring), lax.ppermute(value_leaf, flat, ring)]
-    product, squares = merge(mine, slots, visual, visual_squares, text, text_squares)
+    merged_blocks = merge(1, 2, mine, slots, visual, visual_squares, text, text_squares)
     ends = []
     for step in range(far - 1):
         last = step == far - 2
+        at = 0 if step == 0 else 2 * step - 2
+        sends = [hop(part, at, last, *merged_blocks, streams[part]) for part in range(2)]
         for part in range(2):
-            sent = hop(part, 2 * step, last, product, squares, streams[part])
-            streams[part] = lax.ppermute(sent[0], flat, ring)
+            streams[part] = lax.ppermute(sends[part][0], flat, ring)
             if last:
-                ends.append(lax.ppermute(sent[1], flat, cross))
-    return finish(product, squares, streams[0], streams[1], ends[0], ends[1], cols)
+                ends.append(lax.ppermute(sends[part][1], flat, cross))
+        if step == 0:
+            slots, _, _ = lax.optimization_barrier((slots, sends[0][0], sends[1][0]))
+            merged_blocks = merge(
+                3, n_y - 3, mine, slots, visual, visual_squares, text, text_squares
+            )
+    return finish(*merged_blocks, streams[0], streams[1], ends[0], ends[1], cols)
 
 
 def solution(mesh):

time: 116 us -> 113 us (0.974)
  waiting for transfers between devices: 19.9 us -> 17.8 us
  local copies, waits for them, and re-layouts: 1.55 us -> 0.04 us
    ppermute x8, waiting for transfers between devices: 13 us -> 8.74 us  [the longest x6 5.32 us: local(): streams[part] = lax.ppermute(sends[part][0], flat, ring)]
    unnamed x4 -> x12, local copies, waits for them, and re-layouts: 1.55 us -> 0.04 us
    all_to_all x1, waiting for transfers between devices: 5.69 us -> 6.87 us  [local(): lax.all_to_all(outgoing.reshape(n_grp, capacity, feats), 'grp', 0, 0, til...]
    pallas_call x3 -> x4, Pallas kernels: 18.4 us -> 18.5 us  [the longest x1 8.24 us: text_products(): pl.pallas_call(text_kernel, out_shape=(hbm_out((count, rows, cols), BF16)...]
  transfers between devices with their start and end apart: 14 -> 14, of which waited for: 7 -> 7; matrix products, arithmetic and copies ran while one was open for 2% -> 1% of each run, Pallas kernels for 17% -> 18%
where the time goes in v4:
time: 113 us; the launch traced here: 112 us
  starting transfers between devices  68 us (60%)
  Pallas kernels  23.7 us (21%)
  waiting for transfers between devices  17.8 us (16%)
  other arithmetic  1.2 us (1%)
    ppermute x6, starting transfers between devices, local(): streams[part] = lax.ppermute(sends[part][0], flat, ring)  18.8 us
    ppermute x1, starting transfers between devices, local(): other = lax.ppermute(blocks, 'core', swap)  16.2 us
    ppermute x2, starting transfers between devices, local(): ends.append(lax.ppermute(sends[part][1], flat, cross))  9.73 us
    all_to_all x1, starting transfers between devices, local(): lax.all_to_all(outgoing.reshape(n_grp, capacity, feats), 'grp', 0, 0, til...  9.3 us
    pallas_call x1, Pallas kernels, text_products(): pl.pallas_call(text_kernel, out_shape=(hbm_out((count, rows, cols), BF16)...  8.24 us
    pallas_call x2, Pallas kernels, merge(): pl.pallas_call(functools.partial(merge_kernel, first), out_shape=(jax.Sha...  7.68 us
    all_to_all x1, waiting for transfers between devices, local(): lax.all_to_all(outgoing.reshape(n_grp, capacity, feats), 'grp', 0, 0, til...  6.87 us
    ppermute x6, waiting for transfers between devices, local(): streams[part] = lax.ppermute(sends[part][0], flat, ring)  5.32 us
  transfers between devices with their start and end apart: 14, of which 7 were waited for; matrix products, arithmetic and copies ran while one was open for 1% of the time, Pallas kernels for 18%

profile of v4, /device:TPU:1, one launch (start us, length us, event | category | flops | bytes accessed | tf_op | source)
XLA Modules:
  0.0 111.6 jit_solution(10700352306622830461)
XLA Ops:
  0.7 16.2 %collective-permute-start = (bf16[16,256,256]{2,1,0:T(8,128)(2,1)}, bf16[16,256,256]{2,1,0:T(8,128)(2,1)S(1)}, u32[]{:S(2)}, u32[]{:S(2)}) collective-permute-start(bf16[16,256,256]{2,1,0:T(8,128)(2,1)} %bitcast.9), channel_id=1, source_target_pairs={{0,1},{1,0},{2,3},{3,2},{4,5},{5,4},{6,7},{7,6},{8,9},{9,8},{10,11... | collective-permute-start | bytes 6291464 | tf_op jit(solution)/shard_map/ppermute | solution.py:410
  16.9 2.6 %source.1 = bf16[512,256]{1,0:T(8,128)(2,1)} custom-call(s32[1]{0:T(128)} %bitcast.group_ref, s32[128,128]{1,0:T(8,128)} %bitcast.7, bf16[256,1152]{1,0:T(8,128)(2,1)} %feats_ref.1, bf16[1152,256]{1,0:T(8,128)(2,1)} %proj_ref.1), custom_call_target="tpu_custom_call" | custom-call | tf_op jit(solution)/shard_map/source/pallas_call | solution.py:65
  19.5 9.3 %all-to-all-start = ((bf16[64,8,256]{2,1,0:T(8,128)(2,1)}), bf16[64,8,256]{2,1,0:T(8,128)(2,1)S(1)}, u32[]{:S(2)}, u32[]{:S(2)}) async-start(bf16[64,8,256]{2,1,0:T(8,128)(2,1)} %bitcast.11), calls=%async_computation | async-start | bytes 524288 | tf_op jit(solution)/shard_map/all_to_all | solution.py:402
  28.8 1.2 %multiply_convert_fusion.w_own_ref = bf16[256,1024]{1,0:T(8,128)(2,1)S(1)} fusion(bf16[256,512]{1,0:T(8,128)(2,1)} %param.17, bf16[256,512]{1,0:T(8,128)(2,1)} %param.16, f32[256]{0:T(256)} %param.15), kind=kLoop, calls=%fused_computation | loop fusion | flops 1572864 | bytes 1049600 | tf_op jit(solution)/shard_map/convert_element_type | solution.py:407
  30.0 2.2 %collective-permute-start.1 = (bf16[256,1024]{1,0:T(8,128)(2,1)S(1)}, bf16[256,1024]{1,0:T(8,128)(2,1)S(1)}, u32[]{:S(2)}, u32[]{:S(2)}) collective-permute-start(bf16[256,1024]{1,0:T(8,128)(2,1)S(1)} %multiply_convert_fusion.w_own_ref), channel_id=1, source_target_pairs={{0,1},{1,0},{2,3},{3,2},{4,5},{5,4},{6,7},{7,6},{8,9},{9,8},{10,11... | collective-permute-start | bytes 1572872 | tf_op jit(solution)/shard_map/ppermute | solution.py:408
  32.2 0.5 slots.1.slots_ref
  32.8 1.0 collective-permute-done.1.w_other_ref
  33.8 8.2 %text.1 = (bf16[8,256,1024]{2,1,0:T(8,128)(2,1)}, f32[8,8,256]{2,1,0:T(8,128)S(1)}) custom-call(s32[8]{0:T(128)S(1)} %broadcast_select_fusion.order_ref, bf16[16,256,256]{2,1,0:T(8,128)(2,1)} %bitcast.10, bf16[16,256,256]{2,1,0:T(8,128)(2,1)S(1)} %collective-permute-done.other_ref, bf16[256,1024]{1,0:T(8,128)(2,1)S(1)} %multiply_convert_fusion.w_own_ref, ...), custom_call_target="tpu_custom_call" | custom-call | flops 1 | bytes 1 | tf_op jit(solution)/shard_map/text/pallas_call | solution.py:152
  42.1 6.9 %all-to-all-done = bf16[64,8,256]{2,1,0:T(8,128)(2,1)S(1)} async-done(((bf16[64,8,256]{2,1,0:T(8,128)(2,1)}), bf16[64,8,256]{2,1,0:T(8,128)(2,1)S(1)}, u32[]{:S(2)}, u32[]{:S(2)}) %all-to-all-start) | async-done | bytes 262176 | tf_op jit(solution)/shard_map/all_to_all | solution.py:402
  48.9 3.7 %collective-permute-start.2 = (bf16[512,256]{1,0:T(8,128)(2,1)S(1)}, bf16[512,256]{1,0:T(8,128)(2,1)S(1)}, u32[]{:S(2)}, u32[]{:S(2)}) collective-permute-start(bf16[512,256]{1,0:T(8,128)(2,1)S(1)} %bitcast.5), channel_id=1, source_target_pairs={{0,1},{1,0},{2,3},{3,2},{4,5},{5,4},{6,7},{7,6},{8,9},{9,8},{10,11... | collective-permute-start | bytes 786440 | tf_op jit(solution)/shard_map/ppermute | solution.py:425
  52.6 1.1 %collective-permute-done.2.v_other_ref = bf16[512,256]{1,0:T(8,128)(2,1)S(1)} collective-permute-done((bf16[512,256]{1,0:T(8,128)(2,1)S(1)}, bf16[512,256]{1,0:T(8,128)(2,1)S(1)}, u32[]{:S(2)}, u32[]{:S(2)}) %collective-permute-start.2) | collective-permute-done | bytes 262176 | tf_op jit(solution)/shard_map/ppermute | solution.py:425
  53.8 2.9 %visual.1 = (bf16[512,1024]{1,0:T(8,128)(2,1)S(1)}, f32[8,512]{1,0:T(8,128)S(1)}, bf16[272,512]{1,0:T(8,128)(2,1)S(1)}, bf16[256,512]{1,0:T(8,128)(2,1)S(1)}) custom-call(s32[8]{0:T(128)S(1)} %broadcast_select_fusion.order_ref, bf16[512,256]{1,0:T(8,128)(2,1)S(1)} %bitcast.6, bf16[512,256]{1,0:T(8,128)(2,1)S(1)} %collective-permute-done.2.v_other_ref, ...), custom_call_target="tpu_custom_call" | custom-call | tf_op jit(solution)/shard_map/visual/pallas_call | solution.py:219
  56.6 5.1 %collective-permute-start.3 = (bf16[272,512]{1,0:T(8,128)(2,1)S(1)}, bf16[272,512]{1,0:T(8,128)(2,1)S(1)}, u32[]{:S(2)}, u32[]{:S(2)}) collective-permute-start(bf16[272,512]{1,0:T(8,128)(2,1)S(1)} %get-tuple-element.29), channel_id=1, source_target_pairs={{0,2},{1,15},{2,4},{3,1},{4,6},{5,3},{6,8},{7,5},{8,10},{9,7},{10,... | collective-permute-start | bytes 835592 | tf_op jit(solution)/shard_map/ppermute | solution.py:430
  61.7 3.0 %collective-permute-start.4 = (bf16[256,512]{1,0:T(8,128)(2,1)S(1)}, bf16[256,512]{1,0:T(8,128)(2,1)S(1)}, u32[]{:S(2)}, u32[]{:S(2)}) collective-permute-start(bf16[256,512]{1,0:T(8,128)(2,1)S(1)} %get-tuple-element.30), channel_id=1, source_target_pairs={{0,2},{1,15},{2,4},{3,1},{4,6},{5,3},{6,8},{7,5},{8,10},{9,7},{10,... | collective-permute-start | bytes 786440 | tf_op jit(solution)/shard_map/ppermute | solution.py:430
  64.7 2.6 %merge.2 = (bf16[2,256,1024]{2,1,0:T(8,128)(2,1)S(1)}, f32[2,8,256]{2,1,0:T(8,128)S(1)}) custom-call(s32[8]{0:T(128)S(1)} %broadcast_select_fusion.order_ref, s32[8,512]{1,0:T(8,128)S(1)} %slots.1.slots_ref, bf16[512,1024]{1,0:T(8,128)(2,1)S(1)} %get-tuple-element.25.visual_ref, f32[8,512]{1,0:T(8,128)S(1)} %get-tuple-element.26.vis_squares_ref, ...), custom_call_target="tpu_custom_call" | custom-call | flops 536870912 | bytes 2097152 | tf_op jit(solution)/shard_map/merge/pallas_call | solution.py:257
  67.4 3.0 %collective-permute-start.5 = (bf16[528,512]{1,0:T(8,128)(2,1)S(1)}, bf16[528,512]{1,0:T(8,128)(2,1)S(1)}, u32[]{:S(2)}, u32[]{:S(2)}) collective-permute-start(bf16[528,512]{1,0:T(8,128)(2,1)S(1)} %hop.6), channel_id=1, source_target_pairs={{0,2},{1,15},{2,4},{3,1},{4,6},{5,3},{6,8},{7,5},{8,10},{9,7},{10,... | collective-permute-start | bytes 1622024 | tf_op jit(solution)/shard_map/ppermute | solution.py:438
  70.5 3.0 %collective-permute-start.8 = (bf16[512,512]{1,0:T(8,128)(2,1)S(1)}, bf16[512,512]{1,0:T(8,128)(2,1)S(1)}, u32[]{:S(2)}, u32[]{:S(2)}) collective-permute-start(bf16[512,512]{1,0:T(8,128)(2,1)S(1)} %hop.7), channel_id=1, source_target_pairs={{0,2},{1,15},{2,4},{3,1},{4,6},{5,3},{6,8},{7,5},{8,10},{9,7},{10,... | collective-permute-start | bytes 1572872 | tf_op jit(solution)/shard_map/ppermute | solution.py:438
  73.5 5.1 %merge.3 = (bf16[5,256,1024]{2,1,0:T(8,128)(2,1)S(1)}, f32[5,8,256]{2,1,0:T(8,128)S(1)}) custom-call(s32[8]{0:T(128)S(1)} %broadcast_select_fusion.order_ref, s32[8,512]{1,0:T(8,128)S(1)} %slots.1.slots_ref, bf16[512,1024]{1,0:T(8,128)(2,1)S(1)} %get-tuple-element.25.visual_ref, f32[8,512]{1,0:T(8,128)S(1)} %get-tuple-element.26.vis_squares_ref, ...), custom_call_target="tpu_custom_call" | custom-call | flops 1342177280 | bytes 5242880 | tf_op jit(solution)/shard_map/merge/pallas_call | solution.py:257
  78.6 0.2 hop.8
  78.7 3.1 %collective-permute-start.6 = (bf16[528,512]{1,0:T(8,128)(2,1)S(1)}, bf16[528,512]{1,0:T(8,128)(2,1)S(1)}, u32[]{:S(2)}, u32[]{:S(2)}) collective-permute-start(bf16[528,512]{1,0:T(8,128)(2,1)S(1)} %hop.8), channel_id=1, source_target_pairs={{0,2},{1,15},{2,4},{3,1},{4,6},{5,3},{6,8},{7,5},{8,10},{9,7},{10,... | collective-permute-start | bytes 1622024 | tf_op jit(solution)/shard_map/ppermute | solution.py:438
  81.8 1.6 %collective-permute-done.8.came_ref = bf16[512,512]{1,0:T(8,128)(2,1)S(1)} collective-permute-done((bf16[512,512]{1,0:T(8,128)(2,1)S(1)}, bf16[512,512]{1,0:T(8,128)(2,1)S(1)}, u32[]{:S(2)}, u32[]{:S(2)}) %collective-permute-start.8) | collective-permute-done | bytes 524320 | tf_op jit(solution)/shard_map/ppermute | solution.py:438
  83.5 3.9 %collective-permute-start.9 = (bf16[512,512]{1,0:T(8,128)(2,1)S(1)}, bf16[512,512]{1,0:T(8,128)(2,1)S(1)}, u32[]{:S(2)}, u32[]{:S(2)}) collective-permute-start(bf16[512,512]{1,0:T(8,128)(2,1)S(1)} %hop.10), channel_id=1, source_target_pairs={{0,2},{1,15},{2,4},{3,1},{4,6},{5,3},{6,8},{7,5},{8,10},{9,7},{10,... | collective-permute-start | bytes 1572872 | tf_op jit(solution)/shard_map/ppermute | solution.py:438
  87.4 1.8 %collective-permute-done.6.came_ref = bf16[528,512]{1,0:T(8,128)(2,1)S(1)} collective-permute-done((bf16[528,512]{1,0:T(8,128)(2,1)S(1)}, bf16[528,512]{1,0:T(8,128)(2,1)S(1)}, u32[]{:S(2)}, u32[]{:S(2)}) %collective-permute-start.6) | collective-permute-done | bytes 540704 | tf_op jit(solution)/shard_map/ppermute | solution.py:438
  89.2 0.2 hop.9
  89.4 3.9 %collective-permute-start.7 = (bf16[272,512]{1,0:T(8,128)(2,1)S(1)}, bf16[272,512]{1,0:T(8,128)(2,1)S(1)}, u32[]{:S(2)}, u32[]{:S(2)}) collective-permute-start(bf16[272,512]{1,0:T(8,128)(2,1)S(1)} %get-tuple-element.34), channel_id=1, source_target_pairs={{0,2},{1,15},{2,4},{3,1},{4,6},{5,3},{6,8},{7,5},{8,10},{9,7},{10,... | collective-permute-start | bytes 835592 | tf_op jit(solution)/shard_map/ppermute | solution.py:438
  93.3 6.2 %collective-permute-start.11 = (bf16[272,512]{1,0:T(8,128)(2,1)S(1)}, bf16[272,512]{1,0:T(8,128)(2,1)S(1)}, u32[]{:S(2)}, u32[]{:S(2)}) collective-permute-start(bf16[272,512]{1,0:T(8,128)(2,1)S(1)} %get-tuple-element.36), channel_id=1, source_target_pairs={{0,3},{1,14},{2,5},{3,0},{4,7},{5,2},{6,9},{7,4},{8,11},{9,6},{10,... | collective-permute-start | bytes 835592 | tf_op jit(solution)/shard_map/ppermute | solution.py:440
  99.5 0.2 hop.11
  99.7 1.9 %collective-permute-start.10 = (bf16[256,512]{1,0:T(8,128)(2,1)S(1)}, bf16[256,512]{1,0:T(8,128)(2,1)S(1)}, u32[]{:S(2)}, u32[]{:S(2)}) collective-permute-start(bf16[256,512]{1,0:T(8,128)(2,1)S(1)} %get-tuple-element.35), channel_id=1, source_target_pairs={{0,2},{1,15},{2,4},{3,1},{4,6},{5,3},{6,8},{7,5},{8,10},{9,7},{10,... | collective-permute-start | bytes 786440 | tf_op jit(solution)/shard_map/ppermute | solution.py:438
  101.6 3.5 %collective-permute-start.12 = (bf16[256,512]{1,0:T(8,128)(2,1)S(1)}, bf16[256,512]{1,0:T(8,128)(2,1)S(1)}, u32[]{:S(2)}, u32[]{:S(2)}) collective-permute-start(bf16[256,512]{1,0:T(8,128)(2,1)S(1)} %get-tuple-element.37), channel_id=1, source_target_pairs={{0,3},{1,14},{2,5},{3,0},{4,7},{5,2},{6,9},{7,4},{8,11},{9,6},{10,... | collective-permute-start | bytes 786440 | tf_op jit(solution)/shard_map/ppermute | solution.py:440
  105.2 2.0 %collective-permute-done.10.v_ref = bf16[256,512]{1,0:T(8,128)(2,1)S(1)} collective-permute-done((bf16[256,512]{1,0:T(8,128)(2,1)S(1)}, bf16[256,512]{1,0:T(8,128)(2,1)S(1)}, u32[]{:S(2)}, u32[]{:S(2)}) %collective-permute-start.10) | collective-permute-done | bytes 262176 | tf_op jit(solution)/shard_map/ppermute | solution.py:438
  107.1 3.4 %collective-permute-done.12.v2_ref = bf16[256,512]{1,0:T(8,128)(2,1)S(1)} collective-permute-done((bf16[256,512]{1,0:T(8,128)(2,1)S(1)}, bf16[256,512]{1,0:T(8,128)(2,1)S(1)}, u32[]{:S(2)}, u32[]{:S(2)}) %collective-permute-start.12) | collective-permute-done | bytes 262176 | tf_op jit(solution)/shard_map/ppermute | solution.py:440
  110.5 1.1 finish.1
  (23 shorter events, 0.4 us)
Async XLA Ops:
  0.6 32.1 %copy-start.2 = (s32[8]{0:T(128)S(1)}, s32[8]{0:T(128)}, u32[]{:S(2)}) copy-start(s32[8]{0:T(128)} %constant.48) | copy-start | bytes 100
  0.6 32.1 %copy-start.3 = (s32[8]{0:T(128)S(1)}, s32[8]{0:T(128)}, u32[]{:S(2)}) copy-start(s32[8]{0:T(128)} %constant.47) | copy-start | bytes 100
  0.7 32.1 %copy-start.4 = (s32[8]{0:T(128)S(1)}, s32[8]{0:T(128)}, u32[]{:S(2)}) copy-start(s32[8]{0:T(128)} %constant.45.clone) | copy-start | bytes 100
  0.7 32.1 %copy-start.5 = (s32[8]{0:T(128)S(1)}, s32[8]{0:T(128)}, u32[]{:S(2)}) copy-start(s32[8]{0:T(128)} %constant.44.clone) | copy-start | bytes 100
  0.7 31.6 %copy-start = (s32[16384]{0:T(1024)S(1)}, s32[16384]{0:T(1024)}, u32[]{:S(2)}) copy-start(s32[16384]{0:T(1024)} %param.13) | copy-start | bytes 196612
  0.7 31.6 %copy-start.1 = (s32[1,4096]{1,0:T(1,128)S(1)}, s32[1,4096]{1,0:T(1,128)}, u32[]{:S(2)}) copy-start(s32[1,4096]{1,0:T(1,128)} %layout_ref.1) | copy-start | bytes 49156
  0.7 33.1 %collective-permute-start = (bf16[16,256,256]{2,1,0:T(8,128)(2,1)}, bf16[16,256,256]{2,1,0:T(8,128)(2,1)S(1)}, u32[]{:S(2)}, u32[]{:S(2)}) collective-permute-start(bf16[16,256,256]{2,1,0:T(8,128)(2,1)} %bitcast.9), channel_id=1, source_target_pairs={{0,1},{1,0},{2,3},{3,2},{4,5},{5,4},{6,7},{7,6},{8,9},{9,8},{10,11... | collective-permute-start | bytes 6291464 | tf_op jit(solution)/shard_map/ppermute | solution.py:410
  19.5 29.4 %all-to-all-start = ((bf16[64,8,256]{2,1,0:T(8,128)(2,1)}), bf16[64,8,256]{2,1,0:T(8,128)(2,1)S(1)}, u32[]{:S(2)}, u32[]{:S(2)}) async-start(bf16[64,8,256]{2,1,0:T(8,128)(2,1)} %bitcast.11), calls=%async_computation | async-start | bytes 524288 | tf_op jit(solution)/shard_map/all_to_all | solution.py:402
  30.0 3.8 %collective-permute-start.1 = (bf16[256,1024]{1,0:T(8,128)(2,1)S(1)}, bf16[256,1024]{1,0:T(8,128)(2,1)S(1)}, u32[]{:S(2)}, u32[]{:S(2)}) collective-permute-start(bf16[256,1024]{1,0:T(8,128)(2,1)S(1)} %multiply_convert_fusion.w_own_ref), channel_id=1, source_target_pairs={{0,1},{1,0},{2,3},{3,2},{4,5},{5,4},{6,7},{7,6},{8,9},{9,8},{10,11... | collective-permute-start | bytes 1572872 | tf_op jit(solution)/shard_map/ppermute | solution.py:408
  48.9 4.8 %collective-permute-start.2 = (bf16[512,256]{1,0:T(8,128)(2,1)S(1)}, bf16[512,256]{1,0:T(8,128)(2,1)S(1)}, u32[]{:S(2)}, u32[]{:S(2)}) collective-permute-start(bf16[512,256]{1,0:T(8,128)(2,1)S(1)} %bitcast.5), channel_id=1, source_target_pairs={{0,1},{1,0},{2,3},{3,2},{4,5},{5,4},{6,7},{7,6},{8,9},{9,8},{10,11... | collective-permute-start | bytes 786440 | tf_op jit(solution)/shard_map/ppermute | solution.py:425
  56.6 10.7 %collective-permute-start.3 = (bf16[272,512]{1,0:T(8,128)(2,1)S(1)}, bf16[272,512]{1,0:T(8,128)(2,1)S(1)}, u32[]{:S(2)}, u32[]{:S(2)}) collective-permute-start(bf16[272,512]{1,0:T(8,128)(2,1)S(1)} %get-tuple-element.29), channel_id=1, source_target_pairs={{0,2},{1,15},{2,4},{3,1},{4,6},{5,3},{6,8},{7,5},{8,10},{9,7},{10,... | collective-permute-start | bytes 835592 | tf_op jit(solution)/shard_map/ppermute | solution.py:430
  61.7 8.6 %collective-permute-start.4 = (bf16[256,512]{1,0:T(8,128)(2,1)S(1)}, bf16[256,512]{1,0:T(8,128)(2,1)S(1)}, u32[]{:S(2)}, u32[]{:S(2)}) collective-permute-start(bf16[256,512]{1,0:T(8,128)(2,1)S(1)} %get-tuple-element.30), channel_id=1, source_target_pairs={{0,2},{1,15},{2,4},{3,1},{4,6},{5,3},{6,8},{7,5},{8,10},{9,7},{10,... | collective-permute-start | bytes 786440 | tf_op jit(solution)/shard_map/ppermute | solution.py:430
  67.4 11.2 %collective-permute-start.5 = (bf16[528,512]{1,0:T(8,128)(2,1)S(1)}, bf16[528,512]{1,0:T(8,128)(2,1)S(1)}, u32[]{:S(2)}, u32[]{:S(2)}) collective-permute-start(bf16[528,512]{1,0:T(8,128)(2,1)S(1)} %hop.6), channel_id=1, source_target_pairs={{0,2},{1,15},{2,4},{3,1},{4,6},{5,3},{6,8},{7,5},{8,10},{9,7},{10,... | collective-permute-start | bytes 1622024 | tf_op jit(solution)/shard_map/ppermute | solution.py:438
  70.5 12.9 %collective-permute-start.8 = (bf16[512,512]{1,0:T(8,128)(2,1)S(1)}, bf16[512,512]{1,0:T(8,128)(2,1)S(1)}, u32[]{:S(2)}, u32[]{:S(2)}) collective-permute-start(bf16[512,512]{1,0:T(8,128)(2,1)S(1)} %hop.7), channel_id=1, source_target_pairs={{0,2},{1,15},{2,4},{3,1},{4,6},{5,3},{6,8},{7,5},{8,10},{9,7},{10,... | collective-permute-start | bytes 1572872 | tf_op jit(solution)/shard_map/ppermute | solution.py:438
  78.7 10.5 %collective-permute-start.6 = (bf16[528,512]{1,0:T(8,128)(2,1)S(1)}, bf16[528,512]{1,0:T(8,128)(2,1)S(1)}, u32[]{:S(2)}, u32[]{:S(2)}) collective-permute-start(bf16[528,512]{1,0:T(8,128)(2,1)S(1)} %hop.8), channel_id=1, source_target_pairs={{0,2},{1,15},{2,4},{3,1},{4,6},{5,3},{6,8},{7,5},{8,10},{9,7},{10,... | collective-permute-start | bytes 1622024 | tf_op jit(solution)/shard_map/ppermute | solution.py:438
  83.5 16.0 %collective-permute-start.9 = (bf16[512,512]{1,0:T(8,128)(2,1)S(1)}, bf16[512,512]{1,0:T(8,128)(2,1)S(1)}, u32[]{:S(2)}, u32[]{:S(2)}) collective-permute-start(bf16[512,512]{1,0:T(8,128)(2,1)S(1)} %hop.10), channel_id=1, source_target_pairs={{0,2},{1,15},{2,4},{3,1},{4,6},{5,3},{6,8},{7,5},{8,10},{9,7},{10,... | collective-permute-start | bytes 1572872 | tf_op jit(solution)/shard_map/ppermute | solution.py:438
  89.4 21.2 %collective-permute-start.7 = (bf16[272,512]{1,0:T(8,128)(2,1)S(1)}, bf16[272,512]{1,0:T(8,128)(2,1)S(1)}, u32[]{:S(2)}, u32[]{:S(2)}) collective-permute-start(bf16[272,512]{1,0:T(8,128)(2,1)S(1)} %get-tuple-element.34), channel_id=1, source_target_pairs={{0,2},{1,15},{2,4},{3,1},{4,6},{5,3},{6,8},{7,5},{8,10},{9,7},{10,... | collective-permute-start | bytes 835592 | tf_op jit(solution)/shard_map/ppermute | solution.py:438
  93.3 17.2 %collective-permute-start.11 = (bf16[272,512]{1,0:T(8,128)(2,1)S(1)}, bf16[272,512]{1,0:T(8,128)(2,1)S(1)}, u32[]{:S(2)}, u32[]{:S(2)}) collective-permute-start(bf16[272,512]{1,0:T(8,128)(2,1)S(1)} %get-tuple-element.36), channel_id=1, source_target_pairs={{0,3},{1,14},{2,5},{3,0},{4,7},{5,2},{6,9},{7,4},{8,11},{9,6},{10,... | collective-permute-start | bytes 835592 | tf_op jit(solution)/shard_map/ppermute | solution.py:440
  99.7 7.4 %collective-permute-start.10 = (bf16[256,512]{1,0:T(8,128)(2,1)S(1)}, bf16[256,512]{1,0:T(8,128)(2,1)S(1)}, u32[]{:S(2)}, u32[]{:S(2)}) collective-permute-start(bf16[256,512]{1,0:T(8,128)(2,1)S(1)} %get-tuple-element.35), channel_id=1, source_target_pairs={{0,2},{1,15},{2,4},{3,1},{4,6},{5,3},{6,8},{7,5},{8,10},{9,7},{10,... | collective-permute-start | bytes 786440 | tf_op jit(solution)/shard_map/ppermute | solution.py:438
  101.6 8.9 %collective-permute-start.12 = (bf16[256,512]{1,0:T(8,128)(2,1)S(1)}, bf16[256,512]{1,0:T(8,128)(2,1)S(1)}, u32[]{:S(2)}, u32[]{:S(2)}) collective-permute-start(bf16[256,512]{1,0:T(8,128)(2,1)S(1)} %get-tuple-element.37), channel_id=1, source_target_pairs={{0,3},{1,14},{2,5},{3,0},{4,7},{5,2},{6,9},{7,4},{8,11},{9,6},{10,... | collective-permute-start | bytes 786440 | tf_op jit(solution)/shard_map/ppermute | solution.py:440

commit v5 on v4

--- a/solution.py
+++ b/solution.py
@@ -189,15 +189,34 @@
     return out.astype(BF16), squares
 
 
+def own_kernel(tokens_ref, weight_ref, out_ref, squares_ref):
+    tokens = tokens_ref[...]
+    out_ref[...] = dot(tokens, weight_ref[...])
+    squares_ref[...] = lane_sums(tokens.astype(F32))
+
+
+def own_products(tokens, weight):
+    return pl.pallas_call(
+        own_kernel,
+        out_shape=(
+            jax.ShapeDtypeStruct((tokens.shape[0], weight.shape[1]), F32),
+            jax.ShapeDtypeStruct((8, tokens.shape[0]), F32),
+        ),
+        in_specs=vmem(2),
+        out_specs=tuple(vmem(2)),
+        compiler_params=PARAMS,
+        name="own",
+    )(tokens, weight)
+
+
 def visual_kernel(
-    order_ref, v_own_ref, v_other_ref, w_own_ref, w_other_ref, slots_ref, text_ref, squares_ref,
+    order_ref, own_ref, own_squares_ref, v_other_ref, w_other_ref, slots_ref, text_ref, squares_ref,
     visual_ref, vis_squares_ref, key_ref, value_ref,
 ):
-    own = v_own_ref[...]
     other = v_other_ref[...]
-    visual = (dot(own, w_own_ref[...]) + dot(other, w_other_ref[...])).astype(BF16)
+    visual = (own_ref[...] + dot(other, w_other_ref[...])).astype(BF16)
     visual_ref[...] = visual
-    vis_squares = lane_sums(own.astype(F32)) + lane_sums(other.astype(F32))
+    vis_squares = own_squares_ref[...] + lane_sums(other.astype(F32))
     vis_squares_ref[...] = vis_squares
     out, squares = merged(
         order_ref[0], slots_ref, visual, vis_squares[0:1, :], text_ref[0], squares_ref[0, 0:1, :]
@@ -210,10 +229,10 @@
     key_ref[rows:, :] = stripe_of(wide)
 
 
-def visual_products(order, v_own, v_other, w_own, w_other, slots, text, squares):
+def visual_products(order, own, own_squares, v_other, w_other, slots, text, squares):
     _, rows, cols2 = text.shape
     cols = cols2 // 2
-    count = v_own.shape[0]
+    count = v_other.shape[0]
     whole = lambda a: pl.BlockSpec(a.shape, lambda i, order: (0,) * a.ndim)
     shapes = [((count, cols2), BF16), ((8, count), F32), ((rows + STRIPE, cols), BF16), ((rows, cols), BF16)]
     return pl.pallas_call(
@@ -223,9 +242,9 @@
             num_scalar_prefetch=1,
             grid=(1,),
             in_specs=[
-                whole(v_own),
+                whole(own),
+                whole(own_squares),
                 whole(v_other),
-                whole(w_own),
                 whole(w_other),
                 whole(slots),
                 pl.BlockSpec((1, rows, cols2), lambda i, order: (0, 0, 0)),
@@ -235,7 +254,7 @@
         ),
         compiler_params=PARAMS,
         name="visual",
-    )(order, v_own, v_other, w_own, w_other, slots, text, squares)
+    )(order, own, own_squares, v_other, w_other, slots, text, squares)
 
 
 def merge_kernel(
@@ -334,44 +353,55 @@
     )(product, squares, came)
 
 
-def finish_kernel(product_ref, squares_ref, k_ref, v_ref, k2_ref, v2_ref, key_ref, value_ref):
-    rows = product_ref.shape[1]
-    cols = key_ref.shape[1]
+def scaled_sum(product_ref, a_ref, b_ref, inverse, out_ref):
+    rows, cols = out_ref.shape
+    for i in range(rows // LANES):
+        to = slice(i * LANES, (i + 1) * LANES)
+        scale = jnp.broadcast_to(inverse[:, to], (LANES, LANES)).T
+        for j in range(cols // LANES):
+            lane = slice(j * LANES, (j + 1) * LANES)
+            total = product_ref[0, to, lane].astype(F32) + a_ref[to, lane].astype(F32)
+            out_ref[to, lane] = ((total + b_ref[to, lane].astype(F32)) * scale).astype(BF16)
+
+
+def finish_keys_kernel(product_ref, squares_ref, k_ref, k2_ref, out_ref, inverse_ref):
+    rows = out_ref.shape[0]
     squares = squares_ref[0, 0:1, :]
     squares += stripe_sum(k_ref[rows:, :].astype(F32))[:, :rows]
     squares += stripe_sum(k2_ref[rows:, :].astype(F32))[:, :rows]
     inverse = lax.rsqrt(squares / D + EPS)
-    for i in range(rows // LANES):
-        to = slice(i * LANES, (i + 1) * LANES)
-        scale = jnp.broadcast_to(inverse[:, to], (LANES, LANES)).T
-        for out_ref, a_ref, b_ref, at in (
-            (key_ref, k_ref, k2_ref, 0),
-            (value_ref, v_ref, v2_ref, cols),
-        ):
-            for j in range(cols // LANES):
-                lane = slice(j * LANES, (j + 1) * LANES)
-                own = product_ref[0, to, at + j * LANES : at + (j + 1) * LANES].astype(F32)
-                total = own + a_ref[to, lane].astype(F32) + b_ref[to, lane].astype(F32)
-                out_ref[to, lane] = (total * scale).astype(BF16)
-
-
-def finish(product, squares, k, v, k2, v2, cols):
-    rows = product.shape[1]
-    whole = lambda a: pl.BlockSpec(a.shape, lambda i: (0,) * a.ndim)
-    last = product.shape[0] - 1
-    return pl.pallas_call(
-        finish_kernel,
-        out_shape=(jax.ShapeDtypeStruct((rows, cols), BF16),) * 2,
+    inverse_ref[...] = jnp.broadcast_to(inverse, inverse_ref.shape)
+    scaled_sum(product_ref, k_ref, k2_ref, inverse, out_ref)
+
+
+def finish_values_kernel(product_ref, inverse_ref, v_ref, v2_ref, out_ref):
+    scaled_sum(product_ref, v_ref, v2_ref, inverse_ref[0:1, :], out_ref)
+
+
+def finish(part, product, lane_values, a, b):
+    count, rows, cols2 = product.shape
+    cols = cols2 // 2
+    whole = lambda x: pl.BlockSpec(x.shape, lambda i: (0,) * x.ndim)
+    out_shape = [jax.ShapeDtypeStruct((rows, cols), BF16)]
+    if part == 0:
+        out_shape.append(jax.ShapeDtypeStruct((8, rows), F32))
+        lanes = pl.BlockSpec((1, 8, rows), lambda i: (count - 1, 0, 0))
+    else:
+        lanes = whole(lane_values)
+    return pl.pallas_call(
+        finish_values_kernel if part else finish_keys_kernel,
+        out_shape=tuple(out_shape),
         grid=(1,),
         in_specs=[
-            pl.BlockSpec((1,) + product.shape[1:], lambda i: (last, 0, 0)),
-            pl.BlockSpec((1,) + squares.shape[1:], lambda i: (last, 0, 0)),
-        ]
-        + [whole(a) for a in (k, v, k2, v2)],
-        out_specs=(pl.BlockSpec((rows, cols), lambda i: (0, 0)),) * 2,
+            pl.BlockSpec((1, rows, cols), lambda i: (count - 1, 0, part)),
+            lanes,
+            whole(a),
+            whole(b),
+        ],
+        out_specs=tuple(pl.BlockSpec(x.shape, lambda i: (0, 0)) for x in out_shape),
         compiler_params=PARAMS,
         name="finish",
-    )(product, squares, k, v, k2, v2)
+    )(product, lane_values, a, b)
 
 
 def local(vis_feats, proj_w, text_embed, dest_group, layout, norm_gain, key_w, value_w):
@@ -424,26 +454,29 @@
     arrived, text_squares, slots = lax.optimization_barrier((arrived, text_squares, slots))
     arrived_other = lax.ppermute(arrived, "core", swap)
     visual, visual_squares, key_leaf, value_leaf = visual_products(
-        mine, arrived, arrived_other, weight, w_other, slots, text, text_squares
+        mine, *own_products(arrived, weight), arrived_other, w_other, slots, text, text_squares
     )
     flat = ("y", "core")
     streams = [lax.ppermute(key_leaf, flat, ring), lax.ppermute(value_leaf, flat, ring)]
-    merged_blocks = merge(1, 2, mine, slots, visual, visual_squares, text, text_squares)
+    blocks_of = (mine, slots, visual, visual_squares, text, text_squares)
+    merged_blocks = merge(1, 2, *blocks_of)
     ends = []
     for step in range(far - 1):
         last = step == far - 2
-        at = 0 if step == 0 else 2 * step - 2
-        sends = [hop(part, at, last, *merged_blocks, streams[part]) for part in range(2)]
+        sends = [hop(part, 0, last, *merged_blocks, streams[part]) for part in range(2)]
         for part in range(2):
             streams[part] = lax.ppermute(sends[part][0], flat, ring)
             if last:
                 ends.append(lax.ppermute(sends[part][1], flat, cross))
-        if step == 0:
+        if not last:
             slots, _, _ = lax.optimization_barrier((slots, sends[0][0], sends[1][0]))
             merged_blocks = merge(
-                3, n_y - 3, mine, slots, visual, visual_squares, text, text_squares
+                2 * step + 3, 3 if step == far - 3 else 2, mine, slots, *blocks_of[2:]
             )
-    return finish(*merged_blocks, streams[0], streams[1], ends[0], ends[1], cols)
+    product, squares = merged_blocks
+    key_out, inverse = finish(0, product, squares, streams[0], ends[0])
+    (value_out,) = finish(1, product, inverse, streams[1], ends[1])
+    return (key_out, value_out)
 
 
 def solution(mesh):

time: 113 us -> 112 us (level)
  Pallas kernels: 23.7 us -> 25.5 us
  starting transfers between devices: 68 us -> 66.3 us
    pallas_call x1 -> x3, Pallas kernels: 1.06 us -> 2.21 us  [the longest x2 1.7 us: finish(): pl.pallas_call(finish_values_kernel if part else finish_keys_kernel, out_...]
    pallas_call x2 -> x3, Pallas kernels: 7.68 us -> 8.7 us  [merge(): pl.pallas_call(functools.partial(merge_kernel, first), out_shape=(jax.Sha...]
  transfers between devices with their start and end apart: 14 -> 14, of which waited for: 7 -> 7; matrix products, arithmetic and copies ran while one was open for 1% -> 1% of each run, Pallas kernels for 18% -> 20%
where the time goes in v5:
time: 112 us; the launch traced here: 111 us
  starting transfers between devices  66.3 us (59%)
  Pallas kernels  25.5 us (23%)
  waiting for transfers between devices  17.1 us (15%)
    ppermute x6, starting transfers between devices, local(): streams[part] = lax.ppermute(sends[part][0], flat, ring)  18.2 us
    ppermute x1, starting transfers between devices, local(): other = lax.ppermute(blocks, 'core', swap)  16.2 us
    all_to_all x1, starting transfers between devices, local(): lax.all_to_all(outgoing.reshape(n_grp, capacity, feats), 'grp', 0, 0, til...  9.3 us
    ppermute x2, starting transfers between devices, local(): ends.append(lax.ppermute(sends[part][1], flat, cross))  8.71 us
    pallas_call x3, Pallas kernels, merge(): pl.pallas_call(functools.partial(merge_kernel, first), out_shape=(jax.Sha...  8.7 us
    pallas_call x1, Pallas kernels, text_products(): pl.pallas_call(text_kernel, out_shape=(hbm_out((count, rows, cols), BF16)...  8.27 us
    all_to_all x1, waiting for transfers between devices, local(): lax.all_to_all(outgoing.reshape(n_grp, capacity, feats), 'grp', 0, 0, til...  7.18 us
    ppermute x1, starting transfers between devices, local(): lax.ppermute(key_leaf, flat, ring)  5.1 us
  transfers between devices with their start and end apart: 14, of which 7 were waited for; matrix products, arithmetic and copies ran while one was open for 1% of the time, Pallas kernels for 20%

profile of v5, /device:TPU:1, one launch (start us, length us, event | category | flops | bytes accessed | tf_op | source)
XLA Modules:
  0.0 110.8 jit_solution(1990258903392335653)
XLA Ops:
  0.7 16.2 %collective-permute-start = (bf16[16,256,256]{2,1,0:T(8,128)(2,1)}, bf16[16,256,256]{2,1,0:T(8,128)(2,1)S(1)}, u32[]{:S(2)}, u32[]{:S(2)}) collective-permute-start(bf16[16,256,256]{2,1,0:T(8,128)(2,1)} %bitcast.9), channel_id=1, source_target_pairs={{0,1},{1,0},{2,3},{3,2},{4,5},{5,4},{6,7},{7,6},{8,9},{9,8},{10,11... | collective-permute-start | bytes 6291464 | tf_op jit(solution)/shard_map/ppermute | solution.py:440
  16.9 2.6 %source.1 = bf16[512,256]{1,0:T(8,128)(2,1)} custom-call(s32[1]{0:T(128)} %bitcast.group_ref, s32[128,128]{1,0:T(8,128)} %bitcast.7, bf16[256,1152]{1,0:T(8,128)(2,1)} %feats_ref.1, bf16[1152,256]{1,0:T(8,128)(2,1)} %proj_ref.1), custom_call_target="tpu_custom_call" | custom-call | tf_op jit(solution)/shard_map/source/pallas_call | solution.py:65
  19.5 9.3 %all-to-all-start = ((bf16[64,8,256]{2,1,0:T(8,128)(2,1)}), bf16[64,8,256]{2,1,0:T(8,128)(2,1)S(1)}, u32[]{:S(2)}, u32[]{:S(2)}) async-start(bf16[64,8,256]{2,1,0:T(8,128)(2,1)} %bitcast.11), calls=%async_computation | async-start | bytes 524288 | tf_op jit(solution)/shard_map/all_to_all | solution.py:432
  28.9 0.8 multiply_convert_fusion.w_own_ref.weight_ref
  29.7 2.2 %collective-permute-start.1 = (bf16[256,1024]{1,0:T(8,128)(2,1)S(1)}, bf16[256,1024]{1,0:T(8,128)(2,1)S(1)}, u32[]{:S(2)}, u32[]{:S(2)}) collective-permute-start(bf16[256,1024]{1,0:T(8,128)(2,1)S(1)} %multiply_convert_fusion.w_own_ref.weight_ref), channel_id=1, source_target_pairs={{0,1},{1,0},{2,3},{3,2},{4,5},{5,4},{6,7},{7,6},{8,9},{9,8},{10,11... | collective-permute-start | bytes 1572872 | tf_op jit(solution)/shard_map/ppermute | solution.py:438
  31.9 0.5 slots.1.slots_ref
  32.5 1.0 collective-permute-done.1.w_other_ref
  33.5 8.3 %text.1 = (bf16[8,256,1024]{2,1,0:T(8,128)(2,1)}, f32[8,8,256]{2,1,0:T(8,128)S(1)}) custom-call(s32[8]{0:T(128)S(1)} %broadcast_select_fusion.order_ref, bf16[16,256,256]{2,1,0:T(8,128)(2,1)} %bitcast.10, bf16[16,256,256]{2,1,0:T(8,128)(2,1)S(1)} %collective-permute-done.other_ref, bf16[256,1024]{1,0:T(8,128)(2,1)S(1)} %multiply_convert_fusion.w_own_ref.weight_ref, ...), custom_call_target="tpu_custom_call" | custom-call | flops 1 | bytes 1 | tf_op jit(solution)/shard_map/text/pallas_call | solution.py:152
  41.8 7.2 %all-to-all-done = bf16[64,8,256]{2,1,0:T(8,128)(2,1)S(1)} async-done(((bf16[64,8,256]{2,1,0:T(8,128)(2,1)}), bf16[64,8,256]{2,1,0:T(8,128)(2,1)S(1)}, u32[]{:S(2)}, u32[]{:S(2)}) %all-to-all-start) | async-done | bytes 262176 | tf_op jit(solution)/shard_map/all_to_all | solution.py:432
  49.0 3.7 %collective-permute-start.2 = (bf16[512,256]{1,0:T(8,128)(2,1)S(1)}, bf16[512,256]{1,0:T(8,128)(2,1)S(1)}, u32[]{:S(2)}, u32[]{:S(2)}) collective-permute-start(bf16[512,256]{1,0:T(8,128)(2,1)S(1)} %bitcast.5), channel_id=1, source_target_pairs={{0,1},{1,0},{2,3},{3,2},{4,5},{5,4},{6,7},{7,6},{8,9},{9,8},{10,11... | collective-permute-start | bytes 786440 | tf_op jit(solution)/shard_map/ppermute | solution.py:455
  52.7 0.5 own.1
  53.2 0.6 collective-permute-done.2.v_other_ref
  53.8 2.5 %visual.1 = (bf16[512,1024]{1,0:T(8,128)(2,1)S(1)}, f32[8,512]{1,0:T(8,128)S(1)}, bf16[272,512]{1,0:T(8,128)(2,1)S(1)}, bf16[256,512]{1,0:T(8,128)(2,1)S(1)}) custom-call(s32[8]{0:T(128)S(1)} %broadcast_select_fusion.order_ref, f32[512,1024]{1,0:T(8,128)S(1)} %get-tuple-element.30.own_ref, f32[8,512]{1,0:T(8,128)S(1)} %get-tuple-element.31.own_squares_ref, ...), custom_call_target="tpu_custom_call" | custom-call | tf_op jit(solution)/shard_map/visual/pallas_call | solution.py:238
  56.3 5.1 %collective-permute-start.3 = (bf16[272,512]{1,0:T(8,128)(2,1)S(1)}, bf16[272,512]{1,0:T(8,128)(2,1)S(1)}, u32[]{:S(2)}, u32[]{:S(2)}) collective-permute-start(bf16[272,512]{1,0:T(8,128)(2,1)S(1)} %get-tuple-element.38), channel_id=1, source_target_pairs={{0,2},{1,15},{2,4},{3,1},{4,6},{5,3},{6,8},{7,5},{8,10},{9,7},{10,... | collective-permute-start | bytes 835592 | tf_op jit(solution)/shard_map/ppermute | solution.py:460
  61.4 3.0 %collective-permute-start.4 = (bf16[256,512]{1,0:T(8,128)(2,1)S(1)}, bf16[256,512]{1,0:T(8,128)(2,1)S(1)}, u32[]{:S(2)}, u32[]{:S(2)}) collective-permute-start(bf16[256,512]{1,0:T(8,128)(2,1)S(1)} %get-tuple-element.39), channel_id=1, source_target_pairs={{0,2},{1,15},{2,4},{3,1},{4,6},{5,3},{6,8},{7,5},{8,10},{9,7},{10,... | collective-permute-start | bytes 786440 | tf_op jit(solution)/shard_map/ppermute | solution.py:460
  64.4 2.6 %merge.3 = (bf16[2,256,1024]{2,1,0:T(8,128)(2,1)S(1)}, f32[2,8,256]{2,1,0:T(8,128)S(1)}) custom-call(s32[8]{0:T(128)S(1)} %broadcast_select_fusion.order_ref, s32[8,512]{1,0:T(8,128)S(1)} %slots.1.slots_ref, bf16[512,1024]{1,0:T(8,128)(2,1)S(1)} %get-tuple-element.34.visual_ref, f32[8,512]{1,0:T(8,128)S(1)} %get-tuple-element.35.vis_squares_ref, ...), custom_call_target="tpu_custom_call" | custom-call | flops 536870912 | bytes 2097152 | tf_op jit(solution)/shard_map/merge/pallas_call | solution.py:276
  67.0 3.0 %collective-permute-start.5 = (bf16[528,512]{1,0:T(8,128)(2,1)S(1)}, bf16[528,512]{1,0:T(8,128)(2,1)S(1)}, u32[]{:S(2)}, u32[]{:S(2)}) collective-permute-start(bf16[528,512]{1,0:T(8,128)(2,1)S(1)} %hop.6), channel_id=1, source_target_pairs={{0,2},{1,15},{2,4},{3,1},{4,6},{5,3},{6,8},{7,5},{8,10},{9,7},{10,... | collective-permute-start | bytes 1622024 | tf_op jit(solution)/shard_map/ppermute | solution.py:468
  70.1 3.0 %collective-permute-start.6 = (bf16[512,512]{1,0:T(8,128)(2,1)S(1)}, bf16[512,512]{1,0:T(8,128)(2,1)S(1)}, u32[]{:S(2)}, u32[]{:S(2)}) collective-permute-start(bf16[512,512]{1,0:T(8,128)(2,1)S(1)} %hop.7), channel_id=1, source_target_pairs={{0,2},{1,15},{2,4},{3,1},{4,6},{5,3},{6,8},{7,5},{8,10},{9,7},{10,... | collective-permute-start | bytes 1572872 | tf_op jit(solution)/shard_map/ppermute | solution.py:468
  73.1 2.6 %merge.4 = (bf16[2,256,1024]{2,1,0:T(8,128)(2,1)S(1)}, f32[2,8,256]{2,1,0:T(8,128)S(1)}) custom-call(s32[8]{0:T(128)S(1)} %broadcast_select_fusion.order_ref, s32[8,512]{1,0:T(8,128)S(1)} %slots.1.slots_ref, bf16[512,1024]{1,0:T(8,128)(2,1)S(1)} %get-tuple-element.34.visual_ref, f32[8,512]{1,0:T(8,128)S(1)} %get-tuple-element.35.vis_squares_ref, ...), custom_call_target="tpu_custom_call" | custom-call | flops 536870912 | bytes 2097152 | tf_op jit(solution)/shard_map/merge/pallas_call | solution.py:276
  75.7 1.8 %collective-permute-done.5.came_ref = bf16[528,512]{1,0:T(8,128)(2,1)S(1)} collective-permute-done((bf16[528,512]{1,0:T(8,128)(2,1)S(1)}, bf16[528,512]{1,0:T(8,128)(2,1)S(1)}, u32[]{:S(2)}, u32[]{:S(2)}) %collective-permute-start.5) | collective-permute-done | bytes 540704 | tf_op jit(solution)/shard_map/ppermute | solution.py:468
  77.6 3.9 %collective-permute-start.7 = (bf16[528,512]{1,0:T(8,128)(2,1)S(1)}, bf16[528,512]{1,0:T(8,128)(2,1)S(1)}, u32[]{:S(2)}, u32[]{:S(2)}) collective-permute-start(bf16[528,512]{1,0:T(8,128)(2,1)S(1)} %hop.8), channel_id=1, source_target_pairs={{0,2},{1,15},{2,4},{3,1},{4,6},{5,3},{6,8},{7,5},{8,10},{9,7},{10,... | collective-permute-start | bytes 1622024 | tf_op jit(solution)/shard_map/ppermute | solution.py:468
  81.5 1.6 %collective-permute-done.6.came_ref = bf16[512,512]{1,0:T(8,128)(2,1)S(1)} collective-permute-done((bf16[512,512]{1,0:T(8,128)(2,1)S(1)}, bf16[512,512]{1,0:T(8,128)(2,1)S(1)}, u32[]{:S(2)}, u32[]{:S(2)}) %collective-permute-start.6) | collective-permute-done | bytes 524320 | tf_op jit(solution)/shard_map/ppermute | solution.py:468
  83.2 3.9 %collective-permute-start.10 = (bf16[512,512]{1,0:T(8,128)(2,1)S(1)}, bf16[512,512]{1,0:T(8,128)(2,1)S(1)}, u32[]{:S(2)}, u32[]{:S(2)}) collective-permute-start(bf16[512,512]{1,0:T(8,128)(2,1)S(1)} %hop.9), channel_id=1, source_target_pairs={{0,2},{1,15},{2,4},{3,1},{4,6},{5,3},{6,8},{7,5},{8,10},{9,7},{10,... | collective-permute-start | bytes 1572872 | tf_op jit(solution)/shard_map/ppermute | solution.py:468
  87.1 3.6 %merge.5 = (bf16[3,256,1024]{2,1,0:T(8,128)(2,1)S(1)}, f32[3,8,256]{2,1,0:T(8,128)S(1)}) custom-call(s32[8]{0:T(128)S(1)} %broadcast_select_fusion.order_ref, s32[8,512]{1,0:T(8,128)S(1)} %slots.1.slots_ref, bf16[512,1024]{1,0:T(8,128)(2,1)S(1)} %get-tuple-element.34.visual_ref, f32[8,512]{1,0:T(8,128)S(1)} %get-tuple-element.35.vis_squares_ref, ...), custom_call_target="tpu_custom_call" | custom-call | flops 805306368 | bytes 3145728 | tf_op jit(solution)/shard_map/merge/pallas_call | solution.py:276
  90.8 2.1 %collective-permute-start.8 = (bf16[272,512]{1,0:T(8,128)(2,1)S(1)}, bf16[272,512]{1,0:T(8,128)(2,1)S(1)}, u32[]{:S(2)}, u32[]{:S(2)}) collective-permute-start(bf16[272,512]{1,0:T(8,128)(2,1)S(1)} %get-tuple-element.46), channel_id=1, source_target_pairs={{0,2},{1,15},{2,4},{3,1},{4,6},{5,3},{6,8},{7,5},{8,10},{9,7},{10,... | collective-permute-start | bytes 835592 | tf_op jit(solution)/shard_map/ppermute | solution.py:468
  93.0 5.6 %collective-permute-start.9 = (bf16[272,512]{1,0:T(8,128)(2,1)S(1)}, bf16[272,512]{1,0:T(8,128)(2,1)S(1)}, u32[]{:S(2)}, u32[]{:S(2)}) collective-permute-start(bf16[272,512]{1,0:T(8,128)(2,1)S(1)} %get-tuple-element.47), channel_id=1, source_target_pairs={{0,3},{1,14},{2,5},{3,0},{4,7},{5,2},{6,9},{7,4},{8,11},{9,6},{10,... | collective-permute-start | bytes 835592 | tf_op jit(solution)/shard_map/ppermute | solution.py:470
  98.7 2.3 %collective-permute-start.11 = (bf16[256,512]{1,0:T(8,128)(2,1)S(1)}, bf16[256,512]{1,0:T(8,128)(2,1)S(1)}, u32[]{:S(2)}, u32[]{:S(2)}) collective-permute-start(bf16[256,512]{1,0:T(8,128)(2,1)S(1)} %get-tuple-element.50), channel_id=1, source_target_pairs={{0,2},{1,15},{2,4},{3,1},{4,6},{5,3},{6,8},{7,5},{8,10},{9,7},{10,... | collective-permute-start | bytes 786440 | tf_op jit(solution)/shard_map/ppermute | solution.py:468
  101.0 3.1 %collective-permute-start.12 = (bf16[256,512]{1,0:T(8,128)(2,1)S(1)}, bf16[256,512]{1,0:T(8,128)(2,1)S(1)}, u32[]{:S(2)}, u32[]{:S(2)}) collective-permute-start(bf16[256,512]{1,0:T(8,128)(2,1)S(1)} %get-tuple-element.51), channel_id=1, source_target_pairs={{0,3},{1,14},{2,5},{3,0},{4,7},{5,2},{6,9},{7,4},{8,11},{9,6},{10,... | collective-permute-start | bytes 786440 | tf_op jit(solution)/shard_map/ppermute | solution.py:470
  104.2 0.9 finish.2
  105.0 1.1 collective-permute-done.11.v_ref
  106.1 3.8 %collective-permute-done.12.v2_ref = bf16[256,512]{1,0:T(8,128)(2,1)S(1)} collective-permute-done((bf16[256,512]{1,0:T(8,128)(2,1)S(1)}, bf16[256,512]{1,0:T(8,128)(2,1)S(1)}, u32[]{:S(2)}, u32[]{:S(2)}) %collective-permute-start.12) | collective-permute-done | bytes 262176 | tf_op jit(solution)/shard_map/ppermute | solution.py:470
  109.9 0.8 finish.3
  (30 shorter events, 0.8 us)
Async XLA Ops:
  0.6 31.8 %copy-start.4 = (s32[8]{0:T(128)S(1)}, s32[8]{0:T(128)}, u32[]{:S(2)}) copy-start(s32[8]{0:T(128)} %constant.48) | copy-start | bytes 100
  0.6 31.8 %copy-start.5 = (s32[8]{0:T(128)S(1)}, s32[8]{0:T(128)}, u32[]{:S(2)}) copy-start(s32[8]{0:T(128)} %constant.47) | copy-start | bytes 100
  0.7 31.8 %copy-start.6 = (s32[8]{0:T(128)S(1)}, s32[8]{0:T(128)}, u32[]{:S(2)}) copy-start(s32[8]{0:T(128)} %constant.45.clone) | copy-start | bytes 100
  0.7 31.8 %copy-start.7 = (s32[8]{0:T(128)S(1)}, s32[8]{0:T(128)}, u32[]{:S(2)}) copy-start(s32[8]{0:T(128)} %constant.44.clone) | copy-start | bytes 100
  0.7 31.2 %copy-start = (s32[16384]{0:T(1024)S(1)}, s32[16384]{0:T(1024)}, u32[]{:S(2)}) copy-start(s32[16384]{0:T(1024)} %param.13) | copy-start | bytes 196612
  0.7 28.2 %copy-start.2 = (bf16[256,512]{1,0:T(8,128)(2,1)S(1)}, bf16[256,512]{1,0:T(8,128)(2,1)}, u32[]{:S(2)}) copy-start(bf16[256,512]{1,0:T(8,128)(2,1)} %param.17) | copy-start | bytes 786436
  0.7 28.2 %copy-start.3 = (bf16[256,512]{1,0:T(8,128)(2,1)S(1)}, bf16[256,512]{1,0:T(8,128)(2,1)}, u32[]{:S(2)}) copy-start(bf16[256,512]{1,0:T(8,128)(2,1)} %param.16) | copy-start | bytes 786436
  0.7 31.2 %copy-start.1 = (s32[1,4096]{1,0:T(1,128)S(1)}, s32[1,4096]{1,0:T(1,128)}, u32[]{:S(2)}) copy-start(s32[1,4096]{1,0:T(1,128)} %layout_ref.1) | copy-start | bytes 49156
  0.7 32.8 %collective-permute-start = (bf16[16,256,256]{2,1,0:T(8,128)(2,1)}, bf16[16,256,256]{2,1,0:T(8,128)(2,1)S(1)}, u32[]{:S(2)}, u32[]{:S(2)}) collective-permute-start(bf16[16,256,256]{2,1,0:T(8,128)(2,1)} %bitcast.9), channel_id=1, source_target_pairs={{0,1},{1,0},{2,3},{3,2},{4,5},{5,4},{6,7},{7,6},{8,9},{9,8},{10,11... | collective-permute-start | bytes 6291464 | tf_op jit(solution)/shard_map/ppermute | solution.py:440
  19.5 29.4 %all-to-all-start = ((bf16[64,8,256]{2,1,0:T(8,128)(2,1)}), bf16[64,8,256]{2,1,0:T(8,128)(2,1)S(1)}, u32[]{:S(2)}, u32[]{:S(2)}) async-start(bf16[64,8,256]{2,1,0:T(8,128)(2,1)} %bitcast.11), calls=%async_computation | async-start | bytes 524288 | tf_op jit(solution)/shard_map/all_to_all | solution.py:432
  29.7 3.8 %collective-permute-start.1 = (bf16[256,1024]{1,0:T(8,128)(2,1)S(1)}, bf16[256,1024]{1,0:T(8,128)(2,1)S(1)}, u32[]{:S(2)}, u32[]{:S(2)}) collective-permute-start(bf16[256,1024]{1,0:T(8,128)(2,1)S(1)} %multiply_convert_fusion.w_own_ref.weight_ref), channel_id=1, source_target_pairs={{0,1},{1,0},{2,3},{3,2},{4,5},{5,4},{6,7},{7,6},{8,9},{9,8},{10,11... | collective-permute-start | bytes 1572872 | tf_op jit(solution)/shard_map/ppermute | solution.py:438
  49.0 4.8 %collective-permute-start.2 = (bf16[512,256]{1,0:T(8,128)(2,1)S(1)}, bf16[512,256]{1,0:T(8,128)(2,1)S(1)}, u32[]{:S(2)}, u32[]{:S(2)}) collective-permute-start(bf16[512,256]{1,0:T(8,128)(2,1)S(1)} %bitcast.5), channel_id=1, source_target_pairs={{0,1},{1,0},{2,3},{3,2},{4,5},{5,4},{6,7},{7,6},{8,9},{9,8},{10,11... | collective-permute-start | bytes 786440 | tf_op jit(solution)/shard_map/ppermute | solution.py:455
  56.3 10.7 %collective-permute-start.3 = (bf16[272,512]{1,0:T(8,128)(2,1)S(1)}, bf16[272,512]{1,0:T(8,128)(2,1)S(1)}, u32[]{:S(2)}, u32[]{:S(2)}) collective-permute-start(bf16[272,512]{1,0:T(8,128)(2,1)S(1)} %get-tuple-element.38), channel_id=1, source_target_pairs={{0,2},{1,15},{2,4},{3,1},{4,6},{5,3},{6,8},{7,5},{8,10},{9,7},{10,... | collective-permute-start | bytes 835592 | tf_op jit(solution)/shard_map/ppermute | solution.py:460
  61.4 8.6 %collective-permute-start.4 = (bf16[256,512]{1,0:T(8,128)(2,1)S(1)}, bf16[256,512]{1,0:T(8,128)(2,1)S(1)}, u32[]{:S(2)}, u32[]{:S(2)}) collective-permute-start(bf16[256,512]{1,0:T(8,128)(2,1)S(1)} %get-tuple-element.39), channel_id=1, source_target_pairs={{0,2},{1,15},{2,4},{3,1},{4,6},{5,3},{6,8},{7,5},{8,10},{9,7},{10,... | collective-permute-start | bytes 786440 | tf_op jit(solution)/shard_map/ppermute | solution.py:460
  67.0 10.4 %collective-permute-start.5 = (bf16[528,512]{1,0:T(8,128)(2,1)S(1)}, bf16[528,512]{1,0:T(8,128)(2,1)S(1)}, u32[]{:S(2)}, u32[]{:S(2)}) collective-permute-start(bf16[528,512]{1,0:T(8,128)(2,1)S(1)} %hop.6), channel_id=1, source_target_pairs={{0,2},{1,15},{2,4},{3,1},{4,6},{5,3},{6,8},{7,5},{8,10},{9,7},{10,... | collective-permute-start | bytes 1622024 | tf_op jit(solution)/shard_map/ppermute | solution.py:468
  70.1 12.9 %collective-permute-start.6 = (bf16[512,512]{1,0:T(8,128)(2,1)S(1)}, bf16[512,512]{1,0:T(8,128)(2,1)S(1)}, u32[]{:S(2)}, u32[]{:S(2)}) collective-permute-start(bf16[512,512]{1,0:T(8,128)(2,1)S(1)} %hop.7), channel_id=1, source_target_pairs={{0,2},{1,15},{2,4},{3,1},{4,6},{5,3},{6,8},{7,5},{8,10},{9,7},{10,... | collective-permute-start | bytes 1572872 | tf_op jit(solution)/shard_map/ppermute | solution.py:468
  77.6 13.1 %collective-permute-start.7 = (bf16[528,512]{1,0:T(8,128)(2,1)S(1)}, bf16[528,512]{1,0:T(8,128)(2,1)S(1)}, u32[]{:S(2)}, u32[]{:S(2)}) collective-permute-start(bf16[528,512]{1,0:T(8,128)(2,1)S(1)} %hop.8), channel_id=1, source_target_pairs={{0,2},{1,15},{2,4},{3,1},{4,6},{5,3},{6,8},{7,5},{8,10},{9,7},{10,... | collective-permute-start | bytes 1622024 | tf_op jit(solution)/shard_map/ppermute | solution.py:468
  83.2 15.4 %collective-permute-start.10 = (bf16[512,512]{1,0:T(8,128)(2,1)S(1)}, bf16[512,512]{1,0:T(8,128)(2,1)S(1)}, u32[]{:S(2)}, u32[]{:S(2)}) collective-permute-start(bf16[512,512]{1,0:T(8,128)(2,1)S(1)} %hop.9), channel_id=1, source_target_pairs={{0,2},{1,15},{2,4},{3,1},{4,6},{5,3},{6,8},{7,5},{8,10},{9,7},{10,... | collective-permute-start | bytes 1572872 | tf_op jit(solution)/shard_map/ppermute | solution.py:468
  90.8 13.3 %collective-permute-start.8 = (bf16[272,512]{1,0:T(8,128)(2,1)S(1)}, bf16[272,512]{1,0:T(8,128)(2,1)S(1)}, u32[]{:S(2)}, u32[]{:S(2)}) collective-permute-start(bf16[272,512]{1,0:T(8,128)(2,1)S(1)} %get-tuple-element.46), channel_id=1, source_target_pairs={{0,2},{1,15},{2,4},{3,1},{4,6},{5,3},{6,8},{7,5},{8,10},{9,7},{10,... | collective-permute-start | bytes 835592 | tf_op jit(solution)/shard_map/ppermute | solution.py:468
  93.0 11.2 %collective-permute-start.9 = (bf16[272,512]{1,0:T(8,128)(2,1)S(1)}, bf16[272,512]{1,0:T(8,128)(2,1)S(1)}, u32[]{:S(2)}, u32[]{:S(2)}) collective-permute-start(bf16[272,512]{1,0:T(8,128)(2,1)S(1)} %get-tuple-element.47), channel_id=1, source_target_pairs={{0,3},{1,14},{2,5},{3,0},{4,7},{5,2},{6,9},{7,4},{8,11},{9,6},{10,... | collective-permute-start | bytes 835592 | tf_op jit(solution)/shard_map/ppermute | solution.py:470
  98.7 7.4 %collective-permute-start.11 = (bf16[256,512]{1,0:T(8,128)(2,1)S(1)}, bf16[256,512]{1,0:T(8,128)(2,1)S(1)}, u32[]{:S(2)}, u32[]{:S(2)}) collective-permute-start(bf16[256,512]{1,0:T(8,128)(2,1)S(1)} %get-tuple-element.50), channel_id=1, source_target_pairs={{0,2},{1,15},{2,4},{3,1},{4,6},{5,3},{6,8},{7,5},{8,10},{9,7},{10,... | collective-permute-start | bytes 786440 | tf_op jit(solution)/shard_map/ppermute | solution.py:468
  101.0 8.9 %collective-permute-start.12 = (bf16[256,512]{1,0:T(8,128)(2,1)S(1)}, bf16[256,512]{1,0:T(8,128)(2,1)S(1)}, u32[]{:S(2)}, u32[]{:S(2)}) collective-permute-start(bf16[256,512]{1,0:T(8,128)(2,1)S(1)} %get-tuple-element.51), channel_id=1, source_target_pairs={{0,3},{1,14},{2,5},{3,0},{4,7},{5,2},{6,9},{7,4},{8,11},{9,6},{10,... | collective-permute-start | bytes 786440 | tf_op jit(solution)/shard_map/ppermute | solution.py:470
